TPU v7x, 256 devices: a whole 4x4x8 slice. The times are simulated.
256 devices in a mesh: dom: 256 (over y, z, x, core).
Axes of the slice: x: 4, y: 4, z: 8, core: 2. Of those that a mesh axis runs over, the one named last changes fastest.
Arguments:
- dofs: float32 [56, 9, 32768], P(None, None, 'dom'), may hold values from -6 to 6
- star: float32 [3, 9, 9, 32768], P(None, None, None, 'dom'), may hold values from -8 to 8
- flux_minus: float32 [4, 9, 9, 32768], P(None, None, None, 'dom'), may hold values from -0.4 to 0.4
- flux_plus: float32 [4, 9, 9, 32768], P(None, None, None, 'dom'), may hold values from -0.4 to 0.4
- cohesion: float32 [32768], P('dom'), may hold values from 0.5 to 4
- stiff: float32 [3, 56, 56], replicated, may hold values from -1 to 1
- face_proj: float32 [4, 21, 56], replicated, may hold values from -0.75 to 0.75
- lift: float32 [4, 56, 21], replicated, may hold values from -1.25 to 1.25
- rotate: float32 [3, 21, 21], replicated, may hold values from -1.25 to 1.25
- cluster: int32 [32768], P('dom'), may hold values from 0 to 1, as said below
- neighbor: int32 [4, 32768], P(None, 'dom'), may hold values from 0 to 256, as said below
- neigh_face: int32 [4, 32768], P(None, 'dom'), may hold values from 0 to 3, as said below
- orient: int32 [4, 32768], P(None, 'dom'), may hold values from 0 to 2, as said below
- send_elem: int32 [4, 8192], P(None, 'dom'), may hold values from 0 to 127, as said below
- send_face: int32 [4, 8192], P(None, 'dom'), may hold values from 0 to 3, as said below
Outputs:
- new_dofs: float32 [56, 9, 32768], P(None, None, 'dom')
Inputs may be any that keep to these rules, and one draw needn't show every extreme that they name: `cluster`: each partition has at most 64 fine elements, and it has at most 96 together with the partition half the axis away; both bounds are reached in every draw. `neighbor`: values below 128 name an element of the same partition; 128 + b * 32 + s names slot s of the faces shared with the partition at offset -2, -1, 1, 2 for b = 0, 1, 2, 3, that is slot s of block 3 - b in that partition's send_elem and send_face; 256 marks the mesh's boundary. Every slot of an existing partition is named by exactly one face, and faces pair symmetrically. `neigh_face`: the neighbour's face across each face; for a shared slot it equals the slot's send_face; 0 on the boundary. `orient`: 0 on the boundary; a face pair's codes h and (3 - h) % 3. `send_elem`: block b holds, for slot s, the local element whose face the partition shares with the partition at offset -2, -1, 1, 2 for b = 0, 1, 2, 3. `send_face`: the face of that element in slot s of block b.
All inputs are finite; a program needn't handle non-finite values.
Results may differ from a plain program's by a relative error of at most 0.00024.
Values sent between devices are 32-bit elements; how exact they have to be, the bound alone decides.
No kernel may reach another device: no remote copies, remote signals or barrier semaphores. Data moves between devices by JAX's collectives and lax.ppermute only.
A program may use at most 128 MiB of HBM per device.

v0:
```python
import math

import jax
import jax.numpy as jnp
from jax import lax
from jax.sharding import PartitionSpec as P

ORDER = 6
RATE = 4


PRECISE = lax.Precision.HIGHEST


def from_behind(value, axis, by):
    devices = lax.axis_size(axis)
    pairs = [(i, i + by) for i in range(devices) if 0 <= i + by < devices]
    return lax.ppermute(value, axis, pairs)


def prepare(stiff, star):
    skew = 0.5 * (stiff - jnp.transpose(stiff, (0, 2, 1)))
    sym = 0.5 * (star + jnp.transpose(star, (0, 2, 1, 3)))
    return (skew, sym)


def operator_left(skew, transposed):
    basis_size = skew.shape[1]
    order_axes = (2, 0, 1) if transposed else (1, 0, 2)
    return jnp.transpose(skew, order_axes).reshape(basis_size, 3 * basis_size)


def star_apply(matrices, values):
    return jnp.sum(jnp.expand_dims(matrices, -4) * jnp.expand_dims(values, -3), axis=-2)


def apply_operator(values, left_matrix, sym):
    stacked = jnp.stack([star_apply(sym[direction], values) for direction in range(3)])
    product = jnp.dot(left_matrix, stacked.reshape(left_matrix.shape[1], -1), precision=PRECISE)
    return product.reshape(values.shape)


def derivatives(values, left_matrix, sym):
    series = [values]
    for term in range(ORDER - 1):
        series.append(-apply_operator(series[-1], left_matrix, sym))
    return series


def interval_weights(begin_time, end_time):
    return [
        (end_time ** (term + 1) - begin_time ** (term + 1)) / math.factorial(term + 1)
        for term in range(ORDER)
    ]


def integrate(series, weights):
    running = weights[0] * series[0]
    for term in range(1, ORDER):
        running = running + weights[term] * series[term]
    return running


def traces(values, face_proj):
    face_count, fbasis, basis_size = face_proj.shape
    product = jnp.dot(
        face_proj.reshape(face_count * fbasis, basis_size),
        values.reshape(basis_size, -1),
        precision=PRECISE,
    )
    return product.reshape(face_count, fbasis, values.shape[1], values.shape[2])


def lift_apply(face_values, lift):
    face_count, basis_size, fbasis = lift.shape
    left_matrix = jnp.transpose(lift, (1, 0, 2)).reshape(basis_size, face_count * fbasis)
    product = jnp.dot(left_matrix, face_values.reshape(face_count * fbasis, -1), precision=PRECISE)
    return product.reshape(basis_size, face_values.shape[2], face_values.shape[3])


def rotate_apply(face_values, orient, rotate):
    turned = jnp.einsum("kij,fjqm->kfiqm", rotate, face_values, precision=PRECISE)
    rotation = orient[:, None, None, :]
    return jnp.where(rotation == 0, turned[0], jnp.where(rotation == 1, turned[1], turned[2]))


def plastic(values, cohesion):
    average = values[0]
    mean_stress = (average[0] + average[1] + average[2]) / 3.0
    dev_xx = average[0] - mean_stress
    dev_yy = average[1] - mean_stress
    dev_zz = average[2] - mean_stress
    second = (
        0.5 * (dev_xx * dev_xx + dev_yy * dev_yy + dev_zz * dev_zz)
        + average[3] * average[3]
        + average[4] * average[4]
        + average[5] * average[5]
    )
    factor = cohesion / jnp.maximum(jnp.sqrt(second), cohesion)
    pressure = (values[:, 0] + values[:, 1] + values[:, 2]) / 3.0
    normal = pressure[:, None, :] + factor * (values[:, 0:3, :] - pressure[:, None, :])
    shear_part = factor * values[:, 3:6, :]
    return jnp.concatenate([normal, shear_part, values[:, 6:, :]], axis=1)


def update(
    values,
    predictor,
    own_faces,
    remote_faces,
    orient,
    back_left,
    sym,
    flux_minus,
    flux_plus,
    cohesion,
    lift,
    rotate,
):
    volume_term = apply_operator(predictor, back_left, sym)
    local_term = lift_apply(star_apply(flux_minus, own_faces), lift)
    remote_term = lift_apply(
        star_apply(flux_plus, rotate_apply(remote_faces, orient, rotate)), lift
    )
    return plastic(values + volume_term - local_term - remote_term, cohesion)


def flatten_faces(face_values):
    face_count, fbasis, quantities, columns = face_values.shape
    return jnp.transpose(face_values, (0, 3, 1, 2)).reshape(
        face_count * columns, fbasis * quantities
    )


def gather_faces(
    flattened, columns, ghost_rows, ghost_index, targets, face_ids, ghost_count, fbasis, quantities
):
    is_local = (targets < columns).reshape(-1)[:, None]
    is_ghost = ((targets >= columns) & (targets < columns + ghost_count)).reshape(-1)[:, None]
    local_pick = jnp.take(
        flattened, (face_ids * columns + jnp.minimum(targets, columns - 1)).reshape(-1), axis=0
    )
    ghost_pick = jnp.take(ghost_rows, ghost_index.reshape(-1), axis=0)
    picked = jnp.where(is_local, local_pick, jnp.where(is_ghost, ghost_pick, 0.0))
    return jnp.transpose(picked.reshape(targets.shape[0], -1, fbasis, quantities), (0, 2, 3, 1))


def shards(
    dofs,
    star,
    flux_minus,
    flux_plus,
    cohesion,
    stiff,
    face_proj,
    lift,
    rotate,
    cluster,
    neighbor,
    neigh_face,
    orient,
    send_elem,
    send_face,
):
    skew, sym = prepare(stiff, star)
    forward_left = operator_left(skew, False)
    back_left = operator_left(skew, True)
    elem_count = dofs.shape[2]
    slot_count = send_elem.shape[1]
    ghost_count = 4 * slot_count
    fbasis = face_proj.shape[1]
    quantities = dofs.shape[1]
    fine_cap = elem_count // 2
    fine = cluster == 1
    fine_rows = jnp.nonzero(fine, size=fine_cap, fill_value=elem_count)[0].astype(jnp.int32)
    safe_rows = jnp.minimum(fine_rows, elem_count - 1)
    sym_fine = sym[..., safe_rows]
    minus_fine = flux_minus[..., safe_rows]
    plus_fine = flux_plus[..., safe_rows]
    cohesion_fine = cohesion[safe_rows]
    orient_fine = orient[:, safe_rows]
    neighbor_fine = neighbor[:, safe_rows]
    face_fine = neigh_face[:, safe_rows]
    state_fine = dofs[:, :, safe_rows]
    series = derivatives(dofs, forward_left, sym)
    full = integrate(series, interval_weights(0.0, 1.0))
    pieces = [
        integrate(series, interval_weights(substep / RATE, (substep + 1) / RATE))
        for substep in range(RATE)
    ]
    fine_weights = interval_weights(0.0, 1.0 / RATE)

    def ghost_positions(targets, face_ids):
        slot_pos = jnp.clip(targets - elem_count, 0, ghost_count - 1)
        return face_ids * ghost_count + slot_pos

    index_fine = ghost_positions(neighbor_fine, face_fine)
    index_all = ghost_positions(neighbor, neigh_face)
    offsets = (-2, -1, 1, 2)
    predictor = pieces[0]
    fine_pred = None
    ghost_store = None
    flat_store = None
    for substep in range(RATE):
        if substep > 0:
            predictor = pieces[substep].at[:, :, fine_rows].set(fine_pred, mode="drop")
        face_values = traces(predictor, face_proj)
        flattened = flatten_faces(face_values)
        received = []
        for position in range(4):
            received.append(
                from_behind(predictor[:, :, send_elem[3 - position]], "dom", -offsets[position])
            )
        ghost_pred = jnp.concatenate(received, axis=2)
        ghost_rows = flatten_faces(traces(ghost_pred, face_proj))
        ghost_store = ghost_pred if substep == 0 else ghost_store + ghost_pred
        flat_store = flattened if substep == 0 else flat_store + flattened
        remote = gather_faces(
            flattened,
            elem_count,
            ghost_rows,
            index_fine,
            neighbor_fine,
            face_fine,
            ghost_count,
            fbasis,
            quantities,
        )
        state_fine = update(
            state_fine,
            predictor[:, :, safe_rows],
            face_values[..., safe_rows],
            remote,
            orient_fine,
            back_left,
            sym_fine,
            minus_fine,
            plus_fine,
            cohesion_fine,
            lift,
            rotate,
        )
        if substep < RATE - 1:
            fine_pred = integrate(derivatives(state_fine, forward_left, sym_fine), fine_weights)
    coarse_ghosts = flatten_faces(traces(ghost_store, face_proj))
    remote_all = gather_faces(
        flat_store,
        elem_count,
        coarse_ghosts,
        index_all,
        neighbor,
        neigh_face,
        ghost_count,
        fbasis,
        quantities,
    )
    coarse = update(
        dofs,
        full,
        traces(full, face_proj),
        remote_all,
        orient,
        back_left,
        sym,
        flux_minus,
        flux_plus,
        cohesion,
        lift,
        rotate,
    )
    return coarse.at[:, :, fine_rows].set(state_fine, mode="drop")


def solution(mesh):
    placed = (
        P(None, None, "dom"),
        P(None, None, None, "dom"),
        P(None, None, None, "dom"),
        P(None, None, None, "dom"),
        P("dom"),
        P(),
        P(),
        P(),
        P(),
        P("dom"),
        P(None, "dom"),
        P(None, "dom"),
        P(None, "dom"),
        P(None, "dom"),
        P(None, "dom"),
    )
    return jax.shard_map(
        shards, mesh=mesh, in_specs=placed, out_specs=P(None, None, "dom"), check_vma=False
    )
```

profile of v0, /device:TPU:24, one launch (start us, length us, event | category | flops | bytes accessed | tf_op | source)
XLA Modules:
  0.0 521.6 jit_solution(9011497569682995932)
XLA Ops:
  0.0 2.8 copy.963
  4.9 3.1 fusion
  25.9 3.5 collective-permute-start
  33.9 8.2 %collective-permute-start.2 = (f32[56,9,32]{0,1,2:T(8,128)}, f32[56,9,32]{0,1,2:T(8,128)}, u32[]{:S(2)}, u32[]{:S(2)}) collective-permute-start(f32[56,9,32]{0,1,2:T(8,128)} %bitcast.79), channel_id=1, source_target_pairs={{1,0},{2,1},{3,2},{4,3},{5,4},{6,5},{7,6},{8,7},{9,8},{10,9},{11,1... | collective-permute-start | bytes 193544 | tf_op jit(solution)/shard_map/ppermute | solution.py:18
  43.4 4.2 collective-permute-start.3
  52.2 4.1 gather_fusion.1
  66.6 2.9 fusion.137
  81.5 3.1 gather_fusion.5
  85.8 3.1 gather_fusion.4
  91.7 3.1 gather_fusion.3
  114.0 2.7 gather_fusion.32
  124.7 2.5 copy.1031
  135.6 2.7 gather_fusion.33
  162.7 2.4 reshape.819
  171.5 2.4 reshape.820
  180.3 2.4 reshape.821
  189.0 2.4 reshape.822
  193.5 2.4 convolution_negate_fusion.11
  198.2 2.4 reshape.823
  202.7 3.2 fusion.6
  207.8 4.5 scatter_fusion
  218.3 2.8 multiply_reduce_fusion.48
  227.5 3.0 copy.1068
  230.5 4.1 gather_fusion.15
  234.6 2.4 copy.1069
  250.5 2.5 copy.1065
  259.3 7.9 %collective-permute-start.6 = (f32[56,9,32]{0,1,2:T(8,128)}, f32[56,9,32]{0,1,2:T(8,128)}, u32[]{:S(2)}, u32[]{:S(2)}) collective-permute-start(f32[56,9,32]{0,1,2:T(8,128)} %bitcast.146), channel_id=1, source_target_pairs={{1,0},{2,1},{3,2},{4,3},{5,4},{6,5},{7,6},{8,7},{9,8},{10,9},{11,1... | collective-permute-start | bytes 193544 | tf_op jit(solution)/shard_map/ppermute | solution.py:18
  267.2 4.0 collective-permute-start.7
  302.0 2.4 reshape.836
  308.9 2.4 reshape.837
  316.2 2.4 reshape.838
  323.1 2.4 reshape.839
  330.0 2.4 reshape.840
  333.7 3.0 fusion.9
  338.0 2.6 scatter_fusion.1
  344.8 2.9 multiply_reduce_fusion.30
  355.2 4.1 gather_fusion.21
  359.3 2.4 copy.1110
  375.3 2.4 copy.1106
  382.2 7.9 %collective-permute-start.10 = (f32[56,9,32]{0,1,2:T(8,128)}, f32[56,9,32]{0,1,2:T(8,128)}, u32[]{:S(2)}, u32[]{:S(2)}) collective-permute-start(f32[56,9,32]{0,1,2:T(8,128)} %bitcast.208), channel_id=1, source_target_pairs={{1,0},{2,1},{3,2},{4,3},{5,4},{6,5},{7,6},{8,7},{9,8},{10,9},{11,1... | collective-permute-start | bytes 193544 | tf_op jit(solution)/shard_map/ppermute | solution.py:18
  390.1 4.1 collective-permute-start.11
  437.0 2.6 scatter_fusion.2
  449.1 4.1 gather_fusion.31
  453.2 2.5 copy.1162
  475.1 7.9 %collective-permute-start.14 = (f32[56,9,32]{0,1,2:T(8,128)}, f32[56,9,32]{0,1,2:T(8,128)}, u32[]{:S(2)}, u32[]{:S(2)}) collective-permute-start(f32[56,9,32]{0,1,2:T(8,128)} %bitcast.262), channel_id=1, source_target_pairs={{1,0},{2,1},{3,2},{4,3},{5,4},{6,5},{7,6},{8,7},{9,8},{10,9},{11,1... | collective-permute-start | bytes 193544 | tf_op jit(solution)/shard_map/ppermute | solution.py:18
  483.0 4.1 collective-permute-start.15
  503.5 2.9 add_add_fusion
  517.8 2.6 scatter_fusion.3
  (626 shorter events, 355.3 us)
Async XLA Ops:
  0.0 143.8 %copy-start = (f32[3,21,21]{2,1,0:T(8,128)S(1)}, f32[3,21,21]{2,1,0:T(8,128)}, u32[]{:S(2)}) copy-start(f32[3,21,21]{2,1,0:T(8,128)} %param.27) | copy-start | bytes 15880
  23.5 24.2 %copy-start.91 = (s32[128]{0:T(128)S(1)}, s32[128]{0:T(128)}, u32[]{:S(2)}) copy-start(s32[128]{0:T(128)} %param.28) | copy-start | bytes 1540
  24.0 23.7 %copy-start.74 = (s32[1024]{0:T(1024)}, s32[1024]{0:T(1024)S(1)}, u32[]{:S(2)}) copy-start(s32[1024]{0:T(1024)S(1)} %get-tuple-element.132) | copy-start | bytes 12292
  25.9 30.4 %copy-start.66 = (s32[4,128]{1,0:T(4,128)S(1)}, s32[4,128]{1,0:T(4,128)}, u32[]{:S(2)}) copy-start(s32[4,128]{1,0:T(4,128)} %param.29) | copy-start | bytes 6148
  25.9 92.2 %collective-permute-start = (f32[56,9,32]{0,1,2:T(8,128)}, f32[56,9,32]{0,1,2:T(8,128)}, u32[]{:S(2)}, u32[]{:S(2)}) collective-permute-start(f32[56,9,32]{0,1,2:T(8,128)} %bitcast.73), channel_id=1, source_target_pairs={{0,2},{1,3},{2,4},{3,5},{4,6},{5,7},{6,8},{7,9},{8,10},{9,11},{10,... | collective-permute-start | bytes 193544 | tf_op jit(solution)/shard_map/ppermute | solution.py:18
  29.4 27.7 %copy-start.81 = (s32[4,128]{1,0:T(4,128)S(1)}, s32[4,128]{1,0:T(4,128)}, u32[]{:S(2)}) copy-start(s32[4,128]{1,0:T(4,128)} %param.30) | copy-start | bytes 6148
  30.7 89.0 %collective-permute-start.1 = (f32[56,9,32]{0,1,2:T(8,128)}, f32[56,9,32]{0,1,2:T(8,128)}, u32[]{:S(2)}, u32[]{:S(2)}) collective-permute-start(f32[56,9,32]{0,1,2:T(8,128)} %bitcast.76), channel_id=1, source_target_pairs={{0,1},{1,2},{2,3},{3,4},{4,5},{5,6},{6,7},{7,8},{8,9},{9,10},{10,1... | collective-permute-start | bytes 193544 | tf_op jit(solution)/shard_map/ppermute | solution.py:18
  32.6 15.1 %copy-start.75 = (s32[1024]{0:T(1024)}, s32[1024]{0:T(1024)S(1)}, u32[]{:S(2)}) copy-start(s32[1024]{0:T(1024)S(1)} %get-tuple-element.130) | copy-start | bytes 12292
  32.6 15.1 %copy-start.76 = (s32[1024]{0:T(1024)}, s32[1024]{0:T(1024)S(1)}, u32[]{:S(2)}) copy-start(s32[1024]{0:T(1024)S(1)} %get-tuple-element.131) | copy-start | bytes 12292
  33.9 28.5 %copy-start.80 = (s32[4,128]{1,0:T(4,128)S(1)}, s32[4,128]{1,0:T(4,128)}, u32[]{:S(2)}) copy-start(s32[4,128]{1,0:T(4,128)} %param.31) | copy-start | bytes 6148
  33.9 29.2 %copy-start.64 = (f32[4,21,56]{2,0,1:T(4,128)S(1)}, f32[4,21,56]{2,0,1:T(4,128)}, u32[]{:S(2)}) copy-start(f32[4,21,56]{2,0,1:T(4,128)} %param.25) | copy-start | bytes 56452
  33.9 87.5 %collective-permute-start.2 = (f32[56,9,32]{0,1,2:T(8,128)}, f32[56,9,32]{0,1,2:T(8,128)}, u32[]{:S(2)}, u32[]{:S(2)}) collective-permute-start(f32[56,9,32]{0,1,2:T(8,128)} %bitcast.79), channel_id=1, source_target_pairs={{1,0},{2,1},{3,2},{4,3},{5,4},{6,5},{7,6},{8,7},{9,8},{10,9},{11,1... | collective-permute-start | bytes 193544 | tf_op jit(solution)/shard_map/ppermute | solution.py:18
  43.4 79.6 %collective-permute-start.3 = (f32[56,9,32]{0,1,2:T(8,128)}, f32[56,9,32]{0,1,2:T(8,128)}, u32[]{:S(2)}, u32[]{:S(2)}) collective-permute-start(f32[56,9,32]{0,1,2:T(8,128)} %bitcast.82), channel_id=1, source_target_pairs={{2,0},{3,1},{4,2},{5,3},{6,4},{7,5},{8,6},{9,7},{10,8},{11,9},{12,... | collective-permute-start | bytes 193544 | tf_op jit(solution)/shard_map/ppermute | solution.py:18
  63.1 6.5 %copy-start.4 = (f32[84,56]{1,0:T(8,128)}, f32[84,56]{1,0:T(8,128)S(1)}, u32[]{:S(2)}) copy-start(f32[84,56]{1,0:T(8,128)S(1)} %reshape.801) | copy-start | bytes 56452
  74.9 4.6 copy-start.56
  75.2 10.6 %copy-start.14 = (f32[24,8,4,128]{3,1,2,0:T(8,128)}, f32[24,8,4,128]{3,1,2,0:T(8,128)S(1)}, u32[]{:S(2)}) copy-start(f32[24,8,4,128]{3,1,2,0:T(8,128)S(1)} %copy.1264) | copy-start | bytes 1179652
  76.2 9.6 %copy-start.65 = (f32[4,56,21]{1,0,2:T(4,128)S(1)}, f32[4,56,21]{1,0,2:T(4,128)}, u32[]{:S(2)}) copy-start(f32[4,56,21]{1,0,2:T(4,128)} %param.26) | copy-start | bytes 56452
  84.7 4.7 copy-start.55
  95.2 4.8 copy-start.12
  96.6 4.4 copy-start.1
  96.7 5.6 %copy-start.63 = (f32[56,9,128]{2,0,1:T(8,128)S(1)}, f32[56,9,128]{2,0,1:T(8,128)}, u32[]{:S(2)}) copy-start(f32[56,9,128]{2,0,1:T(8,128)} %get-tuple-element.94) | copy-start | bytes 774148
  97.2 5.6 %copy-start.62 = (f32[56,9,128]{2,0,1:T(8,128)S(1)}, f32[56,9,128]{2,0,1:T(8,128)}, u32[]{:S(2)}) copy-start(f32[56,9,128]{2,0,1:T(8,128)} %get-tuple-element.93) | copy-start | bytes 774148
  221.1 54.7 %collective-permute-start.4 = (f32[56,9,32]{0,1,2:T(8,128)}, f32[56,9,32]{0,1,2:T(8,128)}, u32[]{:S(2)}, u32[]{:S(2)}) collective-permute-start(f32[56,9,32]{0,1,2:T(8,128)} %bitcast.1079), channel_id=1, source_target_pairs={{0,2},{1,3},{2,4},{3,5},{4,6},{5,7},{6,8},{7,9},{8,10},{9,11},{10,... | collective-permute-start | bytes 193544 | tf_op jit(solution)/shard_map/ppermute | solution.py:18
  250.5 20.7 %copy-start.3 = (f32[4,21,9,128]{3,2,1,0:T(8,128)S(1)}, f32[4,21,9,128]{3,2,1,0:T(8,128)}, u32[]{:S(2)}) copy-start(f32[4,21,9,128]{3,2,1,0:T(8,128)} %reshape.825) | copy-start | bytes 1161220
  257.4 20.1 %collective-permute-start.5 = (f32[56,9,32]{0,1,2:T(8,128)}, f32[56,9,32]{0,1,2:T(8,128)}, u32[]{:S(2)}, u32[]{:S(2)}) collective-permute-start(f32[56,9,32]{0,1,2:T(8,128)} %bitcast.145), channel_id=1, source_target_pairs={{0,1},{1,2},{2,3},{3,4},{4,5},{5,6},{6,7},{7,8},{8,9},{9,10},{10,1... | collective-permute-start | bytes 193544 | tf_op jit(solution)/shard_map/ppermute | solution.py:18
  259.3 19.9 %collective-permute-start.6 = (f32[56,9,32]{0,1,2:T(8,128)}, f32[56,9,32]{0,1,2:T(8,128)}, u32[]{:S(2)}, u32[]{:S(2)}) collective-permute-start(f32[56,9,32]{0,1,2:T(8,128)} %bitcast.146), channel_id=1, source_target_pairs={{1,0},{2,1},{3,2},{4,3},{5,4},{6,5},{7,6},{8,7},{9,8},{10,9},{11,1... | collective-permute-start | bytes 193544 | tf_op jit(solution)/shard_map/ppermute | solution.py:18
  267.2 13.7 %collective-permute-start.7 = (f32[56,9,32]{0,1,2:T(8,128)}, f32[56,9,32]{0,1,2:T(8,128)}, u32[]{:S(2)}, u32[]{:S(2)}) collective-permute-start(f32[56,9,32]{0,1,2:T(8,128)} %bitcast.147), channel_id=1, source_target_pairs={{2,0},{3,1},{4,2},{5,3},{6,4},{7,5},{8,6},{9,7},{10,8},{11,9},{12,... | collective-permute-start | bytes 193544 | tf_op jit(solution)/shard_map/ppermute | solution.py:18
  273.9 10.3 %copy-start.5 = (f32[84,56]{1,0:T(8,128)S(1)}, f32[84,56]{1,0:T(8,128)}, u32[]{:S(2)}) copy-start(f32[84,56]{1,0:T(8,128)} %copy-done.4) | copy-start | bytes 56452
  293.6 3.9 copy-start.9
  295.0 4.6 copy-start.71
  299.7 34.0 %copy-start.46 = (f32[56,3,64]{2,0,1:T(8,128)}, f32[56,3,64]{2,0,1:T(8,128)S(1)}, u32[]{:S(2)}) copy-start(f32[56,3,64]{2,0,1:T(8,128)S(1)} %get-tuple-element.105) | copy-start | bytes 129028
  347.7 49.6 %collective-permute-start.8 = (f32[56,9,32]{0,1,2:T(8,128)}, f32[56,9,32]{0,1,2:T(8,128)}, u32[]{:S(2)}, u32[]{:S(2)}) collective-permute-start(f32[56,9,32]{0,1,2:T(8,128)} %bitcast.1080), channel_id=1, source_target_pairs={{0,2},{1,3},{2,4},{3,5},{4,6},{5,7},{6,8},{7,9},{8,10},{9,11},{10,... | collective-permute-start | bytes 193544 | tf_op jit(solution)/shard_map/ppermute | solution.py:18
  380.3 18.0 %collective-permute-start.9 = (f32[56,9,32]{0,1,2:T(8,128)}, f32[56,9,32]{0,1,2:T(8,128)}, u32[]{:S(2)}, u32[]{:S(2)}) collective-permute-start(f32[56,9,32]{0,1,2:T(8,128)} %bitcast.207), channel_id=1, source_target_pairs={{0,1},{1,2},{2,3},{3,4},{4,5},{5,6},{6,7},{7,8},{8,9},{9,10},{10,1... | collective-permute-start | bytes 193544 | tf_op jit(solution)/shard_map/ppermute | solution.py:18
  382.2 17.1 %collective-permute-start.10 = (f32[56,9,32]{0,1,2:T(8,128)}, f32[56,9,32]{0,1,2:T(8,128)}, u32[]{:S(2)}, u32[]{:S(2)}) collective-permute-start(f32[56,9,32]{0,1,2:T(8,128)} %bitcast.208), channel_id=1, source_target_pairs={{1,0},{2,1},{3,2},{4,3},{5,4},{6,5},{7,6},{8,7},{9,8},{10,9},{11,1... | collective-permute-start | bytes 193544 | tf_op jit(solution)/shard_map/ppermute | solution.py:18
  390.1 10.2 %collective-permute-start.11 = (f32[56,9,32]{0,1,2:T(8,128)}, f32[56,9,32]{0,1,2:T(8,128)}, u32[]{:S(2)}, u32[]{:S(2)}) collective-permute-start(f32[56,9,32]{0,1,2:T(8,128)} %bitcast.209), channel_id=1, source_target_pairs={{2,0},{3,1},{4,2},{5,3},{6,4},{7,5},{8,6},{9,7},{10,8},{11,9},{12,... | collective-permute-start | bytes 193544 | tf_op jit(solution)/shard_map/ppermute | solution.py:18
  412.0 22.4 %copy-start.37 = (f32[56,3,64]{2,0,1:T(8,128)}, f32[56,3,64]{2,0,1:T(8,128)S(1)}, u32[]{:S(2)}) copy-start(f32[56,3,64]{2,0,1:T(8,128)S(1)} %get-tuple-element.103) | copy-start | bytes 129028
  444.2 47.3 %collective-permute-start.12 = (f32[56,9,32]{0,1,2:T(8,128)}, f32[56,9,32]{0,1,2:T(8,128)}, u32[]{:S(2)}, u32[]{:S(2)}) collective-permute-start(f32[56,9,32]{0,1,2:T(8,128)} %bitcast.260), channel_id=1, source_target_pairs={{0,2},{1,3},{2,4},{3,5},{4,6},{5,7},{6,8},{7,9},{8,10},{9,11},{10,... | collective-permute-start | bytes 193544 | tf_op jit(solution)/shard_map/ppermute | solution.py:18
  449.0 6.7 %copy-start.13 = (f32[4,9,9,64]{3,0,2,1:T(4,128)S(1)}, f32[4,9,9,64]{3,0,2,1:T(4,128)}, u32[]{:S(2)}) copy-start(f32[4,9,9,64]{3,0,2,1:T(4,128)} %copy-done.12) | copy-start | bytes 248836
  453.2 9.6 %copy-start.15 = (f32[24,8,4,128]{3,1,2,0:T(8,128)S(1)}, f32[24,8,4,128]{3,1,2,0:T(8,128)}, u32[]{:S(2)}) copy-start(f32[24,8,4,128]{3,1,2,0:T(8,128)} %copy-done.14) | copy-start | bytes 1179652
  453.2 9.6 %copy-start.17 = (f32[24,8,4,128]{3,1,2,0:T(8,128)S(1)}, f32[24,8,4,128]{3,1,2,0:T(8,128)}, u32[]{:S(2)}) copy-start(f32[24,8,4,128]{3,1,2,0:T(8,128)} %copy-done.16) | copy-start | bytes 1179652
  453.2 9.6 %copy-start.19 = (f32[24,8,4,128]{3,1,2,0:T(8,128)S(1)}, f32[24,8,4,128]{3,1,2,0:T(8,128)}, u32[]{:S(2)}) copy-start(f32[24,8,4,128]{3,1,2,0:T(8,128)} %copy-done.18) | copy-start | bytes 1179652
  470.3 12.7 %copy-start.54 = (f32[32,56,9]{1,2,0:T(8,128)S(1)}, f32[32,56,9]{1,2,0:T(8,128)}, u32[]{:S(2)}) copy-start(f32[32,56,9]{1,2,0:T(8,128)} %gather_fusion.29) | copy-start | bytes 193540
  471.7 16.3 %copy-start.59 = (f32[56,576]{1,0:T(8,128)S(1)}, f32[56,576]{1,0:T(8,128)}, u32[]{:S(2)}) copy-start(f32[56,576]{1,0:T(8,128)} %convolution_bitcast_fusion.18) | copy-start | bytes 387076
  472.0 17.0 %copy-start.36 = (f32[512,189]{0,1:T(8,128)S(1)}, f32[512,189]{0,1:T(8,128)}, u32[]{:S(2)}) copy-start(f32[512,189]{0,1:T(8,128)} %add_add_fusion.1) | copy-start | bytes 1161220
  473.0 16.2 %copy-start.73 = (s32[1024]{0:T(1024)S(1)}, s32[1024]{0:T(1024)}, u32[]{:S(2)}) copy-start(s32[1024]{0:T(1024)} %get-tuple-element.135) | copy-start | bytes 12292
  473.0 19.4 %collective-permute-start.13 = (f32[56,9,32]{0,1,2:T(8,128)}, f32[56,9,32]{0,1,2:T(8,128)}, u32[]{:S(2)}, u32[]{:S(2)}) collective-permute-start(f32[56,9,32]{0,1,2:T(8,128)} %bitcast.261), channel_id=1, source_target_pairs={{0,1},{1,2},{2,3},{3,4},{4,5},{5,6},{6,7},{7,8},{8,9},{9,10},{10,1... | collective-permute-start | bytes 193544 | tf_op jit(solution)/shard_map/ppermute | solution.py:18
  475.1 18.4 %collective-permute-start.14 = (f32[56,9,32]{0,1,2:T(8,128)}, f32[56,9,32]{0,1,2:T(8,128)}, u32[]{:S(2)}, u32[]{:S(2)}) collective-permute-start(f32[56,9,32]{0,1,2:T(8,128)} %bitcast.262), channel_id=1, source_target_pairs={{1,0},{2,1},{3,2},{4,3},{5,4},{6,5},{7,6},{8,7},{9,8},{10,9},{11,1... | collective-permute-start | bytes 193544 | tf_op jit(solution)/shard_map/ppermute | solution.py:18
  483.0 11.5 %collective-permute-start.15 = (f32[56,9,32]{0,1,2:T(8,128)S(1)}, f32[56,9,32]{0,1,2:T(8,128)S(1)}, u32[]{:S(2)}, u32[]{:S(2)}) collective-permute-start(f32[56,9,32]{0,1,2:T(8,128)S(1)} %bitcast.1081), channel_id=1, source_target_pairs={{2,0},{3,1},{4,2},{5,3},{6,4},{7,5},{8,6},{9,7},{10,8},{11,9},{12,... | collective-permute-start | bytes 193544 | tf_op jit(solution)/shard_map/ppermute | solution.py:18
  (60 other events, 107.5 us)
where the time goes:
time: 530 us; the launch traced here: 522 us
  local copies, waits for them, and re-layouts  307 us (58%)
  other arithmetic  74.3 us (14%)
  matrix products  72.2 us (14%)
  starting transfers between devices  65.3 us (12%)
    ppermute x16, starting transfers between devices, from_behind(): return lax.ppermute(value, axis, pairs)  65.3 us
    reduce_sum x35, other arithmetic, star_apply(): jnp.sum(jnp.expand_dims(matrices, -4) * jnp.expand_dims(values, -3), axis...  43.7 us
    dot_general x25, matrix products, apply_operator(): jnp.dot(left_matrix, stacked.reshape(left_matrix.shape[1], -1), precision...  40.4 us
    unnamed x229, local copies, waits for them, and re-layouts  35.4 us
    reshape x19, local copies, waits for them, and re-layouts, apply_operator(): stacked.reshape(left_matrix.shape[1], -1)  34.1 us
    dot_general x19, local copies, waits for them, and re-layouts, apply_operator(): jnp.dot(left_matrix, stacked.reshape(left_matrix.shape[1], -1), precision...  27.5 us
    gather x8, local copies, waits for them, and re-layouts, shards(): face_values[..., safe_rows]  23.2 us
    another operation x25, local copies, waits for them, and re-layouts, apply_operator(): jnp.stack([star_apply(sym[direction], values) for direction in range(3)])  22.7 us
  transfers between devices with their start and end apart: 16, of which 0 were waited for; matrix products, arithmetic and copies ran while one was open for 37% of the time, Pallas kernels for 0%

commit v1 on v0

v1 whole, which is shorter than its diff:
```python
import functools

import jax
import jax.numpy as jnp
from jax import lax
from jax.experimental import pallas as pl
from jax.experimental.pallas import tpu as pltpu
from jax.sharding import PartitionSpec as P

ORDER = 6
RATE = 4
F32 = jnp.float32
BF16 = jnp.bfloat16
NB = 56
NQ = 9
FR = 24
FA = 4 * FR
LN = 128
PK = 56


def dot(a, b):
    return jnp.dot(a, b, preferred_element_type=F32)


def exact(a, b):
    return jnp.dot(a, b, preferred_element_type=F32, precision=lax.Precision.HIGHEST)


def split(x):
    hi = x.astype(BF16)
    return hi, (x - hi.astype(F32)).astype(BF16)


def two_rows(w, pad):
    if w.shape[0] < pad:
        w = jnp.concatenate([w, jnp.zeros((pad - w.shape[0], w.shape[1]), F32)], axis=0)
    return jnp.concatenate(split(w), axis=0)


def times(w2, rhs, rows):
    half = w2.shape[0] // 2
    hi, lo = split(rhs)
    both = dot(w2, hi)
    return both[:rows] + both[half:half + rows] + dot(w2[:half], lo)[:rows]


def star_rows(s_ref, group, values):
    total = s_ref[group, 0:1, :] * values(0)
    for p in range(1, NQ):
        total = total + s_ref[group, p:p + 1, :] * values(p)
    return total


def operator(x_ref, s_ref, w2):
    out = []
    for q in range(NQ):
        stacked = jnp.concatenate(
            [star_rows(s_ref, c * NQ + q, lambda p: x_ref[p]) for c in range(3)], axis=0)
        out.append(times(w2, stacked, NB))
    return out


def traces(x_ref, p2, t_ref):
    for q in range(NQ):
        t_ref[q] = times(p2, x_ref[q], FA)


def lanes(shape):
    return lax.broadcasted_iota(jnp.int32, shape, len(shape) - 1)


def pick(rows, index):
    return jnp.take_along_axis(rows, index, axis=1, mode="promise_in_bounds")


def send(t_ref, se_ref, sf_ref, out_refs):
    elem = jnp.broadcast_to(se_ref[...], (FR, LN))
    face = jnp.broadcast_to(sf_ref[...], (FR, LN))
    rows = []
    for q in range(NQ):
        got = pick(t_ref[q, 0:FR], elem)
        for f in range(1, 4):
            got = jnp.where(face == f, pick(t_ref[q, f * FR:(f + 1) * FR], elem), got)
        rows.append(got)
    rows.append(jnp.zeros((4 * PK - NQ * FR, LN), F32))
    table = jnp.concatenate(rows, axis=0)
    group = lanes((PK, LN)) // 32
    for k in range(4):
        message = None
        for g in range(4):
            part = table[g * PK:(g + 1) * PK]
            if g != k:
                part = pltpu.roll(part, ((g - k) * 32) % LN, 1)
            message = part if message is None else jnp.where(group == g, part, message)
        out_refs[k][...] = message


def unpack(in_refs):
    group = lanes((PK, LN)) // 32
    parts = []
    for g in range(4):
        rows = None
        for k in range(4):
            part = in_refs[k][...]
            if g != k:
                part = pltpu.roll(part, ((k - g) * 32) % LN, 1)
            rows = part if rows is None else jnp.where(group == k, part, rows)
        parts.append(rows)
    return jnp.concatenate(parts, axis=0)


def local_pick(t_ref, nb_ref, nf_ref, out_ref):
    for f in range(4):
        where = jnp.broadcast_to(nb_ref[f:f + 1, :], (FR, LN))
        face = jnp.broadcast_to(nf_ref[f:f + 1, :], (FR, LN))
        elem = jnp.minimum(where, LN - 1)
        face = jnp.where(where < LN, face, 4)
        for q in range(NQ):
            got = jnp.zeros((FR, LN), F32)
            for g in range(4):
                got = jnp.where(face == g, pick(t_ref[q, g * FR:(g + 1) * FR], elem), got)
            out_ref[q, f * FR:(f + 1) * FR] = got


def ghost_pick(table, nb_ref, local_ref, out_ref):
    for f in range(4):
        where = jnp.broadcast_to(nb_ref[f:f + 1, :], (FR, LN))
        slot = jnp.clip(where - LN, 0, LN - 1)
        ghost = (where >= LN) & (where < 2 * LN)
        for q in range(NQ):
            got = pick(table[q * FR:(q + 1) * FR], slot)
            out_ref[q, f * FR:(f + 1) * FR] = jnp.where(
                ghost, got, local_ref[q, f * FR:(f + 1) * FR])


def flux_rows(f_ref, q, t_ref):
    return jnp.concatenate(
        [star_rows(f_ref, f * NQ + q, lambda p: t_ref[p, f * FR:(f + 1) * FR]) for f in range(4)],
        axis=0)


def own_term(f_ref, t_ref, l2, q):
    return times(l2, flux_rows(f_ref, q, t_ref), NB)


def orient_masks(or_ref):
    codes = jnp.concatenate(
        [jnp.broadcast_to(or_ref[f:f + 1, :], (FR, LN)) for f in range(4)], axis=0)
    return [(codes == k).astype(F32).astype(BF16) for k in range(3)]


def plastic(u_ref, cohesion):
    s = [u_ref[q, 0:1, :] for q in range(6)]
    mean = (s[0] + s[1] + s[2]) / 3.0
    dx, dy, dz = s[0] - mean, s[1] - mean, s[2] - mean
    second = 0.5 * (dx * dx + dy * dy + dz * dz) + s[3] * s[3] + s[4] * s[4] + s[5] * s[5]
    factor = cohesion / jnp.maximum(jnp.sqrt(second), cohesion)
    pressure = (u_ref[0] + u_ref[1] + u_ref[2]) / 3.0
    out = [pressure + factor * (u_ref[i] - pressure) for i in range(3)]
    out += [factor * u_ref[i] for i in range(3, 6)]
    return out + [u_ref[i] for i in range(6, NQ)]


def place(width, offset, rows):
    r = lax.broadcasted_iota(jnp.int32, (rows, width), 0)
    return (lanes((rows, width)) == r + offset).astype(F32)


def first_kernel(dofs, star, stiff, proj, se, sf, s_out, w2_out, p2_out, x_out, pieces, t_out,
                 m0, m1, m2, m3, series):
    for c in range(3):
        for q in range(NQ):
            s_out[c * NQ + q] = 0.5 * (star[c, q] + star[c, :, q, :])
    w = None
    for c in range(3):
        minus = 0.5 * (jnp.transpose(stiff[c]) - stiff[c])
        part = exact(minus, place(3 * NB, c * NB, NB))
        w = part if w is None else w + part
    w2_out[...] = two_rows(w, 64)
    faces = []
    for f in range(4):
        faces += [proj[f], jnp.zeros((FR - proj.shape[1], NB), F32)]
    p2_out[...] = two_rows(jnp.concatenate(faces, axis=0), FA)
    for q in range(NQ):
        x = dofs[:, q, :]
        x_out[q] = x
        series[q] = x
        for s in range(RATE):
            pieces[s, q] = x * (1.0 / RATE)

    def step(k, powers):
        kf = k.astype(F32)
        powers = [powers[j] * ((j + 1) / RATE / (kf + 2.0)) for j in range(RATE)]
        rows = operator(series, s_out, w2_out[...])
        for q in range(NQ):
            series[q] = rows[q]
            for s in range(RATE):
                weight = powers[s] - powers[s - 1] if s else powers[0]
                pieces[s, q] += weight * rows[q]
        return powers

    lax.fori_loop(0, ORDER - 1, step, [jnp.float32((j + 1) / RATE) for j in range(RATE)])
    traces(pieces.at[0], p2_out[...], t_out)
    send(t_out, se, sf, (m0, m1, m2, m3))


def lift_kernel(x_ref, s_ref, w2, p2, pieces, fm_ref, lift, rotate, l2_out, lr2_out, u_out,
                full, t_full):
    own, turned = None, [None] * 3
    for f in range(4):
        spot = place(FA, f * FR, lift.shape[2])
        part = exact(lift[f], spot)
        own = part if own is None else own + part
        for k in range(3):
            part = exact(exact(lift[f], rotate[k]), spot)
            turned[k] = part if turned[k] is None else turned[k] + part
    l2_out[...] = two_rows(own, 64)
    for k in range(3):
        lr2_out[k] = two_rows(turned[k], 64)
    for q in range(NQ):
        full[q] = pieces[0, q] + pieces[1, q] + pieces[2, q] + pieces[3, q]
    traces(full, p2[...], t_full)

    rows = operator(full, s_ref, w2[...])
    for q in range(NQ):
        u_out[q] = x_ref[q] + rows[q] - own_term(fm_ref, t_full, l2_out[...], q)


def local_kernel(q_ref, pred, t_ref, s_ref, w2, fm_ref, l2, nb_ref, nf_ref, u_out, n_out):
    rows = operator(pred, s_ref, w2[...])
    for q in range(NQ):
        u_out[q] = q_ref[q] + rows[q] - own_term(fm_ref, t_ref, l2[...], q)
    local_pick(t_ref, nb_ref, nf_ref, n_out)


def join_kernel(last, *refs):
    (g0, g1, g2, g3, q_ref, u_ref, nl_ref, nacc_ref, fp_ref, lr2, nb_ref, or_ref, coh, fine_ref,
     s_ref, w2, p2, piece, se, sf) = refs[:20]
    table = unpack((g0, g1, g2, g3))
    masks = orient_masks(or_ref)
    fine = fine_ref[...] == 1
    if last:
        uc_ref, out, n_ref, work = refs[20:]
    else:
        q_out, n_out, pred, t_out, m0, m1, m2, m3, n_ref, work, series = refs[20:]

    def face_terms(values):
        for q in range(NQ):
            hi, lo = split(flux_rows(fp_ref, q, n_ref))
            sub = None
            for k in range(3):
                w = lr2[k]
                both = dot(w, hi * masks[k])
                part = both[:NB] + both[64:64 + NB] + dot(w[:64], lo * masks[k])[:NB]
                sub = part if sub is None else sub + part
            work[q] = values[q] - sub

    ghost_pick(table, nb_ref, nl_ref, n_ref)
    face_terms(u_ref)
    after = plastic(work, coh[...])
    if last:
        for q in range(NQ):
            out[:, q, :] = after[q]
        for q in range(NQ):
            n_ref[q] += nacc_ref[q]
        face_terms(uc_ref)
        after = plastic(work, coh[...])
        for q in range(NQ):
            out[:, q, :] = jnp.where(fine, out[:, q, :], after[q])
        return
    for q in range(NQ):
        n_out[q] = nacc_ref[q] + n_ref[q] if nacc_ref is not None else n_ref[q]
        x = jnp.where(fine, after[q], q_ref[q])
        q_out[q] = x
        series[q] = x
        pred[q] = x * (1.0 / RATE)

    def step(k, weight):
        weight = weight * (1.0 / RATE / (k.astype(F32) + 2.0))
        rows = operator(series, s_ref, w2[...])
        for q in range(NQ):
            series[q] = rows[q]
            pred[q] += weight * rows[q]
        return weight

    lax.fori_loop(0, ORDER - 1, step, jnp.float32(1.0 / RATE))
    for q in range(NQ):
        pred[q] = jnp.where(fine, pred[q], piece[0, q])
    traces(pred, p2[...], t_out)
    send(t_out, se, sf, (m0, m1, m2, m3))


BIG = (NQ, NB, LN)
TAB = (NQ, FA, LN)
MSG = (PK, LN)


def call(kernel, name, outs, scratch, args, flops=50_000_000):
    return pl.pallas_call(
        kernel,
        name=name,
        out_shape=[jax.ShapeDtypeStruct(s, d) for s, d in outs],
        in_specs=[pl.BlockSpec(memory_space=pltpu.VMEM)] * len(args),
        out_specs=[pl.BlockSpec(memory_space=pltpu.VMEM)] * len(outs),
        scratch_shapes=[pltpu.VMEM(s, d) for s, d in scratch],
        compiler_params=pltpu.CompilerParams(vmem_limit_bytes=24 << 20),
        cost_estimate=pl.CostEstimate(flops=flops, bytes_accessed=4 << 20, transcendentals=0),
    )(*args)


def partners(devices):
    def pairing(step, start, ends):
        pairs = []
        for i in range(devices):
            j = i - start
            t = start + (j ^ step) if j >= 0 else -1
            if t < start or t >= devices:
                t = ends(i)
            pairs.append((i, t))
        return pairs
    return (
        pairing(1, 0, lambda i: i),
        pairing(1, 1, lambda i: devices - 1 - i),
        pairing(2, 0, lambda i: i),
        pairing(2, 2, lambda i: i ^ 1),
    )


def shards(dofs, star, flux_minus, flux_plus, cohesion, stiff, face_proj, lift, rotate, cluster,
           neighbor, neigh_face, orient, send_elem, send_face):
    devices = lax.axis_size("dom")
    me = lax.axis_index("dom")
    pairings = partners(devices)
    one_up = me % 2 == 0
    two_up = me % 4 < 2
    slots = send_elem.shape[1]

    def reorder(table):
        b0, b1, b2, b3 = table[0], table[1], table[2], table[3]
        return jnp.concatenate([
            jnp.where(one_up, b2, b1), jnp.where(one_up, b1, b2),
            jnp.where(two_up, b3, b0), jnp.where(two_up, b0, b3)]).reshape(1, 4 * slots)

    se, sf = reorder(send_elem), reorder(send_face)
    ghost = neighbor - LN
    block, slot = ghost // slots, ghost % slots
    one = (block == 1) | (block == 2)
    place_of = jnp.where(
        one,
        jnp.where((block == 2) == one_up, 0, 1),
        jnp.where((block == 3) == two_up, 2, 3))
    nb = jnp.where((ghost >= 0) & (ghost < 4 * slots), LN + place_of * slots + slot, neighbor)
    fm = flux_minus.reshape(4 * NQ, NQ, LN)
    fp = flux_plus.reshape(4 * NQ, NQ, LN)
    coh = cohesion.reshape(1, LN)
    fine = cluster.reshape(1, LN)

    def exchange(messages):
        got = [None] * 4
        for k in (2, 3, 1, 0):
            got[k] = lax.ppermute(messages[k], "dom", pairings[k])
        return got

    outs = call(
        first_kernel, "first",
        [((27, NQ, LN), F32), ((128, 3 * NB), BF16), ((2 * FA, NB), BF16), (BIG, F32),
         ((RATE,) + BIG, F32), (TAB, F32)] + [(MSG, F32)] * 4,
        [(BIG, F32)],
        [dofs, star, stiff, face_proj, se, sf])
    s_mat, w2, p2, state, pieces, table = outs[:6]
    got = exchange(outs[6:])
    l2, lr2, coarse = call(
        lift_kernel, "coarse_own",
        [((128, FA), BF16), ((3, 128, FA), BF16), (BIG, F32)],
        [(BIG, F32), (TAB, F32)],
        [state, s_mat, w2, p2, pieces, fm, lift, rotate])
    total = None
    pred = pieces[0]
    for sub in range(RATE):
        u, near = call(
            local_kernel, "local", [(BIG, F32), (TAB, F32)], [],
            [state, pred, table, s_mat, w2, fm, l2, nb, neigh_face])
        last = sub == RATE - 1
        common = [*got, state, u, near, total if total is not None else near, fp, lr2, nb, orient,
                  coh, fine, s_mat, w2, p2]
        if last:
            return call(
                functools.partial(join_kernel, True), "last",
                [((NB, NQ, LN), F32)],
                [(TAB, F32), (BIG, F32)],
                common + [pieces[3:4], se, sf, coarse])[0]
        first = total is None

        def kernel(*refs, first=first):
            refs = list(refs)
            if first:
                refs[7] = None
            join_kernel(False, *refs)

        outs = call(
            kernel, "join",
            [(BIG, F32), (TAB, F32), (BIG, F32), (TAB, F32)] + [(MSG, F32)] * 4,
            [(TAB, F32), (BIG, F32), (BIG, F32)],
            common + [pieces[sub + 1:sub + 2], se, sf])
        state, total, pred, table = outs[:4]
        got = exchange(outs[4:])


def solution(mesh):
    placed = (
        P(None, None, "dom"),
        P(None, None, None, "dom"),
        P(None, None, None, "dom"),
        P(None, None, None, "dom"),
        P("dom"),
        P(),
        P(),
        P(),
        P(),
        P("dom"),
        P(None, "dom"),
        P(None, "dom"),
        P(None, "dom"),
        P(None, "dom"),
        P(None, "dom"),
    )
    return jax.shard_map(
        shards, mesh=mesh, in_specs=placed, out_specs=P(None, None, "dom"), check_vma=False)
```

time: 530 us -> 80.1 us (0.15); the launches traced: 522 us -> 79.8 us
  local copies, waits for them, and re-layouts: 307 us -> 7.22 us
  other arithmetic: 74.3 us -> 0.18 us
  matrix products: 72.2 us -> 0 us
  starting transfers between devices: 65.3 us -> 20.7 us
  Pallas kernels: 0 us -> 32.1 us
  waiting for transfers between devices: 0.04 us -> 19.4 us
    gather x55 -> x0, local copies, waits for them, and re-layouts: 86.9 us -> none  [the longest x8 23.2 us: shards(): face_values[..., safe_rows]]
    reshape x65 -> x0, local copies, waits for them, and re-layouts: 73.5 us -> none  [the longest x19 34.1 us: apply_operator(): stacked.reshape(left_matrix.shape[1], -1)]
    dot_general x50 -> x0, matrix products: 72.2 us -> none  [the longest x25 40.4 us: apply_operator(): jnp.dot(left_matrix, stacked.reshape(left_matrix.shape[1], -1), precision...]
    ppermute x16, starting transfers between devices: 65.3 us -> 20.7 us  [exchange(): got[k] = lax.ppermute(messages[k], 'dom', pairings[k])]
    reduce_sum x36 -> x0, other arithmetic: 44.4 us -> none  [the longest x35 43.7 us: star_apply(): jnp.sum(jnp.expand_dims(matrices, -4) * jnp.expand_dims(values, -3), axis...]
    pallas_call x0 -> x10, Pallas kernels: none -> 32.1 us  [call(): pl.pallas_call(kernel, name=name, out_shape=[jax.ShapeDtypeStruct(s, d) f...]
    dot_general x27 -> x0, local copies, waits for them, and re-layouts: 31.2 us -> none  [the longest x19 27.5 us: apply_operator(): jnp.dot(left_matrix, stacked.reshape(left_matrix.shape[1], -1), precision...]
    unnamed x229 -> x32, local copies, waits for them, and re-layouts: 35.4 us -> 6.37 us
  transfers between devices with their start and end apart: 16 -> 16, of which waited for: 0 -> 7; matrix products, arithmetic and copies ran while one was open for 37% -> 2% of each run, Pallas kernels for 0% -> 11%
where the time goes in v1:
time: 80.1 us; the launch traced here: 79.8 us
  Pallas kernels  32.1 us (40%)
  starting transfers between devices  20.7 us (26%)
  waiting for transfers between devices  19.4 us (24%)
  local copies, waits for them, and re-layouts  7.22 us (9%)
    pallas_call x10, Pallas kernels, call(): pl.pallas_call(kernel, name=name, out_shape=[jax.ShapeDtypeStruct(s, d) f...  32.1 us
    ppermute x16, starting transfers between devices, exchange(): got[k] = lax.ppermute(messages[k], 'dom', pairings[k])  20.7 us
    ppermute x16, waiting for transfers between devices, exchange(): got[k] = lax.ppermute(messages[k], 'dom', pairings[k])  19.4 us
    unnamed x32, local copies, waits for them, and re-layouts  6.37 us
  transfers between devices with their start and end apart: 16, of which 7 were waited for; matrix products, arithmetic and copies ran while one was open for 2% of the time, Pallas kernels for 11%

profile of v1, /device:TPU:24, one launch (start us, length us, event | category | flops | bytes accessed | tf_op | source)
XLA Modules:
  0.0 79.8 jit_solution(15249609353429286346)
XLA Ops:
  0.0 0.8 copy-done.8
  0.8 0.9 %copy.17.star = f32[3,9,9,128]{3,2,1,0:T(8,128)S(1)} copy(f32[3,9,9,128]{3,0,2,1:T(4,128)} %param.16) | data formatting | bytes 248832 | tf_op args[1]
  1.7 0.0 copy-start.11
  1.8 0.0 copy-start
  1.8 0.1 copy.16.dofs
  1.9 0.6 copy-done.11
  2.4 0.0 copy-done.12
  2.4 0.1 add_bitcast_fusion.se.refs_18_
  2.5 0.1 add_bitcast_fusion.1.sf.refs_19_
  2.6 0.1 copy-done
  2.7 5.3 %first.1 = (f32[27,9,128]{2,1,0:T(8,128)S(1)}, bf16[128,168]{1,0:T(8,128)(2,1)S(1)}, bf16[192,56]{1,0:T(8,128)(2,1)S(1)}, f32[9,56,128]{2,1,0:T(8,128)S(1)}, f32...) custom-call(f32[56,9,128]{2,1,0:T(8,128)S(1)} %copy.16.dofs, ...), custom_call_target="tpu_custom_call" | custom-call | flops 50000000 | bytes 4194304 | tf_op jit(solution)/shard_map/first/pallas_call | solution.py:300
  7.9 0.1 collective-permute-start
  8.0 8.3 %collective-permute-start.1 = (f32[56,128]{1,0:T(8,128)S(1)}, f32[56,128]{1,0:T(8,128)S(1)}, u32[]{:S(2)}, u32[]{:S(2)}) collective-permute-start(f32[56,128]{1,0:T(8,128)S(1)} %get-tuple-element.51), channel_id=1, source_target_pairs={{0,255},{1,2},{2,1},{3,4},{4,3},{5,6},{6,5},{7,8},{8,7},{9,10},{10... | collective-permute-start | bytes 86024 | tf_op jit(solution)/shard_map/ppermute | solution.py:362
  16.4 1.4 %collective-permute-start.3 = (f32[56,128]{1,0:T(8,128)S(1)}, f32[56,128]{1,0:T(8,128)S(1)}, u32[]{:S(2)}, u32[]{:S(2)}) collective-permute-start(f32[56,128]{1,0:T(8,128)S(1)} %get-tuple-element.53), channel_id=1, source_target_pairs={{0,1},{1,0},{2,4},{3,5},{4,2},{5,3},{6,8},{7,9},{8,6},{9,7},{10,12... | collective-permute-start | bytes 86024 | tf_op jit(solution)/shard_map/ppermute | solution.py:362
  17.7 0.1 fusion.12
  17.8 0.6 copy-done.10
  18.4 0.1 copy-done.9
  18.5 0.1 copy.20.lift
  18.7 1.0 %copy.19 = f32[4,9,9,128]{3,2,1,0:T(8,128)S(1)} copy(f32[4,9,9,128]{3,0,2,1:T(4,128)} %param.17) | data formatting | bytes 331776 | tf_op args[2]
  19.7 0.7 copy-done.1
  20.4 2.9 %coarse_own.1 = (bf16[128,96]{1,0:T(8,128)(2,1)S(1)}, bf16[3,128,96]{2,1,0:T(8,128)(2,1)S(1)}, f32[9,56,128]{2,1,0:T(8,128)S(1)}) custom-call(f32[9,56,128]{2,1,0:T(8,128)S(1)} %get-tuple-element.54.x_ref.q_ref.refs_4_, f32[27,9,128]{2,1,0:T(8,128)S(1)} %get-tuple-element.57.s_ref.refs_14_, bf16[128,168]{1,0:T(8,128)(2,1)S(1)} %get-tuple-element.58.w2.refs_15_, ...), custom_call_target="tpu_custom_call" | custom-call | flops 50000000 | bytes 4194304 | tf_op jit(solution)/shard_map/coarse_own/pallas_call | solution.py:300
  23.3 0.7 copy-done.2
  24.0 1.4 %local.4 = (f32[9,56,128]{2,1,0:T(8,128)S(1)}, f32[9,96,128]{2,1,0:T(8,128)S(1)}) custom-call(f32[9,56,128]{2,1,0:T(8,128)S(1)} %get-tuple-element.54.x_ref.q_ref.refs_4_, f32[9,56,128]{2,1,0:T(8,128)S(1)} %get-tuple-element.98.pred, f32[9,96,128]{2,1,0:T(8,128)S(1)} %get-tuple-element.56.t_ref, f32[27,9,128]{2,1,0:T(8,128)S(1)} %get-tuple-element.57.s_ref.refs_14_, ...), custom_call_target="tpu_custom_call" | custom-call | flops 50000000 | bytes 4194304 | tf_op jit(solution)/shard_map/local/pallas_call | solution.py:300
  25.5 0.6 copy-done.3
  26.2 5.5 %join.3 = (f32[9,56,128]{2,1,0:T(8,128)S(1)}, f32[9,96,128]{2,1,0:T(8,128)S(1)}, f32[9,56,128]{2,1,0:T(8,128)S(1)}, f32[9,96,128]{2,1,0:T(8,128)S(1)}, f32[56,12...) custom-call(f32[56,128]{1,0:T(8,128)S(1)} %collective-permute-done.refs_0_, ...), custom_call_target="tpu_custom_call" | custom-call | flops 50000000 | bytes 4194304 | tf_op jit(solution)/shard_map/join/pallas_call | solution.py:300
  31.6 0.3 collective-permute-start.4
  31.9 4.8 %collective-permute-start.5 = (f32[56,128]{1,0:T(8,128)S(1)}, f32[56,128]{1,0:T(8,128)S(1)}, u32[]{:S(2)}, u32[]{:S(2)}) collective-permute-start(f32[56,128]{1,0:T(8,128)S(1)} %get-tuple-element.65), channel_id=1, source_target_pairs={{0,255},{1,2},{2,1},{3,4},{4,3},{5,6},{6,5},{7,8},{8,7},{9,10},{10... | collective-permute-start | bytes 86024 | tf_op jit(solution)/shard_map/ppermute | solution.py:362
  36.7 0.4 collective-permute-start.7
  37.1 1.4 %local.5 = (f32[9,56,128]{2,1,0:T(8,128)S(1)}, f32[9,96,128]{2,1,0:T(8,128)S(1)}) custom-call(f32[9,56,128]{2,1,0:T(8,128)S(1)} %get-tuple-element.68.q_ref.refs_4_, f32[9,56,128]{2,1,0:T(8,128)S(1)} %get-tuple-element.69.pred, f32[9,96,128]{2,1,0:T(8,128)S(1)} %get-tuple-element.70.t_ref, f32[27,9,128]{2,1,0:T(8,128)S(1)} %get-tuple-element.57.s_ref.refs_14_, ...), custom_call_target="tpu_custom_call" | custom-call | flops 50000000 | bytes 4194304 | tf_op jit(solution)/shard_map/local/pallas_call | solution.py:300
  38.5 1.0 %collective-permute-done.5.refs_1_ = f32[56,128]{1,0:T(8,128)S(1)} collective-permute-done((f32[56,128]{1,0:T(8,128)S(1)}, f32[56,128]{1,0:T(8,128)S(1)}, u32[]{:S(2)}, u32[]{:S(2)}) %collective-permute-start.5) | collective-permute-done | bytes 28704 | tf_op jit(solution)/shard_map/ppermute | solution.py:362
  39.5 1.1 %collective-permute-done.6.refs_2_ = f32[56,128]{1,0:T(8,128)S(1)} collective-permute-done((f32[56,128]{1,0:T(8,128)S(1)}, f32[56,128]{1,0:T(8,128)S(1)}, u32[]{:S(2)}, u32[]{:S(2)}) %collective-permute-start.6) | collective-permute-done | bytes 28704 | tf_op jit(solution)/shard_map/ppermute | solution.py:362
  40.6 4.2 %collective-permute-done.7.refs_3_ = f32[56,128]{1,0:T(8,128)S(1)} collective-permute-done((f32[56,128]{1,0:T(8,128)S(1)}, f32[56,128]{1,0:T(8,128)S(1)}, u32[]{:S(2)}, u32[]{:S(2)}) %collective-permute-start.7) | collective-permute-done | bytes 28704 | tf_op jit(solution)/shard_map/ppermute | solution.py:362
  44.8 5.5 %join.4 = (f32[9,56,128]{2,1,0:T(8,128)S(1)}, f32[9,96,128]{2,1,0:T(8,128)S(1)}, f32[9,56,128]{2,1,0:T(8,128)S(1)}, f32[9,96,128]{2,1,0:T(8,128)S(1)}, f32[56,12...) custom-call(f32[56,128]{1,0:T(8,128)S(1)} %collective-permute-done.4.refs_0_, ...), custom_call_target="tpu_custom_call" | custom-call | flops 50000000 | bytes 4194304 | tf_op jit(solution)/shard_map/join/pallas_call | solution.py:300
  50.3 0.1 collective-permute-start.8
  50.4 0.5 collective-permute-start.9
  50.9 1.7 %collective-permute-start.10 = (f32[56,128]{1,0:T(8,128)S(1)}, f32[56,128]{1,0:T(8,128)S(1)}, u32[]{:S(2)}, u32[]{:S(2)}) collective-permute-start(f32[56,128]{1,0:T(8,128)S(1)} %get-tuple-element.76), channel_id=1, source_target_pairs={{0,2},{1,3},{2,0},{3,1},{4,6},{5,7},{6,4},{7,5},{8,10},{9,11},{10,... | collective-permute-start | bytes 86024 | tf_op jit(solution)/shard_map/ppermute | solution.py:362
  52.5 1.4 %local.6 = (f32[9,56,128]{2,1,0:T(8,128)S(1)}, f32[9,96,128]{2,1,0:T(8,128)S(1)}) custom-call(f32[9,56,128]{2,1,0:T(8,128)S(1)} %get-tuple-element.78.q_ref.refs_4_, f32[9,56,128]{2,1,0:T(8,128)S(1)} %get-tuple-element.79.pred, f32[9,96,128]{2,1,0:T(8,128)S(1)} %get-tuple-element.80.t_ref, f32[27,9,128]{2,1,0:T(8,128)S(1)} %get-tuple-element.57.s_ref.refs_14_, ...), custom_call_target="tpu_custom_call" | custom-call | flops 50000000 | bytes 4194304 | tf_op jit(solution)/shard_map/local/pallas_call | solution.py:300
  54.0 4.1 %collective-permute-done.9.refs_1_ = f32[56,128]{1,0:T(8,128)S(1)} collective-permute-done((f32[56,128]{1,0:T(8,128)S(1)}, f32[56,128]{1,0:T(8,128)S(1)}, u32[]{:S(2)}, u32[]{:S(2)}) %collective-permute-start.9) | collective-permute-done | bytes 28704 | tf_op jit(solution)/shard_map/ppermute | solution.py:362
  58.0 2.6 %collective-permute-done.11.refs_3_ = f32[56,128]{1,0:T(8,128)S(1)} collective-permute-done((f32[56,128]{1,0:T(8,128)S(1)}, f32[56,128]{1,0:T(8,128)S(1)}, u32[]{:S(2)}, u32[]{:S(2)}) %collective-permute-start.11) | collective-permute-done | bytes 28704 | tf_op jit(solution)/shard_map/ppermute | solution.py:362
  60.6 5.5 %join.5 = (f32[9,56,128]{2,1,0:T(8,128)S(1)}, f32[9,96,128]{2,1,0:T(8,128)S(1)}, f32[9,56,128]{2,1,0:T(8,128)S(1)}, f32[9,96,128]{2,1,0:T(8,128)S(1)}, f32[56,12...) custom-call(f32[56,128]{1,0:T(8,128)S(1)} %collective-permute-done.8.refs_0_, ...), custom_call_target="tpu_custom_call" | custom-call | flops 50000000 | bytes 4194304 | tf_op jit(solution)/shard_map/join/pallas_call | solution.py:300
  66.1 0.1 collective-permute-start.12
  66.2 2.9 %collective-permute-start.13 = (f32[56,128]{1,0:T(8,128)S(1)}, f32[56,128]{1,0:T(8,128)S(1)}, u32[]{:S(2)}, u32[]{:S(2)}) collective-permute-start(f32[56,128]{1,0:T(8,128)S(1)} %get-tuple-element.85), channel_id=1, source_target_pairs={{0,255},{1,2},{2,1},{3,4},{4,3},{5,6},{6,5},{7,8},{8,7},{9,10},{10... | collective-permute-start | bytes 86024 | tf_op jit(solution)/shard_map/ppermute | solution.py:362
  69.1 0.3 collective-permute-start.15
  69.4 1.4 %local.7 = (f32[9,56,128]{2,1,0:T(8,128)S(1)}, f32[9,96,128]{2,1,0:T(8,128)S(1)}) custom-call(f32[9,56,128]{2,1,0:T(8,128)S(1)} %get-tuple-element.88.q_ref.refs_4_, f32[9,56,128]{2,1,0:T(8,128)S(1)} %get-tuple-element.89.pred, f32[9,96,128]{2,1,0:T(8,128)S(1)} %get-tuple-element.90.t_ref, f32[27,9,128]{2,1,0:T(8,128)S(1)} %get-tuple-element.57.s_ref.refs_14_, ...), custom_call_target="tpu_custom_call" | custom-call | flops 50000000 | bytes 4194304 | tf_op jit(solution)/shard_map/local/pallas_call | solution.py:300
  70.8 3.0 %collective-permute-done.13.refs_1_ = f32[56,128]{1,0:T(8,128)S(1)} collective-permute-done((f32[56,128]{1,0:T(8,128)S(1)}, f32[56,128]{1,0:T(8,128)S(1)}, u32[]{:S(2)}, u32[]{:S(2)}) %collective-permute-start.13) | collective-permute-done | bytes 28704 | tf_op jit(solution)/shard_map/ppermute | solution.py:362
  73.8 3.4 %collective-permute-done.15.refs_3_ = f32[56,128]{1,0:T(8,128)S(1)} collective-permute-done((f32[56,128]{1,0:T(8,128)S(1)}, f32[56,128]{1,0:T(8,128)S(1)}, u32[]{:S(2)}, u32[]{:S(2)}) %collective-permute-start.15) | collective-permute-done | bytes 28704 | tf_op jit(solution)/shard_map/ppermute | solution.py:362
  77.2 1.9 %last.1 = f32[56,9,128]{2,1,0:T(8,128)S(1)} custom-call(f32[56,128]{1,0:T(8,128)S(1)} %collective-permute-done.12.refs_0_, f32[56,128]{1,0:T(8,128)S(1)} %collective-permute-done.13.refs_1_, f32[56,128]{1,0:T(8,128)S(1)} %collective-permute-done.14.refs_2_, f32[56,128]{1,0:T(8,128)S(1)} %collective-permute-done.15.refs_3_, ...), custom_call_target="tpu_custom_call" | custom-call | flops 50000000 | bytes 4194304 | tf_op jit(solution)/shard_map/last/pallas_call | solution.py:300
  79.0 0.8 copy.22
  (32 shorter events, 0.1 us)
Async XLA Ops:
  0.0 0.8 copy-start.8
  0.0 1.7 %copy-start.6 = (f32[56,9,128]{2,0,1:T(8,128)S(1)}, f32[56,9,128]{2,0,1:T(8,128)}, u32[]{:S(2)}) copy-start(f32[56,9,128]{2,0,1:T(8,128)} %param.15) | copy-start | bytes 774148
  1.7 0.7 copy-start.11
  1.8 0.7 copy-start.12
  1.8 0.9 %copy-start = (f32[3,56,56]{2,1,0:T(8,128)S(1)}, f32[3,56,56]{2,1,0:T(8,128)}, u32[]{:S(2)}) copy-start(f32[3,56,56]{2,1,0:T(8,128)} %stiff.1) | copy-start | bytes 112900
  7.9 17.5 %collective-permute-start = (f32[56,128]{1,0:T(8,128)S(1)}, f32[56,128]{1,0:T(8,128)S(1)}, u32[]{:S(2)}, u32[]{:S(2)}) collective-permute-start(f32[56,128]{1,0:T(8,128)S(1)} %get-tuple-element.50), channel_id=1, source_target_pairs={{0,1},{1,0},{2,3},{3,2},{4,5},{5,4},{6,7},{7,6},{8,9},{9,8},{10,11... | collective-permute-start | bytes 86024 | tf_op jit(solution)/shard_map/ppermute | solution.py:362
  8.0 17.4 %collective-permute-start.1 = (f32[56,128]{1,0:T(8,128)S(1)}, f32[56,128]{1,0:T(8,128)S(1)}, u32[]{:S(2)}, u32[]{:S(2)}) collective-permute-start(f32[56,128]{1,0:T(8,128)S(1)} %get-tuple-element.51), channel_id=1, source_target_pairs={{0,255},{1,2},{2,1},{3,4},{4,3},{5,6},{6,5},{7,8},{8,7},{9,10},{10... | collective-permute-start | bytes 86024 | tf_op jit(solution)/shard_map/ppermute | solution.py:362
  16.4 9.1 %collective-permute-start.2 = (f32[56,128]{1,0:T(8,128)S(1)}, f32[56,128]{1,0:T(8,128)S(1)}, u32[]{:S(2)}, u32[]{:S(2)}) collective-permute-start(f32[56,128]{1,0:T(8,128)S(1)} %get-tuple-element.52), channel_id=1, source_target_pairs={{0,2},{1,3},{2,0},{3,1},{4,6},{5,7},{6,4},{7,5},{8,10},{9,11},{10,... | collective-permute-start | bytes 86024 | tf_op jit(solution)/shard_map/ppermute | solution.py:362
  16.4 9.1 %collective-permute-start.3 = (f32[56,128]{1,0:T(8,128)S(1)}, f32[56,128]{1,0:T(8,128)S(1)}, u32[]{:S(2)}, u32[]{:S(2)}) collective-permute-start(f32[56,128]{1,0:T(8,128)S(1)} %get-tuple-element.53), channel_id=1, source_target_pairs={{0,1},{1,0},{2,4},{3,5},{4,2},{5,3},{6,8},{7,9},{8,6},{9,7},{10,12... | collective-permute-start | bytes 86024 | tf_op jit(solution)/shard_map/ppermute | solution.py:362
  17.7 0.7 copy-start.10
  17.7 0.8 copy-start.9
  18.6 1.0 %copy-start.7 = (f32[4,9,9,128]{3,0,2,1:T(4,128)S(1)}, f32[4,9,9,128]{3,0,2,1:T(4,128)}, u32[]{:S(2)}) copy-start(f32[4,9,9,128]{3,0,2,1:T(4,128)} %param.18) | copy-start | bytes 497668
  19.7 0.8 copy-start.1
  23.3 0.7 copy-start.2
  25.5 0.7 copy-start.3
  25.5 0.7 copy-start.4
  25.5 0.7 copy-start.5
  31.6 6.9 %collective-permute-start.4 = (f32[56,128]{1,0:T(8,128)S(1)}, f32[56,128]{1,0:T(8,128)S(1)}, u32[]{:S(2)}, u32[]{:S(2)}) collective-permute-start(f32[56,128]{1,0:T(8,128)S(1)} %get-tuple-element.64), channel_id=1, source_target_pairs={{0,1},{1,0},{2,3},{3,2},{4,5},{5,4},{6,7},{7,6},{8,9},{9,8},{10,11... | collective-permute-start | bytes 86024 | tf_op jit(solution)/shard_map/ppermute | solution.py:362
  31.9 7.5 %collective-permute-start.5 = (f32[56,128]{1,0:T(8,128)S(1)}, f32[56,128]{1,0:T(8,128)S(1)}, u32[]{:S(2)}, u32[]{:S(2)}) collective-permute-start(f32[56,128]{1,0:T(8,128)S(1)} %get-tuple-element.65), channel_id=1, source_target_pairs={{0,255},{1,2},{2,1},{3,4},{4,3},{5,6},{6,5},{7,8},{8,7},{9,10},{10... | collective-permute-start | bytes 86024 | tf_op jit(solution)/shard_map/ppermute | solution.py:362
  36.7 3.9 %collective-permute-start.6 = (f32[56,128]{1,0:T(8,128)S(1)}, f32[56,128]{1,0:T(8,128)S(1)}, u32[]{:S(2)}, u32[]{:S(2)}) collective-permute-start(f32[56,128]{1,0:T(8,128)S(1)} %get-tuple-element.66), channel_id=1, source_target_pairs={{0,2},{1,3},{2,0},{3,1},{4,6},{5,7},{6,4},{7,5},{8,10},{9,11},{10,... | collective-permute-start | bytes 86024 | tf_op jit(solution)/shard_map/ppermute | solution.py:362
  36.7 8.1 %collective-permute-start.7 = (f32[56,128]{1,0:T(8,128)S(1)}, f32[56,128]{1,0:T(8,128)S(1)}, u32[]{:S(2)}, u32[]{:S(2)}) collective-permute-start(f32[56,128]{1,0:T(8,128)S(1)} %get-tuple-element.67), channel_id=1, source_target_pairs={{0,1},{1,0},{2,4},{3,5},{4,2},{5,3},{6,8},{7,9},{8,6},{9,7},{10,12... | collective-permute-start | bytes 86024 | tf_op jit(solution)/shard_map/ppermute | solution.py:362
  50.3 3.6 %collective-permute-start.8 = (f32[56,128]{1,0:T(8,128)S(1)}, f32[56,128]{1,0:T(8,128)S(1)}, u32[]{:S(2)}, u32[]{:S(2)}) collective-permute-start(f32[56,128]{1,0:T(8,128)S(1)} %get-tuple-element.74), channel_id=1, source_target_pairs={{0,1},{1,0},{2,3},{3,2},{4,5},{5,4},{6,7},{7,6},{8,9},{9,8},{10,11... | collective-permute-start | bytes 86024 | tf_op jit(solution)/shard_map/ppermute | solution.py:362
  50.4 7.6 %collective-permute-start.9 = (f32[56,128]{1,0:T(8,128)S(1)}, f32[56,128]{1,0:T(8,128)S(1)}, u32[]{:S(2)}, u32[]{:S(2)}) collective-permute-start(f32[56,128]{1,0:T(8,128)S(1)} %get-tuple-element.75), channel_id=1, source_target_pairs={{0,255},{1,2},{2,1},{3,4},{4,3},{5,6},{6,5},{7,8},{8,7},{9,10},{10... | collective-permute-start | bytes 86024 | tf_op jit(solution)/shard_map/ppermute | solution.py:362
  50.9 7.1 %collective-permute-start.10 = (f32[56,128]{1,0:T(8,128)S(1)}, f32[56,128]{1,0:T(8,128)S(1)}, u32[]{:S(2)}, u32[]{:S(2)}) collective-permute-start(f32[56,128]{1,0:T(8,128)S(1)} %get-tuple-element.76), channel_id=1, source_target_pairs={{0,2},{1,3},{2,0},{3,1},{4,6},{5,7},{6,4},{7,5},{8,10},{9,11},{10,... | collective-permute-start | bytes 86024 | tf_op jit(solution)/shard_map/ppermute | solution.py:362
  52.5 8.1 %collective-permute-start.11 = (f32[56,128]{1,0:T(8,128)S(1)}, f32[56,128]{1,0:T(8,128)S(1)}, u32[]{:S(2)}, u32[]{:S(2)}) collective-permute-start(f32[56,128]{1,0:T(8,128)S(1)} %get-tuple-element.77), channel_id=1, source_target_pairs={{0,1},{1,0},{2,4},{3,5},{4,2},{5,3},{6,8},{7,9},{8,6},{9,7},{10,12... | collective-permute-start | bytes 86024 | tf_op jit(solution)/shard_map/ppermute | solution.py:362
  66.1 4.7 %collective-permute-start.12 = (f32[56,128]{1,0:T(8,128)S(1)}, f32[56,128]{1,0:T(8,128)S(1)}, u32[]{:S(2)}, u32[]{:S(2)}) collective-permute-start(f32[56,128]{1,0:T(8,128)S(1)} %get-tuple-element.84), channel_id=1, source_target_pairs={{0,1},{1,0},{2,3},{3,2},{4,5},{5,4},{6,7},{7,6},{8,9},{9,8},{10,11... | collective-permute-start | bytes 86024 | tf_op jit(solution)/shard_map/ppermute | solution.py:362
  66.2 7.6 %collective-permute-start.13 = (f32[56,128]{1,0:T(8,128)S(1)}, f32[56,128]{1,0:T(8,128)S(1)}, u32[]{:S(2)}, u32[]{:S(2)}) collective-permute-start(f32[56,128]{1,0:T(8,128)S(1)} %get-tuple-element.85), channel_id=1, source_target_pairs={{0,255},{1,2},{2,1},{3,4},{4,3},{5,6},{6,5},{7,8},{8,7},{9,10},{10... | collective-permute-start | bytes 86024 | tf_op jit(solution)/shard_map/ppermute | solution.py:362
  69.1 4.7 %collective-permute-start.14 = (f32[56,128]{1,0:T(8,128)S(1)}, f32[56,128]{1,0:T(8,128)S(1)}, u32[]{:S(2)}, u32[]{:S(2)}) collective-permute-start(f32[56,128]{1,0:T(8,128)S(1)} %get-tuple-element.86), channel_id=1, source_target_pairs={{0,2},{1,3},{2,0},{3,1},{4,6},{5,7},{6,4},{7,5},{8,10},{9,11},{10,... | collective-permute-start | bytes 86024 | tf_op jit(solution)/shard_map/ppermute | solution.py:362
  69.1 8.1 %collective-permute-start.15 = (f32[56,128]{1,0:T(8,128)S(1)}, f32[56,128]{1,0:T(8,128)S(1)}, u32[]{:S(2)}, u32[]{:S(2)}) collective-permute-start(f32[56,128]{1,0:T(8,128)S(1)} %get-tuple-element.87), channel_id=1, source_target_pairs={{0,1},{1,0},{2,4},{3,5},{4,2},{5,3},{6,8},{7,9},{8,6},{9,7},{10,12... | collective-permute-start | bytes 86024 | tf_op jit(solution)/shard_map/ppermute | solution.py:362

commit v2 on v1

--- a/solution.py
+++ b/solution.py
@@ -1,4 +1,5 @@
 import functools
+import math
 
 import jax
 import jax.numpy as jnp
@@ -45,10 +46,10 @@
     return both[:rows] + both[half:half + rows] + dot(w2[:half], lo)[:rows]
 
 
-def star_rows(s_ref, group, values):
-    total = s_ref[group, 0:1, :] * values(0)
+def star_rows(s_ref, q, which, values):
+    total = s_ref[q, 0, which:which + 1, :] * values(0)
     for p in range(1, NQ):
-        total = total + s_ref[group, p:p + 1, :] * values(p)
+        total = total + s_ref[q, p, which:which + 1, :] * values(p)
     return total
 
 
@@ -56,7 +57,7 @@
     out = []
     for q in range(NQ):
         stacked = jnp.concatenate(
-            [star_rows(s_ref, c * NQ + q, lambda p: x_ref[p]) for c in range(3)], axis=0)
+            [star_rows(s_ref, q, c, lambda p: x_ref[p]) for c in range(3)], axis=0)
         out.append(times(w2, stacked, NB))
     return out
 
@@ -136,7 +137,7 @@
 
 def flux_rows(f_ref, q, t_ref):
     return jnp.concatenate(
-        [star_rows(f_ref, f * NQ + q, lambda p: t_ref[p, f * FR:(f + 1) * FR]) for f in range(4)],
+        [star_rows(f_ref, q, f, lambda p: t_ref[p, f * FR:(f + 1) * FR]) for f in range(4)],
         axis=0)
 
 
@@ -167,71 +168,118 @@
     return (lanes((rows, width)) == r + offset).astype(F32)
 
 
-def first_kernel(dofs, star, stiff, proj, se, sf, s_out, w2_out, p2_out, x_out, pieces, t_out,
-                 m0, m1, m2, m3, series):
-    for c in range(3):
-        for q in range(NQ):
-            s_out[c * NQ + q] = 0.5 * (star[c, q] + star[c, :, q, :])
-    w = None
-    for c in range(3):
-        minus = 0.5 * (jnp.transpose(stiff[c]) - stiff[c])
-        part = exact(minus, place(3 * NB, c * NB, NB))
-        w = part if w is None else w + part
-    w2_out[...] = two_rows(w, 64)
+def weigh(series, end, begin, q):
+    total = None
+    for k in range(ORDER):
+        term = (end ** (k + 1) - begin ** (k + 1)) / math.factorial(k + 1) * series[k, q]
+        total = term if total is None else total + term
+    return total
+
+
+def slot_row(table, one_up, two_up):
+    values = table[...].astype(F32).astype(BF16)
+    total = None
+    for k, (here, there, up) in enumerate(
+            ((2, 1, one_up), (1, 2, one_up), (3, 0, two_up), (0, 3, two_up))):
+        spread = dot(values, place(LN, 32 * k, 32).astype(BF16))
+        row = jnp.where(up, spread[here:here + 1], spread[there:there + 1])
+        total = row if total is None else total + row
+    return total.astype(jnp.int32)
+
+
+def first_kernel(*refs):
+    ins, outs, scratch = refs[:15], refs[15:36], refs[36:]
+    (s_out, w2_out, p2_out, series, piece, t_out, m0, m1, m2, m3, se_out, sf_out, nb_out) = outs[:13]
+    fm_out, fp_out, nf_out, or_out, coh_out, fine_out, lift_out, turn_out = outs[13:]
+    star, stiff, proj, se, sf, nb, sems = scratch
+    places = (series.at[0], star, fm_out, fp_out, coh_out, stiff, proj, lift_out, turn_out, fine_out, nb,
+              nf_out, or_out, se, sf)
+    copies = [pltpu.make_async_copy(a, b, sems.at[n]) for n, (a, b) in enumerate(zip(ins, places))]
+    early = (5, 1, 0, 6, 13, 14)
+    rest = [n for n in range(15) if n not in early]
+    for n in early:
+        copies[n].start()
+    for n in rest:
+        copies[n].start()
+    copies[5].wait()
+    minus = [0.5 * (jnp.transpose(stiff[c]) - stiff[c]) for c in range(3)]
+    w2_out[...] = two_rows(jnp.concatenate(minus, axis=1), 64)
+    copies[1].wait()
+    for q in range(NQ):
+        for p in range(q + 1):
+            s_out[q, p] = 0.5 * (star[q, p] + star[p, q])
+            if p != q:
+                s_out[p, q] = s_out[q, p]
+    copies[0].wait()
+    for q in range(NQ):
+        piece[q] = series[0, q] * (1.0 / RATE)
+
+    def step(k, weight):
+        weight = weight * (1.0 / RATE / (k.astype(F32) + 2.0))
+        rows = operator(series.at[k], s_out, w2_out[...])
+        for q in range(NQ):
+            series[k + 1, q] = rows[q]
+            piece[q] += weight * rows[q]
+        return weight
+
+    lax.fori_loop(0, ORDER - 1, step, jnp.float32(1.0 / RATE))
+    for n in (6, 13, 14):
+        copies[n].wait()
     faces = []
     for f in range(4):
-        faces += [proj[f], jnp.zeros((FR - proj.shape[1], NB), F32)]
+        faces += [proj[:, f, :], jnp.zeros((FR - proj.shape[0], NB), F32)]
     p2_out[...] = two_rows(jnp.concatenate(faces, axis=0), FA)
-    for q in range(NQ):
-        x = dofs[:, q, :]
-        x_out[q] = x
-        series[q] = x
-        for s in range(RATE):
-            pieces[s, q] = x * (1.0 / RATE)
-
-    def step(k, powers):
-        kf = k.astype(F32)
-        powers = [powers[j] * ((j + 1) / RATE / (kf + 2.0)) for j in range(RATE)]
-        rows = operator(series, s_out, w2_out[...])
-        for q in range(NQ):
-            series[q] = rows[q]
-            for s in range(RATE):
-                weight = powers[s] - powers[s - 1] if s else powers[0]
-                pieces[s, q] += weight * rows[q]
-        return powers
-
-    lax.fori_loop(0, ORDER - 1, step, [jnp.float32((j + 1) / RATE) for j in range(RATE)])
-    traces(pieces.at[0], p2_out[...], t_out)
-    send(t_out, se, sf, (m0, m1, m2, m3))
-
-
-def lift_kernel(x_ref, s_ref, w2, p2, pieces, fm_ref, lift, rotate, l2_out, lr2_out, u_out,
-                full, t_full):
-    own, turned = None, [None] * 3
+    me = lax.axis_index("dom")
+    one_up = lax.rem(me, 2) == 0
+    two_up = lax.rem(me, 4) < 2
+    se_out[...] = slot_row(se, one_up, two_up)
+    sf_out[...] = slot_row(sf, one_up, two_up)
+    traces(piece, p2_out[...], t_out)
+    send(t_out, se_out, sf_out, (m0, m1, m2, m3))
+    for n in rest:
+        copies[n].wait()
+    two = jnp.where(one_up, 0, 1)
+    three = jnp.where(two_up, 2, 3)
+    ghost = nb[...] - LN
+    block, slot = ghost >> 5, ghost & 31
+    place_of = jnp.where(
+        block == 2, two, jnp.where(block == 1, 1 - two, jnp.where(block == 3, three, 5 - three)))
+    nb_out[...] = jnp.where((ghost >= 0) & (ghost < LN), LN + place_of * 32 + slot, nb[...])
+
+
+def lift_kernel(lift, rotate, l2_out, lr2_out):
+    gap = jnp.zeros((FR - lift.shape[0], NB), F32)
+    own, turned = [], [[] for _ in range(3)]
+    turns = [jnp.transpose(rotate[k]) for k in range(3)]
     for f in range(4):
-        spot = place(FA, f * FR, lift.shape[2])
-        part = exact(lift[f], spot)
-        own = part if own is None else own + part
+        flipped = lift[:, f, :]
+        own += [flipped, gap]
         for k in range(3):
-            part = exact(exact(lift[f], rotate[k]), spot)
-            turned[k] = part if turned[k] is None else turned[k] + part
-    l2_out[...] = two_rows(own, 64)
+            turned[k] += [exact(turns[k], flipped), gap]
+    l2_out[...] = two_rows(jnp.transpose(jnp.concatenate(own, axis=0)), 64)
     for k in range(3):
-        lr2_out[k] = two_rows(turned[k], 64)
-    for q in range(NQ):
-        full[q] = pieces[0, q] + pieces[1, q] + pieces[2, q] + pieces[3, q]
+        lr2_out[k] = two_rows(jnp.transpose(jnp.concatenate(turned[k], axis=0)), 64)
+
+
+def coarse_kernel(series, s_ref, w2, p2, fm_ref, l2, after, u_out, full, t_full):
+    del after
+    for q in range(NQ):
+        full[q] = weigh(series, 1.0, 0.0, q)
     traces(full, p2[...], t_full)
-
     rows = operator(full, s_ref, w2[...])
     for q in range(NQ):
-        u_out[q] = x_ref[q] + rows[q] - own_term(fm_ref, t_full, l2_out[...], q)
-
-
-def local_kernel(q_ref, pred, t_ref, s_ref, w2, fm_ref, l2, nb_ref, nf_ref, u_out, n_out):
+        u_out[q] = series[0, q] + rows[q] - own_term(fm_ref, t_full, l2[...], q)
+
+
+def local_kernel(sub, q_ref, pred, t_ref, s_ref, w2, fm_ref, l2, nb_ref, nf_ref, series, u_out,
+                 n_out, *next_out):
     rows = operator(pred, s_ref, w2[...])
     for q in range(NQ):
         u_out[q] = q_ref[q] + rows[q] - own_term(fm_ref, t_ref, l2[...], q)
     local_pick(t_ref, nb_ref, nf_ref, n_out)
+    if next_out:
+        for q in range(NQ):
+            next_out[0][q] = weigh(series, (sub + 2) / RATE, (sub + 1) / RATE, q)
 
 
 def join_kernel(last, *refs):
@@ -254,21 +302,19 @@
                 both = dot(w, hi * masks[k])
                 part = both[:NB] + both[64:64 + NB] + dot(w[:64], lo * masks[k])[:NB]
                 sub = part if sub is None else sub + part
-            work[q] = values[q] - sub
+            work[q] = values(q) - sub
 
     ghost_pick(table, nb_ref, nl_ref, n_ref)
-    face_terms(u_ref)
+    if last:
+        for q in range(NQ):
+            n_ref[q] = jnp.where(fine, n_ref[q], nacc_ref[q] + n_ref[q])
+        face_terms(lambda q: jnp.where(fine, u_ref[q], uc_ref[q]))
+        after = plastic(work, coh[...])
+        for q in range(NQ):
+            out[q] = after[q]
+        return
+    face_terms(lambda q: u_ref[q])
     after = plastic(work, coh[...])
-    if last:
-        for q in range(NQ):
-            out[:, q, :] = after[q]
-        for q in range(NQ):
-            n_ref[q] += nacc_ref[q]
-        face_terms(uc_ref)
-        after = plastic(work, coh[...])
-        for q in range(NQ):
-            out[:, q, :] = jnp.where(fine, out[:, q, :], after[q])
-        return
     for q in range(NQ):
         n_out[q] = nacc_ref[q] + n_ref[q] if nacc_ref is not None else n_ref[q]
         x = jnp.where(fine, after[q], q_ref[q])
@@ -286,7 +332,7 @@
 
     lax.fori_loop(0, ORDER - 1, step, jnp.float32(1.0 / RATE))
     for q in range(NQ):
-        pred[q] = jnp.where(fine, pred[q], piece[0, q])
+        pred[q] = jnp.where(fine, pred[q], piece[q])
     traces(pred, p2[...], t_out)
     send(t_out, se, sf, (m0, m1, m2, m3))
 
@@ -296,16 +342,16 @@
 MSG = (PK, LN)
 
 
-def call(kernel, name, outs, scratch, args, flops=50_000_000):
+def call(kernel, name, outs, scratch, args, size=4, space=pltpu.VMEM, limit=24):
     return pl.pallas_call(
         kernel,
         name=name,
         out_shape=[jax.ShapeDtypeStruct(s, d) for s, d in outs],
-        in_specs=[pl.BlockSpec(memory_space=pltpu.VMEM)] * len(args),
+        in_specs=[pl.BlockSpec(memory_space=space)] * len(args),
         out_specs=[pl.BlockSpec(memory_space=pltpu.VMEM)] * len(outs),
-        scratch_shapes=[pltpu.VMEM(s, d) for s, d in scratch],
-        compiler_params=pltpu.CompilerParams(vmem_limit_bytes=24 << 20),
-        cost_estimate=pl.CostEstimate(flops=flops, bytes_accessed=4 << 20, transcendentals=0),
+        scratch_shapes=[pltpu.VMEM(*x) if isinstance(x, tuple) else x for x in scratch],
+        compiler_params=pltpu.CompilerParams(vmem_limit_bytes=limit << 20),
+        cost_estimate=pl.CostEstimate(flops=50_000_000, bytes_accessed=size << 20, transcendentals=0),
     )(*args)
 
 
@@ -330,31 +376,7 @@
 def shards(dofs, star, flux_minus, flux_plus, cohesion, stiff, face_proj, lift, rotate, cluster,
            neighbor, neigh_face, orient, send_elem, send_face):
     devices = lax.axis_size("dom")
-    me = lax.axis_index("dom")
     pairings = partners(devices)
-    one_up = me % 2 == 0
-    two_up = me % 4 < 2
-    slots = send_elem.shape[1]
-
-    def reorder(table):
-        b0, b1, b2, b3 = table[0], table[1], table[2], table[3]
-        return jnp.concatenate([
-            jnp.where(one_up, b2, b1), jnp.where(one_up, b1, b2),
-            jnp.where(two_up, b3, b0), jnp.where(two_up, b0, b3)]).reshape(1, 4 * slots)
-
-    se, sf = reorder(send_elem), reorder(send_face)
-    ghost = neighbor - LN
-    block, slot = ghost // slots, ghost % slots
-    one = (block == 1) | (block == 2)
-    place_of = jnp.where(
-        one,
-        jnp.where((block == 2) == one_up, 0, 1),
-        jnp.where((block == 3) == two_up, 2, 3))
-    nb = jnp.where((ghost >= 0) & (ghost < 4 * slots), LN + place_of * slots + slot, neighbor)
-    fm = flux_minus.reshape(4 * NQ, NQ, LN)
-    fp = flux_plus.reshape(4 * NQ, NQ, LN)
-    coh = cohesion.reshape(1, LN)
-    fine = cluster.reshape(1, LN)
 
     def exchange(messages):
         got = [None] * 4
@@ -362,34 +384,49 @@
             got[k] = lax.ppermute(messages[k], "dom", pairings[k])
         return got
 
+    i32 = jnp.int32
+    args = [
+        jnp.transpose(dofs, (1, 0, 2)), jnp.transpose(star, (1, 2, 0, 3)),
+        jnp.transpose(flux_minus, (1, 2, 0, 3)), jnp.transpose(flux_plus, (1, 2, 0, 3)),
+        cohesion.reshape(1, LN), stiff, jnp.transpose(face_proj, (1, 0, 2)),
+        jnp.transpose(lift, (2, 0, 1)), rotate, cluster.reshape(1, LN), neighbor, neigh_face,
+        orient, send_elem, send_face]
+    scratch = [pltpu.VMEM(args[n].shape, args[n].dtype) for n in (1, 5, 6, 13, 14, 10)]
     outs = call(
         first_kernel, "first",
-        [((27, NQ, LN), F32), ((128, 3 * NB), BF16), ((2 * FA, NB), BF16), (BIG, F32),
-         ((RATE,) + BIG, F32), (TAB, F32)] + [(MSG, F32)] * 4,
-        [(BIG, F32)],
-        [dofs, star, stiff, face_proj, se, sf])
-    s_mat, w2, p2, state, pieces, table = outs[:6]
-    got = exchange(outs[6:])
-    l2, lr2, coarse = call(
-        lift_kernel, "coarse_own",
-        [((128, FA), BF16), ((3, 128, FA), BF16), (BIG, F32)],
-        [(BIG, F32), (TAB, F32)],
-        [state, s_mat, w2, p2, pieces, fm, lift, rotate])
-    total = None
-    pred = pieces[0]
+        [((NQ, NQ, 3, LN), F32), ((128, 3 * NB), BF16), ((2 * FA, NB), BF16),
+         ((ORDER,) + BIG, F32), (BIG, F32), (TAB, F32)] + [(MSG, F32)] * 4
+        + [((1, LN), i32), ((1, LN), i32), ((4, LN), i32), (args[2].shape, F32),
+           (args[3].shape, F32), ((4, LN), i32), ((4, LN), i32), ((1, LN), F32), ((1, LN), i32),
+           (args[7].shape, F32), (args[8].shape, F32)],
+        scratch + [pltpu.SemaphoreType.DMA((15,))],
+        [pltpu.with_memory_space_constraint(a, pltpu.HBM) for a in args], space=pltpu.HBM)
+    s_mat, w2, p2, series, pred, table = outs[:6]
+    got = exchange(outs[6:10])
+    se, sf, nb, fm, fp, nf, turn_code, coh, fine, lift, rotate = outs[10:]
+    l2, lr2 = call(
+        lift_kernel, "lifts", [((128, FA), BF16), ((3, 128, FA), BF16)], [],
+        [lift, rotate])
+    total = coarse = None
+    state = series[0]
     for sub in range(RATE):
-        u, near = call(
-            local_kernel, "local", [(BIG, F32), (TAB, F32)], [],
-            [state, pred, table, s_mat, w2, fm, l2, nb, neigh_face])
         last = sub == RATE - 1
-        common = [*got, state, u, near, total if total is not None else near, fp, lr2, nb, orient,
+        u, near, *piece = call(
+            functools.partial(local_kernel, sub), "local",
+            [(BIG, F32), (TAB, F32)] + ([] if last else [(BIG, F32)]), [],
+            [state, pred, table, s_mat, w2, fm, l2, nb, nf, series])
+        if sub == 1:
+            coarse = call(
+                coarse_kernel, "coarse_own", [(BIG, F32)], [(BIG, F32), (TAB, F32)],
+                [series, s_mat, w2, p2, fm, l2, outs[4]], 8)[0]
+        common = [*got, state, u, near, total if total is not None else near, fp, lr2, nb, turn_code,
                   coh, fine, s_mat, w2, p2]
         if last:
-            return call(
-                functools.partial(join_kernel, True), "last",
-                [((NB, NQ, LN), F32)],
+            out = call(
+                functools.partial(join_kernel, True), "last", [(BIG, F32)],
                 [(TAB, F32), (BIG, F32)],
-                common + [pieces[3:4], se, sf, coarse])[0]
+                common + [near, se, sf, coarse])[0]
+            return jnp.transpose(out, (1, 0, 2))
         first = total is None
 
         def kernel(*refs, first=first):
@@ -402,7 +439,7 @@
             kernel, "join",
             [(BIG, F32), (TAB, F32), (BIG, F32), (TAB, F32)] + [(MSG, F32)] * 4,
             [(TAB, F32), (BIG, F32), (BIG, F32)],
-            common + [pieces[sub + 1:sub + 2], se, sf])
+            common + [piece[0], se, sf])
         state, total, pred, table = outs[:4]
         got = exchange(outs[4:])
 

time: 80.1 us -> 72.1 us (0.900)
  local copies, waits for them, and re-layouts: 7.22 us -> 0.02 us
  waiting for transfers between devices: 19.4 us -> 22.9 us
  starting transfers between devices: 20.7 us -> 17.8 us
  Pallas kernels: 32.1 us -> 31.1 us
    unnamed x32 -> x0, local copies, waits for them, and re-layouts: 6.37 us -> none
    ppermute x16, waiting for transfers between devices: 19.4 us -> 22.9 us  [exchange(): got[k] = lax.ppermute(messages[k], 'dom', pairings[k])]
    ppermute x16, starting transfers between devices: 20.7 us -> 17.8 us  [exchange(): got[k] = lax.ppermute(messages[k], 'dom', pairings[k])]
    pallas_call x10 -> x11, Pallas kernels: 32.1 us -> 31.1 us  [call(): pl.pallas_call(kernel, name=name, out_shape=[jax.ShapeDtypeStruct(s, d) f...]
  transfers between devices with their start and end apart: 16 -> 16, of which waited for: 7 -> 8; matrix products, arithmetic and copies ran while one was open for 2% -> 0% of each run, Pallas kernels for 11% -> 10%
where the time goes in v2:
time: 72.1 us; the launch traced here: 72 us
  Pallas kernels  31.1 us (43%)
  waiting for transfers between devices  22.9 us (32%)
  starting transfers between devices  17.8 us (25%)
    pallas_call x11, Pallas kernels, call(): pl.pallas_call(kernel, name=name, out_shape=[jax.ShapeDtypeStruct(s, d) f...  31.1 us
    ppermute x16, waiting for transfers between devices, exchange(): got[k] = lax.ppermute(messages[k], 'dom', pairings[k])  22.9 us
    ppermute x16, starting transfers between devices, exchange(): got[k] = lax.ppermute(messages[k], 'dom', pairings[k])  17.8 us
  transfers between devices with their start and end apart: 16, of which 8 were waited for; matrix products, arithmetic and copies ran while one was open for 0% of the time, Pallas kernels for 10%

profile of v2, /device:TPU:24, one launch (start us, length us, event | category | flops | bytes accessed | tf_op | source)
XLA Modules:
  0.0 72.0 jit_solution(3291542203301532099)
XLA Ops:
  0.0 5.8 %first.1 = (f32[9,9,3,128]{3,2,1,0:T(4,128)S(1)}, bf16[128,168]{1,0:T(8,128)(2,1)S(1)}, bf16[192,56]{1,0:T(8,128)(2,1)S(1)}, f32[6,9,56,128]{3,2,1,0:T(8,128)S(1...) custom-call(f32[9,56,128]{2,1,0:T(8,128)} %bitcast.11, ...), custom_call_target="tpu_custom_call" | custom-call | flops 50000000 | bytes 4194304 | tf_op jit(solution)/shard_map/first/pallas_call | solution.py:346
  5.8 0.1 collective-permute-start
  5.9 8.3 %collective-permute-start.1 = (f32[56,128]{1,0:T(8,128)S(1)}, f32[56,128]{1,0:T(8,128)S(1)}, u32[]{:S(2)}, u32[]{:S(2)}) collective-permute-start(f32[56,128]{1,0:T(8,128)S(1)} %get-tuple-element.64), channel_id=1, source_target_pairs={{0,255},{1,2},{2,1},{3,4},{4,3},{5,6},{6,5},{7,8},{8,7},{9,10},{10... | collective-permute-start | bytes 86024 | tf_op jit(solution)/shard_map/ppermute | solution.py:384
  14.3 0.0 collective-permute-start.2
  14.3 1.4 %collective-permute-start.3 = (f32[56,128]{1,0:T(8,128)S(1)}, f32[56,128]{1,0:T(8,128)S(1)}, u32[]{:S(2)}, u32[]{:S(2)}) collective-permute-start(f32[56,128]{1,0:T(8,128)S(1)} %get-tuple-element.66), channel_id=1, source_target_pairs={{0,1},{1,0},{2,4},{3,5},{4,2},{5,3},{6,8},{7,9},{8,6},{9,7},{10,12... | collective-permute-start | bytes 86024 | tf_op jit(solution)/shard_map/ppermute | solution.py:384
  15.7 0.5 lifts.1
  16.2 1.4 %local.4 = (f32[9,56,128]{2,1,0:T(8,128)S(1)}, f32[9,96,128]{2,1,0:T(8,128)S(1)}, f32[9,56,128]{2,1,0:T(8,128)S(1)}) custom-call(f32[9,56,128]{2,1,0:T(8,128)S(1)} %slice_bitcast_fusion.q_ref.refs_4_, f32[9,56,128]{2,1,0:T(8,128)S(1)} %get-tuple-element.68.pred, f32[9,96,128]{2,1,0:T(8,128)S(1)} %get-tuple-element.69.t_ref, ...), custom_call_target="tpu_custom_call" | custom-call | flops 50000000 | bytes 4194304 | tf_op jit(solution)/shard_map/local/pallas_call | solution.py:346
  17.7 0.0 collective-permute-done.refs_0_
  17.7 0.0 collective-permute-done.1.refs_1_
  17.7 0.5 collective-permute-done.2.refs_2_
  18.1 4.2 %collective-permute-done.3.refs_3_ = f32[56,128]{1,0:T(8,128)S(1)} collective-permute-done((f32[56,128]{1,0:T(8,128)S(1)}, f32[56,128]{1,0:T(8,128)S(1)}, u32[]{:S(2)}, u32[]{:S(2)}) %collective-permute-start.3) | collective-permute-done | bytes 28704 | tf_op jit(solution)/shard_map/ppermute | solution.py:384
  22.4 5.4 %join.3 = (f32[9,56,128]{2,1,0:T(8,128)S(1)}, f32[9,96,128]{2,1,0:T(8,128)S(1)}, f32[9,56,128]{2,1,0:T(8,128)S(1)}, f32[9,96,128]{2,1,0:T(8,128)S(1)}, f32[56,12...) custom-call(f32[56,128]{1,0:T(8,128)S(1)} %collective-permute-done.refs_0_, ...), custom_call_target="tpu_custom_call" | custom-call | flops 50000000 | bytes 4194304 | tf_op jit(solution)/shard_map/join/pallas_call | solution.py:346
  27.7 0.1 collective-permute-start.4
  27.8 1.5 %collective-permute-start.5 = (f32[56,128]{1,0:T(8,128)S(1)}, f32[56,128]{1,0:T(8,128)S(1)}, u32[]{:S(2)}, u32[]{:S(2)}) collective-permute-start(f32[56,128]{1,0:T(8,128)S(1)} %get-tuple-element.90), channel_id=1, source_target_pairs={{0,255},{1,2},{2,1},{3,4},{4,3},{5,6},{6,5},{7,8},{8,7},{9,10},{10... | collective-permute-start | bytes 86024 | tf_op jit(solution)/shard_map/ppermute | solution.py:384
  29.3 0.6 collective-permute-start.6
  30.0 0.0 collective-permute-start.7
  30.0 1.4 %local.5 = (f32[9,56,128]{2,1,0:T(8,128)S(1)}, f32[9,96,128]{2,1,0:T(8,128)S(1)}, f32[9,56,128]{2,1,0:T(8,128)S(1)}) custom-call(f32[9,56,128]{2,1,0:T(8,128)S(1)} %get-tuple-element.93.q_ref.refs_4_, f32[9,56,128]{2,1,0:T(8,128)S(1)} %get-tuple-element.94.pred, f32[9,96,128]{2,1,0:T(8,128)S(1)} %get-tuple-element.95.t_ref, ...), custom_call_target="tpu_custom_call" | custom-call | flops 50000000 | bytes 4194304 | tf_op jit(solution)/shard_map/local/pallas_call | solution.py:346
  31.4 0.0 collective-permute-done.4.refs_0_
  31.4 4.1 %collective-permute-done.5.refs_1_ = f32[56,128]{1,0:T(8,128)S(1)} collective-permute-done((f32[56,128]{1,0:T(8,128)S(1)}, f32[56,128]{1,0:T(8,128)S(1)}, u32[]{:S(2)}, u32[]{:S(2)}) %collective-permute-start.5) | collective-permute-done | bytes 28704 | tf_op jit(solution)/shard_map/ppermute | solution.py:384
  35.4 0.0 collective-permute-done.6.refs_2_
  35.4 2.6 %collective-permute-done.7.refs_3_ = f32[56,128]{1,0:T(8,128)S(1)} collective-permute-done((f32[56,128]{1,0:T(8,128)S(1)}, f32[56,128]{1,0:T(8,128)S(1)}, u32[]{:S(2)}, u32[]{:S(2)}) %collective-permute-start.7) | collective-permute-done | bytes 28704 | tf_op jit(solution)/shard_map/ppermute | solution.py:384
  38.1 5.4 %join.4 = (f32[9,56,128]{2,1,0:T(8,128)S(1)}, f32[9,96,128]{2,1,0:T(8,128)S(1)}, f32[9,56,128]{2,1,0:T(8,128)S(1)}, f32[9,96,128]{2,1,0:T(8,128)S(1)}, f32[56,12...) custom-call(f32[56,128]{1,0:T(8,128)S(1)} %collective-permute-done.4.refs_0_, ...), custom_call_target="tpu_custom_call" | custom-call | flops 50000000 | bytes 4194304 | tf_op jit(solution)/shard_map/join/pallas_call | solution.py:346
  43.5 0.1 collective-permute-start.8
  43.6 2.9 %collective-permute-start.9 = (f32[56,128]{1,0:T(8,128)S(1)}, f32[56,128]{1,0:T(8,128)S(1)}, u32[]{:S(2)}, u32[]{:S(2)}) collective-permute-start(f32[56,128]{1,0:T(8,128)S(1)} %get-tuple-element.101), channel_id=1, source_target_pairs={{0,255},{1,2},{2,1},{3,4},{4,3},{5,6},{6,5},{7,8},{8,7},{9,10},{10... | collective-permute-start | bytes 86024 | tf_op jit(solution)/shard_map/ppermute | solution.py:384
  46.4 0.0 collective-permute-start.10
  46.5 0.3 collective-permute-start.11
  46.8 1.4 %local.6 = (f32[9,56,128]{2,1,0:T(8,128)S(1)}, f32[9,96,128]{2,1,0:T(8,128)S(1)}, f32[9,56,128]{2,1,0:T(8,128)S(1)}) custom-call(f32[9,56,128]{2,1,0:T(8,128)S(1)} %get-tuple-element.104.q_ref.refs_4_, f32[9,56,128]{2,1,0:T(8,128)S(1)} %get-tuple-element.105.pred, f32[9,96,128]{2,1,0:T(8,128)S(1)} %get-tuple-element.106.t_ref, ...), custom_call_target="tpu_custom_call" | custom-call | flops 50000000 | bytes 4194304 | tf_op jit(solution)/shard_map/local/pallas_call | solution.py:346
  48.2 0.0 collective-permute-done.8.refs_0_
  48.2 3.0 %collective-permute-done.9.refs_1_ = f32[56,128]{1,0:T(8,128)S(1)} collective-permute-done((f32[56,128]{1,0:T(8,128)S(1)}, f32[56,128]{1,0:T(8,128)S(1)}, u32[]{:S(2)}, u32[]{:S(2)}) %collective-permute-start.9) | collective-permute-done | bytes 28704 | tf_op jit(solution)/shard_map/ppermute | solution.py:384
  51.2 0.0 collective-permute-done.10.refs_2_
  51.2 3.4 %collective-permute-done.11.refs_3_ = f32[56,128]{1,0:T(8,128)S(1)} collective-permute-done((f32[56,128]{1,0:T(8,128)S(1)}, f32[56,128]{1,0:T(8,128)S(1)}, u32[]{:S(2)}, u32[]{:S(2)}) %collective-permute-start.11) | collective-permute-done | bytes 28704 | tf_op jit(solution)/shard_map/ppermute | solution.py:384
  54.5 5.4 %join.5 = (f32[9,56,128]{2,1,0:T(8,128)S(1)}, f32[9,96,128]{2,1,0:T(8,128)S(1)}, f32[9,56,128]{2,1,0:T(8,128)S(1)}, f32[9,96,128]{2,1,0:T(8,128)S(1)}, f32[56,12...) custom-call(f32[56,128]{1,0:T(8,128)S(1)} %collective-permute-done.8.refs_0_, ...), custom_call_target="tpu_custom_call" | custom-call | flops 50000000 | bytes 4194304 | tf_op jit(solution)/shard_map/join/pallas_call | solution.py:346
  59.9 0.1 collective-permute-start.12
  60.0 2.1 %collective-permute-start.13 = (f32[56,128]{1,0:T(8,128)S(1)}, f32[56,128]{1,0:T(8,128)S(1)}, u32[]{:S(2)}, u32[]{:S(2)}) collective-permute-start(f32[56,128]{1,0:T(8,128)S(1)} %get-tuple-element.112), channel_id=1, source_target_pairs={{0,255},{1,2},{2,1},{3,4},{4,3},{5,6},{6,5},{7,8},{8,7},{9,10},{10... | collective-permute-start | bytes 86024 | tf_op jit(solution)/shard_map/ppermute | solution.py:384
  62.1 0.0 collective-permute-start.14
  62.1 0.3 collective-permute-start.15
  62.4 1.3 %coarse_own.1.refs_20_ = f32[9,56,128]{2,1,0:T(8,128)S(1)} custom-call(f32[6,9,56,128]{3,2,1,0:T(8,128)S(1)} %get-tuple-element.67.series, f32[9,9,3,128]{3,2,1,0:T(4,128)S(1)} %get-tuple-element.70.s_ref.refs_14_, bf16[128,168]{1,0:T(8,128)(2,1)S(1)} %get-tuple-element.71.w2.refs_15_, bf16[192,56]{1,0:T(8,128)(2,1)S(1)} %get-tuple-element.85.refs_16_.p2, ...), custom_call_target="tpu_custom_call" | custom-call | flops 50000000 | bytes 8388608 | tf_op jit(solution)/shard_map/coarse_own/pallas_call | solution.py:346
  63.7 1.3 %local.7 = (f32[9,56,128]{2,1,0:T(8,128)S(1)}, f32[9,96,128]{2,1,0:T(8,128)S(1)}) custom-call(f32[9,56,128]{2,1,0:T(8,128)S(1)} %get-tuple-element.115.q_ref.refs_4_, f32[9,56,128]{2,1,0:T(8,128)S(1)} %get-tuple-element.116.pred, f32[9,96,128]{2,1,0:T(8,128)S(1)} %get-tuple-element.117.t_ref, f32[9,9,3,128]{3,2,1,0:T(4,128)S(1)} %get-tuple-element.70.s_ref.refs_14_, ...), custom_call_target="tpu_custom_call" | custom-call | flops 50000000 | bytes 4194304 | tf_op jit(solution)/shard_map/local/pallas_call | solution.py:346
  65.0 0.0 collective-permute-done.12.refs_0_
  65.0 2.6 %collective-permute-done.13.refs_1_ = f32[56,128]{1,0:T(8,128)S(1)} collective-permute-done((f32[56,128]{1,0:T(8,128)S(1)}, f32[56,128]{1,0:T(8,128)S(1)}, u32[]{:S(2)}, u32[]{:S(2)}) %collective-permute-start.13) | collective-permute-done | bytes 28704 | tf_op jit(solution)/shard_map/ppermute | solution.py:384
  67.6 0.0 collective-permute-done.14.refs_2_
  67.6 2.6 %collective-permute-done.15.refs_3_ = f32[56,128]{1,0:T(8,128)S(1)} collective-permute-done((f32[56,128]{1,0:T(8,128)S(1)}, f32[56,128]{1,0:T(8,128)S(1)}, u32[]{:S(2)}, u32[]{:S(2)}) %collective-permute-start.15) | collective-permute-done | bytes 28704 | tf_op jit(solution)/shard_map/ppermute | solution.py:384
  70.2 1.8 %last.1 = f32[9,56,128]{2,1,0:T(8,128)} custom-call(f32[56,128]{1,0:T(8,128)S(1)} %collective-permute-done.12.refs_0_, f32[56,128]{1,0:T(8,128)S(1)} %collective-permute-done.13.refs_1_, f32[56,128]{1,0:T(8,128)S(1)} %collective-permute-done.14.refs_2_, f32[56,128]{1,0:T(8,128)S(1)} %collective-permute-done.15.refs_3_, ...), custom_call_target="tpu_custom_call" | custom-call | flops 50000000 | bytes 4194304 | tf_op jit(solution)/shard_map/last/pallas_call | solution.py:346
  (1 shorter events, 0.0 us)
Async XLA Ops:
  5.8 11.8 %collective-permute-start = (f32[56,128]{1,0:T(8,128)S(1)}, f32[56,128]{1,0:T(8,128)S(1)}, u32[]{:S(2)}, u32[]{:S(2)}) collective-permute-start(f32[56,128]{1,0:T(8,128)S(1)} %get-tuple-element.63), channel_id=1, source_target_pairs={{0,1},{1,0},{2,3},{3,2},{4,5},{5,4},{6,7},{7,6},{8,9},{9,8},{10,11... | collective-permute-start | bytes 86024 | tf_op jit(solution)/shard_map/ppermute | solution.py:384
  5.9 11.7 %collective-permute-start.1 = (f32[56,128]{1,0:T(8,128)S(1)}, f32[56,128]{1,0:T(8,128)S(1)}, u32[]{:S(2)}, u32[]{:S(2)}) collective-permute-start(f32[56,128]{1,0:T(8,128)S(1)} %get-tuple-element.64), channel_id=1, source_target_pairs={{0,255},{1,2},{2,1},{3,4},{4,3},{5,6},{6,5},{7,8},{8,7},{9,10},{10... | collective-permute-start | bytes 86024 | tf_op jit(solution)/shard_map/ppermute | solution.py:384
  14.3 3.9 %collective-permute-start.2 = (f32[56,128]{1,0:T(8,128)S(1)}, f32[56,128]{1,0:T(8,128)S(1)}, u32[]{:S(2)}, u32[]{:S(2)}) collective-permute-start(f32[56,128]{1,0:T(8,128)S(1)} %get-tuple-element.65), channel_id=1, source_target_pairs={{0,2},{1,3},{2,0},{3,1},{4,6},{5,7},{6,4},{7,5},{8,10},{9,11},{10,... | collective-permute-start | bytes 86024 | tf_op jit(solution)/shard_map/ppermute | solution.py:384
  14.3 8.1 %collective-permute-start.3 = (f32[56,128]{1,0:T(8,128)S(1)}, f32[56,128]{1,0:T(8,128)S(1)}, u32[]{:S(2)}, u32[]{:S(2)}) collective-permute-start(f32[56,128]{1,0:T(8,128)S(1)} %get-tuple-element.66), channel_id=1, source_target_pairs={{0,1},{1,0},{2,4},{3,5},{4,2},{5,3},{6,8},{7,9},{8,6},{9,7},{10,12... | collective-permute-start | bytes 86024 | tf_op jit(solution)/shard_map/ppermute | solution.py:384
  27.7 3.6 %collective-permute-start.4 = (f32[56,128]{1,0:T(8,128)S(1)}, f32[56,128]{1,0:T(8,128)S(1)}, u32[]{:S(2)}, u32[]{:S(2)}) collective-permute-start(f32[56,128]{1,0:T(8,128)S(1)} %get-tuple-element.89.after), channel_id=1, source_target_pairs={{0,1},{1,0},{2,3},{3,2},{4,5},{5,4},{6,7},{7,6},{8,9},{9,8},{10,11... | collective-permute-start | bytes 86024 | tf_op jit(solution)/shard_map/ppermute | solution.py:384
  27.8 7.6 %collective-permute-start.5 = (f32[56,128]{1,0:T(8,128)S(1)}, f32[56,128]{1,0:T(8,128)S(1)}, u32[]{:S(2)}, u32[]{:S(2)}) collective-permute-start(f32[56,128]{1,0:T(8,128)S(1)} %get-tuple-element.90), channel_id=1, source_target_pairs={{0,255},{1,2},{2,1},{3,4},{4,3},{5,6},{6,5},{7,8},{8,7},{9,10},{10... | collective-permute-start | bytes 86024 | tf_op jit(solution)/shard_map/ppermute | solution.py:384
  29.3 6.1 %collective-permute-start.6 = (f32[56,128]{1,0:T(8,128)S(1)}, f32[56,128]{1,0:T(8,128)S(1)}, u32[]{:S(2)}, u32[]{:S(2)}) collective-permute-start(f32[56,128]{1,0:T(8,128)S(1)} %get-tuple-element.91), channel_id=1, source_target_pairs={{0,2},{1,3},{2,0},{3,1},{4,6},{5,7},{6,4},{7,5},{8,10},{9,11},{10,... | collective-permute-start | bytes 86024 | tf_op jit(solution)/shard_map/ppermute | solution.py:384
  30.0 8.1 %collective-permute-start.7 = (f32[56,128]{1,0:T(8,128)S(1)}, f32[56,128]{1,0:T(8,128)S(1)}, u32[]{:S(2)}, u32[]{:S(2)}) collective-permute-start(f32[56,128]{1,0:T(8,128)S(1)} %get-tuple-element.92), channel_id=1, source_target_pairs={{0,1},{1,0},{2,4},{3,5},{4,2},{5,3},{6,8},{7,9},{8,6},{9,7},{10,12... | collective-permute-start | bytes 86024 | tf_op jit(solution)/shard_map/ppermute | solution.py:384
  43.5 4.7 %collective-permute-start.8 = (f32[56,128]{1,0:T(8,128)S(1)}, f32[56,128]{1,0:T(8,128)S(1)}, u32[]{:S(2)}, u32[]{:S(2)}) collective-permute-start(f32[56,128]{1,0:T(8,128)S(1)} %get-tuple-element.100), channel_id=1, source_target_pairs={{0,1},{1,0},{2,3},{3,2},{4,5},{5,4},{6,7},{7,6},{8,9},{9,8},{10,11... | collective-permute-start | bytes 86024 | tf_op jit(solution)/shard_map/ppermute | solution.py:384
  43.6 7.6 %collective-permute-start.9 = (f32[56,128]{1,0:T(8,128)S(1)}, f32[56,128]{1,0:T(8,128)S(1)}, u32[]{:S(2)}, u32[]{:S(2)}) collective-permute-start(f32[56,128]{1,0:T(8,128)S(1)} %get-tuple-element.101), channel_id=1, source_target_pairs={{0,255},{1,2},{2,1},{3,4},{4,3},{5,6},{6,5},{7,8},{8,7},{9,10},{10... | collective-permute-start | bytes 86024 | tf_op jit(solution)/shard_map/ppermute | solution.py:384
  46.4 4.7 %collective-permute-start.10 = (f32[56,128]{1,0:T(8,128)S(1)}, f32[56,128]{1,0:T(8,128)S(1)}, u32[]{:S(2)}, u32[]{:S(2)}) collective-permute-start(f32[56,128]{1,0:T(8,128)S(1)} %get-tuple-element.102), channel_id=1, source_target_pairs={{0,2},{1,3},{2,0},{3,1},{4,6},{5,7},{6,4},{7,5},{8,10},{9,11},{10,... | collective-permute-start | bytes 86024 | tf_op jit(solution)/shard_map/ppermute | solution.py:384
  46.5 8.1 %collective-permute-start.11 = (f32[56,128]{1,0:T(8,128)S(1)}, f32[56,128]{1,0:T(8,128)S(1)}, u32[]{:S(2)}, u32[]{:S(2)}) collective-permute-start(f32[56,128]{1,0:T(8,128)S(1)} %get-tuple-element.103), channel_id=1, source_target_pairs={{0,1},{1,0},{2,4},{3,5},{4,2},{5,3},{6,8},{7,9},{8,6},{9,7},{10,12... | collective-permute-start | bytes 86024 | tf_op jit(solution)/shard_map/ppermute | solution.py:384
  59.9 5.1 %collective-permute-start.12 = (f32[56,128]{1,0:T(8,128)S(1)}, f32[56,128]{1,0:T(8,128)S(1)}, u32[]{:S(2)}, u32[]{:S(2)}) collective-permute-start(f32[56,128]{1,0:T(8,128)S(1)} %get-tuple-element.111), channel_id=1, source_target_pairs={{0,1},{1,0},{2,3},{3,2},{4,5},{5,4},{6,7},{7,6},{8,9},{9,8},{10,11... | collective-permute-start | bytes 86024 | tf_op jit(solution)/shard_map/ppermute | solution.py:384
  60.0 7.6 %collective-permute-start.13 = (f32[56,128]{1,0:T(8,128)S(1)}, f32[56,128]{1,0:T(8,128)S(1)}, u32[]{:S(2)}, u32[]{:S(2)}) collective-permute-start(f32[56,128]{1,0:T(8,128)S(1)} %get-tuple-element.112), channel_id=1, source_target_pairs={{0,255},{1,2},{2,1},{3,4},{4,3},{5,6},{6,5},{7,8},{8,7},{9,10},{10... | collective-permute-start | bytes 86024 | tf_op jit(solution)/shard_map/ppermute | solution.py:384
  62.1 5.5 %collective-permute-start.14 = (f32[56,128]{1,0:T(8,128)S(1)}, f32[56,128]{1,0:T(8,128)S(1)}, u32[]{:S(2)}, u32[]{:S(2)}) collective-permute-start(f32[56,128]{1,0:T(8,128)S(1)} %get-tuple-element.113), channel_id=1, source_target_pairs={{0,2},{1,3},{2,0},{3,1},{4,6},{5,7},{6,4},{7,5},{8,10},{9,11},{10,... | collective-permute-start | bytes 86024 | tf_op jit(solution)/shard_map/ppermute | solution.py:384
  62.1 8.1 %collective-permute-start.15 = (f32[56,128]{1,0:T(8,128)S(1)}, f32[56,128]{1,0:T(8,128)S(1)}, u32[]{:S(2)}, u32[]{:S(2)}) collective-permute-start(f32[56,128]{1,0:T(8,128)S(1)} %get-tuple-element.114), channel_id=1, source_target_pairs={{0,1},{1,0},{2,4},{3,5},{4,2},{5,3},{6,8},{7,9},{8,6},{9,7},{10,12... | collective-permute-start | bytes 86024 | tf_op jit(solution)/shard_map/ppermute | solution.py:384

commit v3 on v2

--- a/solution.py
+++ b/solution.py
@@ -18,6 +18,7 @@
 FA = 4 * FR
 LN = 128
 PK = 56
+PAIRS = 5
 
 
 def dot(a, b):
@@ -33,17 +34,24 @@
     return hi, (x - hi.astype(F32)).astype(BF16)
 
 
-def two_rows(w, pad):
-    if w.shape[0] < pad:
-        w = jnp.concatenate([w, jnp.zeros((pad - w.shape[0], w.shape[1]), F32)], axis=0)
-    return jnp.concatenate(split(w), axis=0)
+def two_rows(w):
+    hi, lo = split(w)
+    return jnp.concatenate([hi.astype(F32), lo.astype(F32)], axis=0).astype(BF16)
 
 
 def times(w2, rhs, rows):
-    half = w2.shape[0] // 2
     hi, lo = split(rhs)
     both = dot(w2, hi)
-    return both[:rows] + both[half:half + rows] + dot(w2[:half], lo)[:rows]
+    return both[:rows] + both[rows:] + dot(w2[:rows], lo)
+
+
+def side_by_side(w2, halves):
+    out = dot(w2, halves)
+    return out[:NB, :LN] + out[NB:, :LN] + out[:NB, LN:]
+
+
+def lift_times(w2, rhs):
+    return side_by_side(w2, jnp.concatenate(split(rhs), axis=1))
 
 
 def star_rows(s_ref, q, which, values):
@@ -58,8 +66,26 @@
     for q in range(NQ):
         stacked = jnp.concatenate(
             [star_rows(s_ref, q, c, lambda p: x_ref[p]) for c in range(3)], axis=0)
-        out.append(times(w2, stacked, NB))
+        out.append(lift_times(w2, stacked))
     return out
+
+
+def packed_operator(y_ref, s_ref, w2):
+    out = []
+    for j in range(PAIRS):
+        parts = []
+        for c in range(3):
+            total = s_ref[j, 0, c:c + 1, :] * y_ref[0]
+            for m in range(1, 2 * PAIRS):
+                total = total + s_ref[j, m, c:c + 1, :] * y_ref[m]
+            parts.append(total)
+        out.append(lift_times(w2, jnp.concatenate(parts, axis=0)))
+    return out
+
+
+def both_ways(y_ref, j, rows):
+    y_ref[2 * j] = rows
+    y_ref[2 * j + 1] = pltpu.roll(rows, LN // 2, 1)
 
 
 def traces(x_ref, p2, t_ref):
@@ -142,13 +168,14 @@
 
 
 def own_term(f_ref, t_ref, l2, q):
-    return times(l2, flux_rows(f_ref, q, t_ref), NB)
+    return lift_times(l2, flux_rows(f_ref, q, t_ref))
 
 
 def orient_masks(or_ref):
     codes = jnp.concatenate(
         [jnp.broadcast_to(or_ref[f:f + 1, :], (FR, LN)) for f in range(4)], axis=0)
-    return [(codes == k).astype(F32).astype(BF16) for k in range(3)]
+    masks = [(codes == k).astype(F32).astype(BF16) for k in range(3)]
+    return [jnp.concatenate([m, m], axis=1) for m in masks]
 
 
 def plastic(u_ref, cohesion):
@@ -203,7 +230,7 @@
         copies[n].start()
     copies[5].wait()
     minus = [0.5 * (jnp.transpose(stiff[c]) - stiff[c]) for c in range(3)]
-    w2_out[...] = two_rows(jnp.concatenate(minus, axis=1), 64)
+    w2_out[...] = two_rows(jnp.concatenate(minus, axis=1))
     copies[1].wait()
     for q in range(NQ):
         for p in range(q + 1):
@@ -214,21 +241,18 @@
     for q in range(NQ):
         piece[q] = series[0, q] * (1.0 / RATE)
 
-    def step(k, weight):
-        weight = weight * (1.0 / RATE / (k.astype(F32) + 2.0))
+    for k in range(ORDER - 1):
+        weight = (1.0 / RATE) ** (k + 2) / math.factorial(k + 2)
         rows = operator(series.at[k], s_out, w2_out[...])
         for q in range(NQ):
             series[k + 1, q] = rows[q]
             piece[q] += weight * rows[q]
-        return weight
-
-    lax.fori_loop(0, ORDER - 1, step, jnp.float32(1.0 / RATE))
     for n in (6, 13, 14):
         copies[n].wait()
     faces = []
     for f in range(4):
         faces += [proj[:, f, :], jnp.zeros((FR - proj.shape[0], NB), F32)]
-    p2_out[...] = two_rows(jnp.concatenate(faces, axis=0), FA)
+    p2_out[...] = two_rows(jnp.concatenate(faces, axis=0))
     me = lax.axis_index("dom")
     one_up = lax.rem(me, 2) == 0
     two_up = lax.rem(me, 4) < 2
@@ -247,7 +271,36 @@
     nb_out[...] = jnp.where((ghost >= 0) & (ghost < LN), LN + place_of * 32 + slot, nb[...])
 
 
-def lift_kernel(lift, rotate, l2_out, lr2_out):
+def lift_kernel(lift, rotate, s_ref, fine_ref, l2_out, lr2_out, order_out, spot_out, pack_out, rows):
+    is_fine = jnp.broadcast_to(fine_ref[...], (LN, LN))
+    down = lax.broadcasted_iota(jnp.int32, (LN, LN), 0)
+    across = lanes((LN, LN))
+    ahead = (down < across).astype(F32).astype(BF16)
+    spot = dot(is_fine.astype(F32).astype(BF16), ahead)
+    own_spot = jnp.transpose(spot).astype(jnp.int32)
+    own_fine = jnp.transpose(is_fine.astype(F32)) > 0.5
+    chosen = own_fine & (own_spot == across % (LN // 2))
+    order = dot(across.astype(F32).astype(BF16), chosen.astype(F32).astype(BF16)).astype(jnp.int32)
+    order_out[...] = order[0:8]
+    low = jnp.minimum(spot.astype(jnp.int32), LN // 2 - 1)
+    spot_out[0] = low[0:8]
+    spot_out[1] = low[0:8] + LN // 2
+    order = order[0:8]
+    for q in range(NQ):
+        for p in range(q + 1):
+            got = pick(jnp.concatenate([s_ref[q, p], jnp.zeros((5, LN), F32)], axis=0), order)
+            rows[q, p] = got
+            rows[p, q] = got
+    left = lanes((3, LN)) < LN // 2
+
+    def entry(q, p):
+        return rows[q, p, 0:3] if q < NQ and p < NQ else jnp.zeros((3, LN), F32)
+
+    for j in range(PAIRS):
+        for i in range(PAIRS):
+            a, b = 2 * j, 2 * i
+            pack_out[j, b] = jnp.where(left, entry(a, b), entry(a + 1, b + 1))
+            pack_out[j, b + 1] = jnp.where(left, entry(a, b + 1), entry(a + 1, b))
     gap = jnp.zeros((FR - lift.shape[0], NB), F32)
     own, turned = [], [[] for _ in range(3)]
     turns = [jnp.transpose(rotate[k]) for k in range(3)]
@@ -256,9 +309,8 @@
         own += [flipped, gap]
         for k in range(3):
             turned[k] += [exact(turns[k], flipped), gap]
-    l2_out[...] = two_rows(jnp.transpose(jnp.concatenate(own, axis=0)), 64)
-    for k in range(3):
-        lr2_out[k] = two_rows(jnp.transpose(jnp.concatenate(turned[k], axis=0)), 64)
+    l2_out[...] = two_rows(jnp.transpose(jnp.concatenate(own, axis=0)))
+    lr2_out[...] = two_rows(jnp.transpose(jnp.concatenate(turned[0] + turned[1] + turned[2], axis=0)))
 
 
 def coarse_kernel(series, s_ref, w2, p2, fm_ref, l2, after, u_out, full, t_full):
@@ -283,25 +335,20 @@
 
 
 def join_kernel(last, *refs):
-    (g0, g1, g2, g3, q_ref, u_ref, nl_ref, nacc_ref, fp_ref, lr2, nb_ref, or_ref, coh, fine_ref,
-     s_ref, w2, p2, piece, se, sf) = refs[:20]
+    (g2, g3, g1, g0, q_ref, u_ref, nl_ref, nacc_ref, fp_ref, lr2, nb_ref, or_ref, coh, fine_ref,
+     pack_ref, w2, p2, piece, se, sf, order_ref, spot_ref) = refs[:22]
     table = unpack((g0, g1, g2, g3))
     masks = orient_masks(or_ref)
     fine = fine_ref[...] == 1
     if last:
-        uc_ref, out, n_ref, work = refs[20:]
+        uc_ref, out, n_ref, work = refs[22:]
     else:
-        q_out, n_out, pred, t_out, m0, m1, m2, m3, n_ref, work, series = refs[20:]
+        q_out, n_out, pred, t_out, m0, m1, m2, m3, n_ref, work, series, sums = refs[22:]
 
     def face_terms(values):
         for q in range(NQ):
-            hi, lo = split(flux_rows(fp_ref, q, n_ref))
-            sub = None
-            for k in range(3):
-                w = lr2[k]
-                both = dot(w, hi * masks[k])
-                part = both[:NB] + both[64:64 + NB] + dot(w[:64], lo * masks[k])[:NB]
-                sub = part if sub is None else sub + part
+            halves = jnp.concatenate(split(flux_rows(fp_ref, q, n_ref)), axis=1)
+            sub = side_by_side(lr2[...], jnp.concatenate([halves * m for m in masks], axis=0))
             work[q] = values(q) - sub
 
     ghost_pick(table, nb_ref, nl_ref, n_ref)
@@ -319,20 +366,25 @@
         n_out[q] = nacc_ref[q] + n_ref[q] if nacc_ref is not None else n_ref[q]
         x = jnp.where(fine, after[q], q_ref[q])
         q_out[q] = x
-        series[q] = x
-        pred[q] = x * (1.0 / RATE)
-
-    def step(k, weight):
-        weight = weight * (1.0 / RATE / (k.astype(F32) + 2.0))
-        rows = operator(series, s_ref, w2[...])
-        for q in range(NQ):
-            series[q] = rows[q]
-            pred[q] += weight * rows[q]
-        return weight
-
-    lax.fori_loop(0, ORDER - 1, step, jnp.float32(1.0 / RATE))
-    for q in range(NQ):
-        pred[q] = jnp.where(fine, pred[q], piece[q])
+    order = jnp.broadcast_to(order_ref[0:1, :], (NB, LN))
+    left = lanes((NB, LN)) < LN // 2
+    for j in range(PAIRS):
+        rows = pick(q_out[2 * j], order)
+        other = pick(q_out[2 * j + 1], order) if 2 * j + 1 < NQ else jnp.zeros((NB, LN), F32)
+        rows = jnp.where(left, rows, other)
+        both_ways(series.at[0], j, rows)
+        sums[j] = rows * (1.0 / RATE)
+
+    for k in range(ORDER - 1):
+        weight = (1.0 / RATE) ** (k + 2) / math.factorial(k + 2)
+        rows = packed_operator(series.at[k % 2], pack_ref, w2[...])
+        for j in range(PAIRS):
+            if k < ORDER - 2:
+                both_ways(series.at[(k + 1) % 2], j, rows[j])
+            sums[j] += weight * rows[j]
+    for q in range(NQ):
+        spot = jnp.broadcast_to(spot_ref[q % 2, 0:1, :], (NB, LN))
+        pred[q] = jnp.where(fine, pick(sums[q // 2], spot), piece[q])
     traces(pred, p2[...], t_out)
     send(t_out, se, sf, (m0, m1, m2, m3))
 
@@ -394,7 +446,7 @@
     scratch = [pltpu.VMEM(args[n].shape, args[n].dtype) for n in (1, 5, 6, 13, 14, 10)]
     outs = call(
         first_kernel, "first",
-        [((NQ, NQ, 3, LN), F32), ((128, 3 * NB), BF16), ((2 * FA, NB), BF16),
+        [((NQ, NQ, 3, LN), F32), ((2 * NB, 3 * NB), BF16), ((2 * FA, NB), BF16),
          ((ORDER,) + BIG, F32), (BIG, F32), (TAB, F32)] + [(MSG, F32)] * 4
         + [((1, LN), i32), ((1, LN), i32), ((4, LN), i32), (args[2].shape, F32),
            (args[3].shape, F32), ((4, LN), i32), ((4, LN), i32), ((1, LN), F32), ((1, LN), i32),
@@ -404,9 +456,12 @@
     s_mat, w2, p2, series, pred, table = outs[:6]
     got = exchange(outs[6:10])
     se, sf, nb, fm, fp, nf, turn_code, coh, fine, lift, rotate = outs[10:]
-    l2, lr2 = call(
-        lift_kernel, "lifts", [((128, FA), BF16), ((3, 128, FA), BF16)], [],
-        [lift, rotate])
+    l2, lr2, order, spot, pack = call(
+        lift_kernel, "lifts",
+        [((2 * NB, FA), BF16), ((2 * NB, 3 * FA), BF16), ((8, LN), i32), ((2, 8, LN), i32),
+         ((PAIRS, 2 * PAIRS, 3, LN), F32)],
+        [((NQ, NQ, 8, LN), F32)],
+        [lift, rotate, s_mat, fine])
     total = coarse = None
     state = series[0]
     for sub in range(RATE):
@@ -419,13 +474,13 @@
             coarse = call(
                 coarse_kernel, "coarse_own", [(BIG, F32)], [(BIG, F32), (TAB, F32)],
                 [series, s_mat, w2, p2, fm, l2, outs[4]], 8)[0]
-        common = [*got, state, u, near, total if total is not None else near, fp, lr2, nb, turn_code,
-                  coh, fine, s_mat, w2, p2]
+        common = [got[2], got[3], got[1], got[0], state, u, near, total if total is not None else near, fp, lr2, nb, turn_code,
+                  coh, fine, pack, w2, p2]
         if last:
             out = call(
                 functools.partial(join_kernel, True), "last", [(BIG, F32)],
                 [(TAB, F32), (BIG, F32)],
-                common + [near, se, sf, coarse])[0]
+                common + [near, se, sf, order, spot, coarse])[0]
             return jnp.transpose(out, (1, 0, 2))
         first = total is None
 
@@ -438,8 +493,8 @@
         outs = call(
             kernel, "join",
             [(BIG, F32), (TAB, F32), (BIG, F32), (TAB, F32)] + [(MSG, F32)] * 4,
-            [(TAB, F32), (BIG, F32), (BIG, F32)],
-            common + [piece[0], se, sf])
+            [(TAB, F32), (BIG, F32), ((2, 2 * PAIRS, NB, LN), F32), ((PAIRS, NB, LN), F32)],
+            common + [piece[0], se, sf, order, spot])
         state, total, pred, table = outs[:4]
         got = exchange(outs[4:])
 

time: 72.1 us -> 62.9 us (0.87)
  Pallas kernels: 31.1 us -> 27 us
  waiting for transfers between devices: 22.9 us -> 19.1 us
  starting transfers between devices: 17.8 us -> 16.6 us
    pallas_call x11, Pallas kernels: 31.1 us -> 27 us  [call(): pl.pallas_call(kernel, name=name, out_shape=[jax.ShapeDtypeStruct(s, d) f...]
    ppermute x16, waiting for transfers between devices: 22.9 us -> 19.1 us  [exchange(): got[k] = lax.ppermute(messages[k], 'dom', pairings[k])]
    ppermute x16, starting transfers between devices: 17.8 us -> 16.6 us  [exchange(): got[k] = lax.ppermute(messages[k], 'dom', pairings[k])]
  transfers between devices with their start and end apart: 16 -> 16, of which waited for: 8 -> 8; matrix products, arithmetic and copies ran while one was open for 0% -> 0% of each run, Pallas kernels for 10% -> 12%
where the time goes in v3:
time: 62.9 us; the launch traced here: 62.8 us
  Pallas kernels  27 us (43%)
  waiting for transfers between devices  19.1 us (30%)
  starting transfers between devices  16.6 us (26%)
    pallas_call x11, Pallas kernels, call(): pl.pallas_call(kernel, name=name, out_shape=[jax.ShapeDtypeStruct(s, d) f...  27 us
    ppermute x16, waiting for transfers between devices, exchange(): got[k] = lax.ppermute(messages[k], 'dom', pairings[k])  19.1 us
    ppermute x16, starting transfers between devices, exchange(): got[k] = lax.ppermute(messages[k], 'dom', pairings[k])  16.6 us
  transfers between devices with their start and end apart: 16, of which 8 were waited for; matrix products, arithmetic and copies ran while one was open for 0% of the time, Pallas kernels for 12%

profile of v3, /device:TPU:24, one launch (start us, length us, event | category | flops | bytes accessed | tf_op | source)
XLA Modules:
  0.0 62.8 jit_solution(16157973283250718672)
XLA Ops:
  0.0 5.5 %first.1 = (f32[9,9,3,128]{3,2,1,0:T(4,128)S(1)}, bf16[112,168]{1,0:T(8,128)(2,1)S(1)}, bf16[192,56]{1,0:T(8,128)(2,1)S(1)}, f32[6,9,56,128]{3,2,1,0:T(8,128)S(1...) custom-call(f32[9,56,128]{2,1,0:T(8,128)} %bitcast.11, ...), custom_call_target="tpu_custom_call" | custom-call | flops 50000000 | bytes 4194304 | tf_op jit(solution)/shard_map/first/pallas_call | solution.py:398
  5.5 1.6 %collective-permute-start = (f32[56,128]{1,0:T(8,128)S(1)}, f32[56,128]{1,0:T(8,128)S(1)}, u32[]{:S(2)}, u32[]{:S(2)}) collective-permute-start(f32[56,128]{1,0:T(8,128)S(1)} %get-tuple-element.66), channel_id=1, source_target_pairs={{0,2},{1,3},{2,0},{3,1},{4,6},{5,7},{6,4},{7,5},{8,10},{9,11},{10,... | collective-permute-start | bytes 86024 | tf_op jit(solution)/shard_map/ppermute | solution.py:436
  7.1 7.6 %collective-permute-start.1 = (f32[56,128]{1,0:T(8,128)S(1)}, f32[56,128]{1,0:T(8,128)S(1)}, u32[]{:S(2)}, u32[]{:S(2)}) collective-permute-start(f32[56,128]{1,0:T(8,128)S(1)} %get-tuple-element.67), channel_id=1, source_target_pairs={{0,1},{1,0},{2,4},{3,5},{4,2},{5,3},{6,8},{7,9},{8,6},{9,7},{10,12... | collective-permute-start | bytes 86024 | tf_op jit(solution)/shard_map/ppermute | solution.py:436
  14.7 0.0 collective-permute-start.2
  14.7 0.0 collective-permute-start.3
  14.7 0.7 %lifts.1 = (bf16[112,96]{1,0:T(8,128)(2,1)S(1)}, bf16[112,288]{1,0:T(8,128)(2,1)S(1)}, s32[8,128]{1,0:T(8,128)S(1)}, s32[2,8,128]{2,1,0:T(8,128)S(1)}, f32[5,10,3,128]{3,2,1,0:T(4,128)S(1)}) custom-call(f32[21,4,56]{2,1,0:T(4,128)S(1)} %get-tuple-element.76.lift, f32[3,21,21]{2,1,0:T(8,128)S(1)} %get-tuple-element.77.rotate, ...), custom_call_target="tpu_custom_call" | custom-call | flops 50000000 | bytes 4194304 | tf_op jit(solution)/shard_map/lifts/pallas_call | solution.py:398
  15.5 1.4 %local.4 = (f32[9,56,128]{2,1,0:T(8,128)S(1)}, f32[9,96,128]{2,1,0:T(8,128)S(1)}, f32[9,56,128]{2,1,0:T(8,128)S(1)}) custom-call(f32[9,56,128]{2,1,0:T(8,128)S(1)} %slice_bitcast_fusion.q_ref.refs_4_, f32[9,56,128]{2,1,0:T(8,128)S(1)} %get-tuple-element.71.pred, f32[9,96,128]{2,1,0:T(8,128)S(1)} %get-tuple-element.72.t_ref, ...), custom_call_target="tpu_custom_call" | custom-call | flops 50000000 | bytes 4194304 | tf_op jit(solution)/shard_map/local/pallas_call | solution.py:398
  16.8 0.0 collective-permute-done.refs_0_
  16.8 0.0 collective-permute-done.1.refs_1_
  16.9 5.3 %collective-permute-done.2.refs_2_ = f32[56,128]{1,0:T(8,128)S(1)} collective-permute-done((f32[56,128]{1,0:T(8,128)S(1)}, f32[56,128]{1,0:T(8,128)S(1)}, u32[]{:S(2)}, u32[]{:S(2)}) %collective-permute-start.2) | collective-permute-done | bytes 28704 | tf_op jit(solution)/shard_map/ppermute | solution.py:436
  22.2 0.0 collective-permute-done.3.refs_3_
  22.2 4.1 %join.3 = (f32[9,56,128]{2,1,0:T(8,128)S(1)}, f32[9,96,128]{2,1,0:T(8,128)S(1)}, f32[9,56,128]{2,1,0:T(8,128)S(1)}, f32[9,96,128]{2,1,0:T(8,128)S(1)}, f32[56,12...) custom-call(f32[56,128]{1,0:T(8,128)S(1)} %collective-permute-done.refs_0_, ...), custom_call_target="tpu_custom_call" | custom-call | flops 50000000 | bytes 4194304 | tf_op jit(solution)/shard_map/join/pallas_call | solution.py:398
  26.3 0.1 collective-permute-start.4
  26.4 1.3 %collective-permute-start.5 = (f32[56,128]{1,0:T(8,128)S(1)}, f32[56,128]{1,0:T(8,128)S(1)}, u32[]{:S(2)}, u32[]{:S(2)}) collective-permute-start(f32[56,128]{1,0:T(8,128)S(1)} %get-tuple-element.96), channel_id=1, source_target_pairs={{0,1},{1,0},{2,4},{3,5},{4,2},{5,3},{6,8},{7,9},{8,6},{9,7},{10,12... | collective-permute-start | bytes 86024 | tf_op jit(solution)/shard_map/ppermute | solution.py:436
  27.7 0.1 collective-permute-start.6
  27.8 0.7 %collective-permute-start.7 = (f32[56,128]{1,0:T(8,128)S(1)}, f32[56,128]{1,0:T(8,128)S(1)}, u32[]{:S(2)}, u32[]{:S(2)}) collective-permute-start(f32[56,128]{1,0:T(8,128)S(1)} %get-tuple-element.98.after), channel_id=1, source_target_pairs={{0,1},{1,0},{2,3},{3,2},{4,5},{5,4},{6,7},{7,6},{8,9},{9,8},{10,11... | collective-permute-start | bytes 86024 | tf_op jit(solution)/shard_map/ppermute | solution.py:436
  28.5 1.4 %local.5 = (f32[9,56,128]{2,1,0:T(8,128)S(1)}, f32[9,96,128]{2,1,0:T(8,128)S(1)}, f32[9,56,128]{2,1,0:T(8,128)S(1)}) custom-call(f32[9,56,128]{2,1,0:T(8,128)S(1)} %get-tuple-element.99.q_ref.refs_4_, f32[9,56,128]{2,1,0:T(8,128)S(1)} %get-tuple-element.100.pred, f32[9,96,128]{2,1,0:T(8,128)S(1)} %get-tuple-element.101.t_ref, ...), custom_call_target="tpu_custom_call" | custom-call | flops 50000000 | bytes 4194304 | tf_op jit(solution)/shard_map/local/pallas_call | solution.py:398
  29.9 0.4 collective-permute-done.4.refs_0_
  30.3 4.5 %collective-permute-done.5.refs_1_ = f32[56,128]{1,0:T(8,128)S(1)} collective-permute-done((f32[56,128]{1,0:T(8,128)S(1)}, f32[56,128]{1,0:T(8,128)S(1)}, u32[]{:S(2)}, u32[]{:S(2)}) %collective-permute-start.5) | collective-permute-done | bytes 28704 | tf_op jit(solution)/shard_map/ppermute | solution.py:436
  34.8 0.5 collective-permute-done.6.refs_2_
  35.2 0.0 collective-permute-done.7.refs_3_
  35.2 4.1 %join.4 = (f32[9,56,128]{2,1,0:T(8,128)S(1)}, f32[9,96,128]{2,1,0:T(8,128)S(1)}, f32[9,56,128]{2,1,0:T(8,128)S(1)}, f32[9,96,128]{2,1,0:T(8,128)S(1)}, f32[56,12...) custom-call(f32[56,128]{1,0:T(8,128)S(1)} %collective-permute-done.4.refs_0_, ...), custom_call_target="tpu_custom_call" | custom-call | flops 50000000 | bytes 4194304 | tf_op jit(solution)/shard_map/join/pallas_call | solution.py:398
  39.4 0.1 collective-permute-start.8
  39.5 1.2 %collective-permute-start.9 = (f32[56,128]{1,0:T(8,128)S(1)}, f32[56,128]{1,0:T(8,128)S(1)}, u32[]{:S(2)}, u32[]{:S(2)}) collective-permute-start(f32[56,128]{1,0:T(8,128)S(1)} %get-tuple-element.107), channel_id=1, source_target_pairs={{0,1},{1,0},{2,4},{3,5},{4,2},{5,3},{6,8},{7,9},{8,6},{9,7},{10,12... | collective-permute-start | bytes 86024 | tf_op jit(solution)/shard_map/ppermute | solution.py:436
  40.7 1.2 %collective-permute-start.10 = (f32[56,128]{1,0:T(8,128)S(1)}, f32[56,128]{1,0:T(8,128)S(1)}, u32[]{:S(2)}, u32[]{:S(2)}) collective-permute-start(f32[56,128]{1,0:T(8,128)S(1)} %get-tuple-element.108), channel_id=1, source_target_pairs={{0,255},{1,2},{2,1},{3,4},{4,3},{5,6},{6,5},{7,8},{8,7},{9,10},{10... | collective-permute-start | bytes 86024 | tf_op jit(solution)/shard_map/ppermute | solution.py:436
  41.9 0.0 collective-permute-start.11
  41.9 1.4 %local.6 = (f32[9,56,128]{2,1,0:T(8,128)S(1)}, f32[9,96,128]{2,1,0:T(8,128)S(1)}, f32[9,56,128]{2,1,0:T(8,128)S(1)}) custom-call(f32[9,56,128]{2,1,0:T(8,128)S(1)} %get-tuple-element.110.q_ref.refs_4_, f32[9,56,128]{2,1,0:T(8,128)S(1)} %get-tuple-element.111.pred, f32[9,96,128]{2,1,0:T(8,128)S(1)} %get-tuple-element.112.t_ref, ...), custom_call_target="tpu_custom_call" | custom-call | flops 50000000 | bytes 4194304 | tf_op jit(solution)/shard_map/local/pallas_call | solution.py:398
  43.3 0.0 collective-permute-done.8.refs_0_
  43.4 4.3 %collective-permute-done.9.refs_1_ = f32[56,128]{1,0:T(8,128)S(1)} collective-permute-done((f32[56,128]{1,0:T(8,128)S(1)}, f32[56,128]{1,0:T(8,128)S(1)}, u32[]{:S(2)}, u32[]{:S(2)}) %collective-permute-start.9) | collective-permute-done | bytes 28704 | tf_op jit(solution)/shard_map/ppermute | solution.py:436
  47.6 0.6 collective-permute-done.10.refs_2_
  48.2 0.0 collective-permute-done.11.refs_3_
  48.2 4.1 %join.5 = (f32[9,56,128]{2,1,0:T(8,128)S(1)}, f32[9,96,128]{2,1,0:T(8,128)S(1)}, f32[9,56,128]{2,1,0:T(8,128)S(1)}, f32[9,96,128]{2,1,0:T(8,128)S(1)}, f32[56,12...) custom-call(f32[56,128]{1,0:T(8,128)S(1)} %collective-permute-done.8.refs_0_, ...), custom_call_target="tpu_custom_call" | custom-call | flops 50000000 | bytes 4194304 | tf_op jit(solution)/shard_map/join/pallas_call | solution.py:398
  52.3 0.1 collective-permute-start.12
  52.4 1.2 %collective-permute-start.13 = (f32[56,128]{1,0:T(8,128)S(1)}, f32[56,128]{1,0:T(8,128)S(1)}, u32[]{:S(2)}, u32[]{:S(2)}) collective-permute-start(f32[56,128]{1,0:T(8,128)S(1)} %get-tuple-element.118), channel_id=1, source_target_pairs={{0,1},{1,0},{2,4},{3,5},{4,2},{5,3},{6,8},{7,9},{8,6},{9,7},{10,12... | collective-permute-start | bytes 86024 | tf_op jit(solution)/shard_map/ppermute | solution.py:436
  53.6 1.4 %collective-permute-start.14 = (f32[56,128]{1,0:T(8,128)S(1)}, f32[56,128]{1,0:T(8,128)S(1)}, u32[]{:S(2)}, u32[]{:S(2)}) collective-permute-start(f32[56,128]{1,0:T(8,128)S(1)} %get-tuple-element.119), channel_id=1, source_target_pairs={{0,255},{1,2},{2,1},{3,4},{4,3},{5,6},{6,5},{7,8},{8,7},{9,10},{10... | collective-permute-start | bytes 86024 | tf_op jit(solution)/shard_map/ppermute | solution.py:436
  55.0 0.0 collective-permute-start.15
  55.0 1.2 %coarse_own.1.refs_22_ = f32[9,56,128]{2,1,0:T(8,128)S(1)} custom-call(f32[6,9,56,128]{3,2,1,0:T(8,128)S(1)} %get-tuple-element.70.series, f32[9,9,3,128]{3,2,1,0:T(4,128)S(1)} %get-tuple-element.73.s_ref, bf16[112,168]{1,0:T(8,128)(2,1)S(1)} %get-tuple-element.74.w2.refs_15_, bf16[192,56]{1,0:T(8,128)(2,1)S(1)} %get-tuple-element.89.refs_16_.p2, ...), custom_call_target="tpu_custom_call" | custom-call | flops 50000000 | bytes 8388608 | tf_op jit(solution)/shard_map/coarse_own/pallas_call | solution.py:398
  56.2 1.4 %local.7 = (f32[9,56,128]{2,1,0:T(8,128)S(1)}, f32[9,96,128]{2,1,0:T(8,128)S(1)}) custom-call(f32[9,56,128]{2,1,0:T(8,128)S(1)} %get-tuple-element.121.q_ref.refs_4_, f32[9,56,128]{2,1,0:T(8,128)S(1)} %get-tuple-element.122.pred, f32[9,96,128]{2,1,0:T(8,128)S(1)} %get-tuple-element.123.t_ref, f32[9,9,3,128]{3,2,1,0:T(4,128)S(1)} %get-tuple-element.73.s_ref, ...), custom_call_target="tpu_custom_call" | custom-call | flops 50000000 | bytes 4194304 | tf_op jit(solution)/shard_map/local/pallas_call | solution.py:398
  57.6 0.0 collective-permute-done.12.refs_0_
  57.6 3.0 %collective-permute-done.13.refs_1_ = f32[56,128]{1,0:T(8,128)S(1)} collective-permute-done((f32[56,128]{1,0:T(8,128)S(1)}, f32[56,128]{1,0:T(8,128)S(1)}, u32[]{:S(2)}, u32[]{:S(2)}) %collective-permute-start.13) | collective-permute-done | bytes 28704 | tf_op jit(solution)/shard_map/ppermute | solution.py:436
  60.6 0.5 collective-permute-done.14.refs_2_
  61.1 0.0 collective-permute-done.15.refs_3_
  61.1 1.7 %last.1 = f32[9,56,128]{2,1,0:T(8,128)} custom-call(f32[56,128]{1,0:T(8,128)S(1)} %collective-permute-done.12.refs_0_, f32[56,128]{1,0:T(8,128)S(1)} %collective-permute-done.13.refs_1_, f32[56,128]{1,0:T(8,128)S(1)} %collective-permute-done.14.refs_2_, f32[56,128]{1,0:T(8,128)S(1)} %collective-permute-done.15.refs_3_, ...), custom_call_target="tpu_custom_call" | custom-call | flops 50000000 | bytes 4194304 | tf_op jit(solution)/shard_map/last/pallas_call | solution.py:398
  (1 shorter events, 0.0 us)
Async XLA Ops:
  5.5 11.3 %collective-permute-start = (f32[56,128]{1,0:T(8,128)S(1)}, f32[56,128]{1,0:T(8,128)S(1)}, u32[]{:S(2)}, u32[]{:S(2)}) collective-permute-start(f32[56,128]{1,0:T(8,128)S(1)} %get-tuple-element.66), channel_id=1, source_target_pairs={{0,2},{1,3},{2,0},{3,1},{4,6},{5,7},{6,4},{7,5},{8,10},{9,11},{10,... | collective-permute-start | bytes 86024 | tf_op jit(solution)/shard_map/ppermute | solution.py:436
  7.1 9.7 %collective-permute-start.1 = (f32[56,128]{1,0:T(8,128)S(1)}, f32[56,128]{1,0:T(8,128)S(1)}, u32[]{:S(2)}, u32[]{:S(2)}) collective-permute-start(f32[56,128]{1,0:T(8,128)S(1)} %get-tuple-element.67), channel_id=1, source_target_pairs={{0,1},{1,0},{2,4},{3,5},{4,2},{5,3},{6,8},{7,9},{8,6},{9,7},{10,12... | collective-permute-start | bytes 86024 | tf_op jit(solution)/shard_map/ppermute | solution.py:436
  14.7 7.5 %collective-permute-start.2 = (f32[56,128]{1,0:T(8,128)S(1)}, f32[56,128]{1,0:T(8,128)S(1)}, u32[]{:S(2)}, u32[]{:S(2)}) collective-permute-start(f32[56,128]{1,0:T(8,128)S(1)} %get-tuple-element.68), channel_id=1, source_target_pairs={{0,255},{1,2},{2,1},{3,4},{4,3},{5,6},{6,5},{7,8},{8,7},{9,10},{10... | collective-permute-start | bytes 86024 | tf_op jit(solution)/shard_map/ppermute | solution.py:436
  14.7 7.5 %collective-permute-start.3 = (f32[56,128]{1,0:T(8,128)S(1)}, f32[56,128]{1,0:T(8,128)S(1)}, u32[]{:S(2)}, u32[]{:S(2)}) collective-permute-start(f32[56,128]{1,0:T(8,128)S(1)} %get-tuple-element.69), channel_id=1, source_target_pairs={{0,1},{1,0},{2,3},{3,2},{4,5},{5,4},{6,7},{7,6},{8,9},{9,8},{10,11... | collective-permute-start | bytes 86024 | tf_op jit(solution)/shard_map/ppermute | solution.py:436
  26.3 4.0 %collective-permute-start.4 = (f32[56,128]{1,0:T(8,128)S(1)}, f32[56,128]{1,0:T(8,128)S(1)}, u32[]{:S(2)}, u32[]{:S(2)}) collective-permute-start(f32[56,128]{1,0:T(8,128)S(1)} %get-tuple-element.95), channel_id=1, source_target_pairs={{0,2},{1,3},{2,0},{3,1},{4,6},{5,7},{6,4},{7,5},{8,10},{9,11},{10,... | collective-permute-start | bytes 86024 | tf_op jit(solution)/shard_map/ppermute | solution.py:436
  26.4 8.4 %collective-permute-start.5 = (f32[56,128]{1,0:T(8,128)S(1)}, f32[56,128]{1,0:T(8,128)S(1)}, u32[]{:S(2)}, u32[]{:S(2)}) collective-permute-start(f32[56,128]{1,0:T(8,128)S(1)} %get-tuple-element.96), channel_id=1, source_target_pairs={{0,1},{1,0},{2,4},{3,5},{4,2},{5,3},{6,8},{7,9},{8,6},{9,7},{10,12... | collective-permute-start | bytes 86024 | tf_op jit(solution)/shard_map/ppermute | solution.py:436
  27.7 7.5 %collective-permute-start.6 = (f32[56,128]{1,0:T(8,128)S(1)}, f32[56,128]{1,0:T(8,128)S(1)}, u32[]{:S(2)}, u32[]{:S(2)}) collective-permute-start(f32[56,128]{1,0:T(8,128)S(1)} %get-tuple-element.97), channel_id=1, source_target_pairs={{0,255},{1,2},{2,1},{3,4},{4,3},{5,6},{6,5},{7,8},{8,7},{9,10},{10... | collective-permute-start | bytes 86024 | tf_op jit(solution)/shard_map/ppermute | solution.py:436
  27.8 7.4 %collective-permute-start.7 = (f32[56,128]{1,0:T(8,128)S(1)}, f32[56,128]{1,0:T(8,128)S(1)}, u32[]{:S(2)}, u32[]{:S(2)}) collective-permute-start(f32[56,128]{1,0:T(8,128)S(1)} %get-tuple-element.98.after), channel_id=1, source_target_pairs={{0,1},{1,0},{2,3},{3,2},{4,5},{5,4},{6,7},{7,6},{8,9},{9,8},{10,11... | collective-permute-start | bytes 86024 | tf_op jit(solution)/shard_map/ppermute | solution.py:436
  39.4 4.0 %collective-permute-start.8 = (f32[56,128]{1,0:T(8,128)S(1)}, f32[56,128]{1,0:T(8,128)S(1)}, u32[]{:S(2)}, u32[]{:S(2)}) collective-permute-start(f32[56,128]{1,0:T(8,128)S(1)} %get-tuple-element.106), channel_id=1, source_target_pairs={{0,2},{1,3},{2,0},{3,1},{4,6},{5,7},{6,4},{7,5},{8,10},{9,11},{10,... | collective-permute-start | bytes 86024 | tf_op jit(solution)/shard_map/ppermute | solution.py:436
  39.5 8.2 %collective-permute-start.9 = (f32[56,128]{1,0:T(8,128)S(1)}, f32[56,128]{1,0:T(8,128)S(1)}, u32[]{:S(2)}, u32[]{:S(2)}) collective-permute-start(f32[56,128]{1,0:T(8,128)S(1)} %get-tuple-element.107), channel_id=1, source_target_pairs={{0,1},{1,0},{2,4},{3,5},{4,2},{5,3},{6,8},{7,9},{8,6},{9,7},{10,12... | collective-permute-start | bytes 86024 | tf_op jit(solution)/shard_map/ppermute | solution.py:436
  40.7 7.5 %collective-permute-start.10 = (f32[56,128]{1,0:T(8,128)S(1)}, f32[56,128]{1,0:T(8,128)S(1)}, u32[]{:S(2)}, u32[]{:S(2)}) collective-permute-start(f32[56,128]{1,0:T(8,128)S(1)} %get-tuple-element.108), channel_id=1, source_target_pairs={{0,255},{1,2},{2,1},{3,4},{4,3},{5,6},{6,5},{7,8},{8,7},{9,10},{10... | collective-permute-start | bytes 86024 | tf_op jit(solution)/shard_map/ppermute | solution.py:436
  41.9 6.3 %collective-permute-start.11 = (f32[56,128]{1,0:T(8,128)S(1)}, f32[56,128]{1,0:T(8,128)S(1)}, u32[]{:S(2)}, u32[]{:S(2)}) collective-permute-start(f32[56,128]{1,0:T(8,128)S(1)} %get-tuple-element.109), channel_id=1, source_target_pairs={{0,1},{1,0},{2,3},{3,2},{4,5},{5,4},{6,7},{7,6},{8,9},{9,8},{10,11... | collective-permute-start | bytes 86024 | tf_op jit(solution)/shard_map/ppermute | solution.py:436
  52.3 5.3 %collective-permute-start.12 = (f32[56,128]{1,0:T(8,128)S(1)}, f32[56,128]{1,0:T(8,128)S(1)}, u32[]{:S(2)}, u32[]{:S(2)}) collective-permute-start(f32[56,128]{1,0:T(8,128)S(1)} %get-tuple-element.117), channel_id=1, source_target_pairs={{0,2},{1,3},{2,0},{3,1},{4,6},{5,7},{6,4},{7,5},{8,10},{9,11},{10,... | collective-permute-start | bytes 86024 | tf_op jit(solution)/shard_map/ppermute | solution.py:436
  52.4 8.2 %collective-permute-start.13 = (f32[56,128]{1,0:T(8,128)S(1)}, f32[56,128]{1,0:T(8,128)S(1)}, u32[]{:S(2)}, u32[]{:S(2)}) collective-permute-start(f32[56,128]{1,0:T(8,128)S(1)} %get-tuple-element.118), channel_id=1, source_target_pairs={{0,1},{1,0},{2,4},{3,5},{4,2},{5,3},{6,8},{7,9},{8,6},{9,7},{10,12... | collective-permute-start | bytes 86024 | tf_op jit(solution)/shard_map/ppermute | solution.py:436
  53.6 7.5 %collective-permute-start.14 = (f32[56,128]{1,0:T(8,128)S(1)}, f32[56,128]{1,0:T(8,128)S(1)}, u32[]{:S(2)}, u32[]{:S(2)}) collective-permute-start(f32[56,128]{1,0:T(8,128)S(1)} %get-tuple-element.119), channel_id=1, source_target_pairs={{0,255},{1,2},{2,1},{3,4},{4,3},{5,6},{6,5},{7,8},{8,7},{9,10},{10... | collective-permute-start | bytes 86024 | tf_op jit(solution)/shard_map/ppermute | solution.py:436
  55.0 6.2 %collective-permute-start.15 = (f32[56,128]{1,0:T(8,128)S(1)}, f32[56,128]{1,0:T(8,128)S(1)}, u32[]{:S(2)}, u32[]{:S(2)}) collective-permute-start(f32[56,128]{1,0:T(8,128)S(1)} %get-tuple-element.120), channel_id=1, source_target_pairs={{0,1},{1,0},{2,3},{3,2},{4,5},{5,4},{6,7},{7,6},{8,9},{9,8},{10,11... | collective-permute-start | bytes 86024 | tf_op jit(solution)/shard_map/ppermute | solution.py:436

commit v4 on v3

--- a/solution.py
+++ b/solution.py
@@ -101,17 +101,15 @@
     return jnp.take_along_axis(rows, index, axis=1, mode="promise_in_bounds")
 
 
-def send(t_ref, se_ref, sf_ref, out_refs):
-    elem = jnp.broadcast_to(se_ref[...], (FR, LN))
-    face = jnp.broadcast_to(sf_ref[...], (FR, LN))
-    rows = []
-    for q in range(NQ):
-        got = pick(t_ref[q, 0:FR], elem)
-        for f in range(1, 4):
-            got = jnp.where(face == f, pick(t_ref[q, f * FR:(f + 1) * FR], elem), got)
-        rows.append(got)
-    rows.append(jnp.zeros((4 * PK - NQ * FR, LN), F32))
-    table = jnp.concatenate(rows, axis=0)
+def chosen_face(face, rows):
+    got = rows(0)
+    for f in range(1, 4):
+        got = jnp.where(face == f, rows(f), got)
+    return got
+
+
+def pack(rows, out_refs):
+    table = jnp.concatenate(rows + [jnp.zeros((4 * PK - NQ * FR, LN), F32)], axis=0)
     group = lanes((PK, LN)) // 32
     for k in range(4):
         message = None
@@ -121,6 +119,24 @@
                 part = pltpu.roll(part, ((g - k) * 32) % LN, 1)
             message = part if message is None else jnp.where(group == g, part, message)
         out_refs[k][...] = message
+
+
+def send(t_ref, se_ref, sf_ref, out_refs):
+    elem = jnp.broadcast_to(se_ref[...], (FR, LN))
+    face = jnp.broadcast_to(sf_ref[...], (FR, LN))
+    pack([chosen_face(face, lambda f: pick(t_ref[q, f * FR:(f + 1) * FR], elem))
+          for q in range(NQ)], out_refs)
+
+
+def send_packed(t_ref, coarse_ref, spot_ref, slot_fine, sf_ref, out_refs):
+    face = jnp.broadcast_to(sf_ref[...], (FR, LN))
+    is_fine = jnp.broadcast_to(slot_fine[0:1, :], (FR, LN)) == 1
+    rows = []
+    for q in range(NQ):
+        spot = jnp.broadcast_to(spot_ref[q % 2, 0:1, :], (FR, LN))
+        got = chosen_face(face, lambda f: pick(t_ref[q // 2, f * FR:(f + 1) * FR], spot))
+        rows.append(jnp.where(is_fine, got, coarse_ref[q]))
+    pack(rows, out_refs)
 
 
 def unpack(in_refs):
@@ -150,15 +166,19 @@
             out_ref[q, f * FR:(f + 1) * FR] = got
 
 
-def ghost_pick(table, nb_ref, local_ref, out_ref):
+def ghost_rows(values, nb_ref):
+    out = []
     for f in range(4):
         where = jnp.broadcast_to(nb_ref[f:f + 1, :], (FR, LN))
         slot = jnp.clip(where - LN, 0, LN - 1)
         ghost = (where >= LN) & (where < 2 * LN)
-        for q in range(NQ):
-            got = pick(table[q * FR:(q + 1) * FR], slot)
-            out_ref[q, f * FR:(f + 1) * FR] = jnp.where(
-                ghost, got, local_ref[q, f * FR:(f + 1) * FR])
+        out.append(jnp.where(ghost, pick(values, slot), 0.0))
+    return jnp.concatenate(out, axis=0)
+
+
+def turned_lift(lr2, masks, rows):
+    halves = jnp.concatenate(split(rows), axis=1)
+    return side_by_side(lr2, jnp.concatenate([halves * m for m in masks], axis=0))
 
 
 def flux_rows(f_ref, q, t_ref):
@@ -271,7 +291,8 @@
     nb_out[...] = jnp.where((ghost >= 0) & (ghost < LN), LN + place_of * 32 + slot, nb[...])
 
 
-def lift_kernel(lift, rotate, s_ref, fine_ref, l2_out, lr2_out, order_out, spot_out, pack_out, rows):
+def lift_kernel(lift, rotate, s_ref, fine_ref, se_ref, nb_ref, fp_ref, l2_out, lr2_out, order_out,
+                spot_out, pack_out, slot_spot, slot_fine, slot_flux, rows):
     is_fine = jnp.broadcast_to(fine_ref[...], (LN, LN))
     down = lax.broadcasted_iota(jnp.int32, (LN, LN), 0)
     across = lanes((LN, LN))
@@ -286,6 +307,22 @@
     spot_out[0] = low[0:8]
     spot_out[1] = low[0:8] + LN // 2
     order = order[0:8]
+    elem = jnp.broadcast_to(se_ref[...], (8, LN))
+    slot_spot[0] = pick(low[0:8], elem)
+    slot_spot[1] = slot_spot[0] + LN // 2
+    slot_fine[...] = pick(jnp.broadcast_to(fine_ref[...], (8, LN)), elem)
+    target = face = jnp.zeros((LN, LN), F32)
+    for f in range(4):
+        named = jnp.transpose(jnp.broadcast_to(nb_ref[f:f + 1, :], (LN, LN)).astype(F32))
+        hit = (named == (across + LN).astype(F32)).astype(F32).astype(BF16)
+        target = target + dot(across.astype(F32).astype(BF16), hit)
+        face = face + f * dot(jnp.ones((LN, LN), BF16), hit)
+    target = target[0:8].astype(jnp.int32)
+    face = face[0:1].astype(jnp.int32)
+    for q in range(NQ):
+        for p in range(NQ):
+            got = pick(jnp.concatenate([fp_ref[q, p], jnp.zeros((4, LN), F32)], axis=0), target)
+            slot_flux[q, p:p + 1, :] = chosen_face(face, lambda f: got[f:f + 1])
     for q in range(NQ):
         for p in range(q + 1):
             got = pick(jnp.concatenate([s_ref[q, p], jnp.zeros((5, LN), F32)], axis=0), order)
@@ -323,49 +360,72 @@
         u_out[q] = series[0, q] + rows[q] - own_term(fm_ref, t_full, l2[...], q)
 
 
-def local_kernel(sub, q_ref, pred, t_ref, s_ref, w2, fm_ref, l2, nb_ref, nf_ref, series, u_out,
-                 n_out, *next_out):
+def local_kernel(sub, *refs):
+    (q_ref, s_ref, w2, p2, fm_ref, l2, fp_ref, lr2, nb_ref, nf_ref, or_ref, series, se, sf, fine_ref,
+     spot_ref) = refs[:16]
+    if sub == 0:
+        pred, t_ref = refs[16:18]
+        rest = refs[18:]
+    else:
+        sums, piece = refs[16:18]
+        pred, t_ref = refs[-2:]
+        rest = refs[18:-2]
+        fine = fine_ref[...] == 1
+        for q in range(NQ):
+            spot = jnp.broadcast_to(spot_ref[q % 2, 0:1, :], (NB, LN))
+            pred[q] = jnp.where(fine, pick(sums[q // 2], spot), piece[q])
+        traces(pred, p2[...], t_ref)
+    u_out, near_out, *coming, n_ref = rest
     rows = operator(pred, s_ref, w2[...])
     for q in range(NQ):
         u_out[q] = q_ref[q] + rows[q] - own_term(fm_ref, t_ref, l2[...], q)
-    local_pick(t_ref, nb_ref, nf_ref, n_out)
-    if next_out:
+    local_pick(t_ref, nb_ref, nf_ref, n_ref)
+    masks = orient_masks(or_ref)
+    for q in range(NQ):
+        near_out[q] = turned_lift(lr2[...], masks, flux_rows(fp_ref, q, n_ref))
+    if coming:
+        piece_out, slots_out = coming
+        elem = jnp.broadcast_to(se[...], (NB, LN))
+        face = jnp.broadcast_to(sf[...], (FR, LN))
         for q in range(NQ):
-            next_out[0][q] = weigh(series, (sub + 2) / RATE, (sub + 1) / RATE, q)
-
-
-def join_kernel(last, *refs):
-    (g2, g3, g1, g0, q_ref, u_ref, nl_ref, nacc_ref, fp_ref, lr2, nb_ref, or_ref, coh, fine_ref,
-     pack_ref, w2, p2, piece, se, sf, order_ref, spot_ref) = refs[:22]
+            values = weigh(series, (sub + 2) / RATE, (sub + 1) / RATE, q)
+            piece_out[q] = values
+            table = times(p2[...], pick(values, elem), FA)
+            slots_out[q] = chosen_face(face, lambda f: table[f * FR:(f + 1) * FR])
+
+
+def ghost_terms(refs):
+    (g2, g3, g1, g0, flux, lr2, nb_ref, or_ref) = refs
     table = unpack((g0, g1, g2, g3))
     masks = orient_masks(or_ref)
+    for q in range(NQ):
+        total = flux[q, 0:1, :] * table[:FR]
+        for p in range(1, NQ):
+            total = total + flux[q, p:p + 1, :] * table[p * FR:(p + 1) * FR]
+        yield q, turned_lift(lr2[...], masks, ghost_rows(total, nb_ref))
+
+
+def last_kernel(*refs):
+    u_ref, near, acc, uc_ref, coh, fine_ref, out, work = refs[8:]
     fine = fine_ref[...] == 1
-    if last:
-        uc_ref, out, n_ref, work = refs[22:]
-    else:
-        q_out, n_out, pred, t_out, m0, m1, m2, m3, n_ref, work, series, sums = refs[22:]
-
-    def face_terms(values):
-        for q in range(NQ):
-            halves = jnp.concatenate(split(flux_rows(fp_ref, q, n_ref)), axis=1)
-            sub = side_by_side(lr2[...], jnp.concatenate([halves * m for m in masks], axis=0))
-            work[q] = values(q) - sub
-
-    ghost_pick(table, nb_ref, nl_ref, n_ref)
-    if last:
-        for q in range(NQ):
-            n_ref[q] = jnp.where(fine, n_ref[q], nacc_ref[q] + n_ref[q])
-        face_terms(lambda q: jnp.where(fine, u_ref[q], uc_ref[q]))
-        after = plastic(work, coh[...])
-        for q in range(NQ):
-            out[q] = after[q]
-        return
-    face_terms(lambda q: u_ref[q])
+    for q, term in ghost_terms(refs[:8]):
+        work[q] = jnp.where(fine, u_ref[q], uc_ref[q] - acc[q]) - near[q] - term
     after = plastic(work, coh[...])
     for q in range(NQ):
-        n_out[q] = nacc_ref[q] + n_ref[q] if nacc_ref is not None else n_ref[q]
-        x = jnp.where(fine, after[q], q_ref[q])
-        q_out[q] = x
+        out[q] = after[q]
+
+
+def join_kernel(first, *refs):
+    (u_ref, near, acc, coh, fine_ref, q_ref, pack_ref, w2, p2, slots, sf, order_ref, spot_ref,
+     slot_fine, q_out, acc_out, sums, m0, m1, m2, m3, work, series, t_ref) = refs[8:]
+    fine = fine_ref[...] == 1
+    for q, term in ghost_terms(refs[:8]):
+        term = near[q] + term
+        work[q] = u_ref[q] - term
+        acc_out[q] = term if first else acc[q] + term
+    after = plastic(work, coh[...])
+    for q in range(NQ):
+        q_out[q] = jnp.where(fine, after[q], q_ref[q])
     order = jnp.broadcast_to(order_ref[0:1, :], (NB, LN))
     left = lanes((NB, LN)) < LN // 2
     for j in range(PAIRS):
@@ -374,7 +434,6 @@
         rows = jnp.where(left, rows, other)
         both_ways(series.at[0], j, rows)
         sums[j] = rows * (1.0 / RATE)
-
     for k in range(ORDER - 1):
         weight = (1.0 / RATE) ** (k + 2) / math.factorial(k + 2)
         rows = packed_operator(series.at[k % 2], pack_ref, w2[...])
@@ -382,11 +441,9 @@
             if k < ORDER - 2:
                 both_ways(series.at[(k + 1) % 2], j, rows[j])
             sums[j] += weight * rows[j]
-    for q in range(NQ):
-        spot = jnp.broadcast_to(spot_ref[q % 2, 0:1, :], (NB, LN))
-        pred[q] = jnp.where(fine, pick(sums[q // 2], spot), piece[q])
-    traces(pred, p2[...], t_out)
-    send(t_out, se, sf, (m0, m1, m2, m3))
+    for j in range(PAIRS):
+        t_ref[j] = times(p2[...], sums[j], FA)
+    send_packed(t_ref, slots, spot_ref, slot_fine, sf, (m0, m1, m2, m3))
 
 
 BIG = (NQ, NB, LN)
@@ -456,47 +513,42 @@
     s_mat, w2, p2, series, pred, table = outs[:6]
     got = exchange(outs[6:10])
     se, sf, nb, fm, fp, nf, turn_code, coh, fine, lift, rotate = outs[10:]
-    l2, lr2, order, spot, pack = call(
+    l2, lr2, order, spot, packed, slot_spot, slot_fine, slot_flux = call(
         lift_kernel, "lifts",
         [((2 * NB, FA), BF16), ((2 * NB, 3 * FA), BF16), ((8, LN), i32), ((2, 8, LN), i32),
-         ((PAIRS, 2 * PAIRS, 3, LN), F32)],
+         ((PAIRS, 2 * PAIRS, 3, LN), F32), ((2, 8, LN), i32), ((8, LN), i32), ((NQ, NQ, LN), F32)],
         [((NQ, NQ, 8, LN), F32)],
-        [lift, rotate, s_mat, fine])
-    total = coarse = None
+        [lift, rotate, s_mat, fine, se, nb, fp])
+    acc = sums = piece = None
     state = series[0]
+    half = ((PAIRS, NB, LN), F32)
     for sub in range(RATE):
         last = sub == RATE - 1
-        u, near, *piece = call(
+        u, near, *coming = call(
             functools.partial(local_kernel, sub), "local",
-            [(BIG, F32), (TAB, F32)] + ([] if last else [(BIG, F32)]), [],
-            [state, pred, table, s_mat, w2, fm, l2, nb, nf, series])
+            [(BIG, F32), (BIG, F32)] + ([] if last else [(BIG, F32), ((NQ, FR, LN), F32)]),
+            [(TAB, F32)] + ([(BIG, F32), (TAB, F32)] if sub else []),
+            [state, s_mat, w2, p2, fm, l2, fp, lr2, nb, nf, turn_code, series, se, sf, fine, spot]
+            + ([sums, piece] if sub else [pred, table]), 8)
         if sub == 1:
             coarse = call(
                 coarse_kernel, "coarse_own", [(BIG, F32)], [(BIG, F32), (TAB, F32)],
-                [series, s_mat, w2, p2, fm, l2, outs[4]], 8)[0]
-        common = [got[2], got[3], got[1], got[0], state, u, near, total if total is not None else near, fp, lr2, nb, turn_code,
-                  coh, fine, pack, w2, p2]
+                [series, s_mat, w2, p2, fm, l2, outs[3]], 8)[0]
+        common = [got[2], got[3], got[1], got[0], slot_flux, lr2, nb, turn_code, u, near]
         if last:
             out = call(
-                functools.partial(join_kernel, True), "last", [(BIG, F32)],
-                [(TAB, F32), (BIG, F32)],
-                common + [near, se, sf, order, spot, coarse])[0]
+                last_kernel, "last", [(BIG, F32)], [(BIG, F32)],
+                common + [acc, coarse, coh, fine])[0]
             return jnp.transpose(out, (1, 0, 2))
-        first = total is None
-
-        def kernel(*refs, first=first):
-            refs = list(refs)
-            if first:
-                refs[7] = None
-            join_kernel(False, *refs)
-
+        piece, slots = coming
         outs = call(
-            kernel, "join",
-            [(BIG, F32), (TAB, F32), (BIG, F32), (TAB, F32)] + [(MSG, F32)] * 4,
-            [(TAB, F32), (BIG, F32), ((2, 2 * PAIRS, NB, LN), F32), ((PAIRS, NB, LN), F32)],
-            common + [piece[0], se, sf, order, spot])
-        state, total, pred, table = outs[:4]
-        got = exchange(outs[4:])
+            functools.partial(join_kernel, acc is None), "join",
+            [(BIG, F32), (BIG, F32), half] + [(MSG, F32)] * 4,
+            [(BIG, F32), ((2, 2 * PAIRS, NB, LN), F32), ((PAIRS, FA, LN), F32)],
+            common + [near if acc is None else acc, coh, fine, state, packed, w2, p2, slots, sf,
+                      order, slot_spot, slot_fine])
+        state, acc, sums = outs[:3]
+        got = exchange(outs[3:])
 
 
 def solution(mesh):

time: 62.9 us -> 63.4 us (level)
  waiting for transfers between devices: 19.1 us -> 16.6 us
  Pallas kernels: 27 us -> 29.3 us
    ppermute x16, waiting for transfers between devices: 19.1 us -> 16.6 us  [exchange(): got[k] = lax.ppermute(messages[k], 'dom', pairings[k])]
    pallas_call x11, Pallas kernels: 27 us -> 29.3 us  [call(): pl.pallas_call(kernel, name=name, out_shape=[jax.ShapeDtypeStruct(s, d) f...]
    ppermute x16, starting transfers between devices: 16.6 us -> 17.2 us  [exchange(): got[k] = lax.ppermute(messages[k], 'dom', pairings[k])]
  transfers between devices with their start and end apart: 16 -> 16, of which waited for: 8 -> 7; matrix products, arithmetic and copies ran while one was open for 0% -> 0% of each run, Pallas kernels for 12% -> 18%
where the time goes in v4:
time: 63.4 us; the launch traced here: 63.3 us
  Pallas kernels  29.3 us (46%)
  starting transfers between devices  17.2 us (27%)
  waiting for transfers between devices  16.6 us (26%)
    pallas_call x11, Pallas kernels, call(): pl.pallas_call(kernel, name=name, out_shape=[jax.ShapeDtypeStruct(s, d) f...  29.3 us
    ppermute x16, starting transfers between devices, exchange(): got[k] = lax.ppermute(messages[k], 'dom', pairings[k])  17.2 us
    ppermute x16, waiting for transfers between devices, exchange(): got[k] = lax.ppermute(messages[k], 'dom', pairings[k])  16.6 us
  transfers between devices with their start and end apart: 16, of which 7 were waited for; matrix products, arithmetic and copies ran while one was open for 0% of the time, Pallas kernels for 18%

profile of v4, /device:TPU:24, one launch (start us, length us, event | category | flops | bytes accessed | tf_op | source)
XLA Modules:
  0.0 63.3 jit_solution(8908096264245872476)
XLA Ops:
  0.0 5.5 %first.1 = (f32[9,9,3,128]{3,2,1,0:T(4,128)S(1)}, bf16[112,168]{1,0:T(8,128)(2,1)S(1)}, bf16[192,56]{1,0:T(8,128)(2,1)S(1)}, f32[6,9,56,128]{3,2,1,0:T(8,128)S(1...) custom-call(f32[9,56,128]{2,1,0:T(8,128)} %bitcast.11, ...), custom_call_target="tpu_custom_call" | custom-call | flops 50000000 | bytes 4194304 | tf_op jit(solution)/shard_map/first/pallas_call | solution.py:455
  5.5 1.6 %collective-permute-start = (f32[56,128]{1,0:T(8,128)S(1)}, f32[56,128]{1,0:T(8,128)S(1)}, u32[]{:S(2)}, u32[]{:S(2)}) collective-permute-start(f32[56,128]{1,0:T(8,128)S(1)} %get-tuple-element.69), channel_id=1, source_target_pairs={{0,2},{1,3},{2,0},{3,1},{4,6},{5,7},{6,4},{7,5},{8,10},{9,11},{10,... | collective-permute-start | bytes 86024 | tf_op jit(solution)/shard_map/ppermute | solution.py:493
  7.1 7.6 %collective-permute-start.1 = (f32[56,128]{1,0:T(8,128)S(1)}, f32[56,128]{1,0:T(8,128)S(1)}, u32[]{:S(2)}, u32[]{:S(2)}) collective-permute-start(f32[56,128]{1,0:T(8,128)S(1)} %get-tuple-element.70), channel_id=1, source_target_pairs={{0,1},{1,0},{2,4},{3,5},{4,2},{5,3},{6,8},{7,9},{8,6},{9,7},{10,12... | collective-permute-start | bytes 86024 | tf_op jit(solution)/shard_map/ppermute | solution.py:493
  14.7 0.0 collective-permute-start.2
  14.7 0.0 collective-permute-start.3
  14.7 0.8 %lifts.1 = (bf16[112,96]{1,0:T(8,128)(2,1)S(1)}, bf16[112,288]{1,0:T(8,128)(2,1)S(1)}, s32[8,128]{1,0:T(8,128)S(1)}, s32[2,8,128]{2,1,0:T(8,128)S(1)}, f32[5,10,...) custom-call(f32[21,4,56]{2,1,0:T(4,128)S(1)} %get-tuple-element.73.lift, ...), custom_call_target="tpu_custom_call" | custom-call | flops 50000000 | bytes 4194304 | tf_op jit(solution)/shard_map/lifts/pallas_call | solution.py:455
  15.5 2.3 %local.4 = (f32[9,56,128]{2,1,0:T(8,128)S(1)}, f32[9,56,128]{2,1,0:T(8,128)S(1)}, f32[9,56,128]{2,1,0:T(8,128)S(1)}, f32[9,24,128]{2,1,0:T(8,128)S(1)}) custom-call(f32[9,56,128]{2,1,0:T(8,128)S(1)} %slice_bitcast_fusion.refs_0_.refs_13_, f32[9,9,3,128]{3,2,1,0:T(4,128)S(1)} %get-tuple-element.75.s_ref.refs_1_, ...), custom_call_target="tpu_custom_call" | custom-call | flops 50000000 | bytes 8388608 | tf_op jit(solution)/shard_map/local/pallas_call | solution.py:455
  17.8 0.0 collective-permute-done.refs_0_
  17.8 0.0 collective-permute-done.1.refs_1_
  17.8 4.4 %collective-permute-done.2.refs_2_ = f32[56,128]{1,0:T(8,128)S(1)} collective-permute-done((f32[56,128]{1,0:T(8,128)S(1)}, f32[56,128]{1,0:T(8,128)S(1)}, u32[]{:S(2)}, u32[]{:S(2)}) %collective-permute-start.2) | collective-permute-done | bytes 28704 | tf_op jit(solution)/shard_map/ppermute | solution.py:493
  22.2 0.0 collective-permute-done.3.refs_3_
  22.2 3.7 %join.3 = (f32[9,56,128]{2,1,0:T(8,128)S(1)}, f32[9,56,128]{2,1,0:T(8,128)S(1)}, f32[5,56,128]{2,1,0:T(8,128)S(1)}, f32[56,128]{1,0:T(8,128)S(1)}, f32[56,128]{1...) custom-call(f32[56,128]{1,0:T(8,128)S(1)} %collective-permute-done.refs_0_, ...), custom_call_target="tpu_custom_call" | custom-call | flops 50000000 | bytes 4194304 | tf_op jit(solution)/shard_map/join/pallas_call | solution.py:455
  25.9 0.3 collective-permute-start.4
  26.2 2.1 %collective-permute-start.5 = (f32[56,128]{1,0:T(8,128)S(1)}, f32[56,128]{1,0:T(8,128)S(1)}, u32[]{:S(2)}, u32[]{:S(2)}) collective-permute-start(f32[56,128]{1,0:T(8,128)S(1)} %get-tuple-element.102), channel_id=1, source_target_pairs={{0,1},{1,0},{2,4},{3,5},{4,2},{5,3},{6,8},{7,9},{8,6},{9,7},{10,12... | collective-permute-start | bytes 86024 | tf_op jit(solution)/shard_map/ppermute | solution.py:493
  28.3 0.2 collective-permute-start.6
  28.5 0.0 collective-permute-start.7
  28.5 2.4 %local.5 = (f32[9,56,128]{2,1,0:T(8,128)S(1)}, f32[9,56,128]{2,1,0:T(8,128)S(1)}, f32[9,56,128]{2,1,0:T(8,128)S(1)}, f32[9,24,128]{2,1,0:T(8,128)S(1)}) custom-call(f32[9,56,128]{2,1,0:T(8,128)S(1)} %get-tuple-element.105.refs_0_.refs_13_, f32[9,9,3,128]{3,2,1,0:T(4,128)S(1)} %get-tuple-element.75.s_ref.refs_1_, ...), custom_call_target="tpu_custom_call" | custom-call | flops 50000000 | bytes 8388608 | tf_op jit(solution)/shard_map/local/pallas_call | solution.py:455
  30.9 0.0 collective-permute-done.4.refs_0_
  30.9 3.4 %collective-permute-done.5.refs_1_ = f32[56,128]{1,0:T(8,128)S(1)} collective-permute-done((f32[56,128]{1,0:T(8,128)S(1)}, f32[56,128]{1,0:T(8,128)S(1)}, u32[]{:S(2)}, u32[]{:S(2)}) %collective-permute-start.5) | collective-permute-done | bytes 28704 | tf_op jit(solution)/shard_map/ppermute | solution.py:493
  34.4 1.4 %collective-permute-done.6.refs_2_ = f32[56,128]{1,0:T(8,128)S(1)} collective-permute-done((f32[56,128]{1,0:T(8,128)S(1)}, f32[56,128]{1,0:T(8,128)S(1)}, u32[]{:S(2)}, u32[]{:S(2)}) %collective-permute-start.6) | collective-permute-done | bytes 28704 | tf_op jit(solution)/shard_map/ppermute | solution.py:493
  35.8 0.0 collective-permute-done.7.refs_3_
  35.8 3.7 %join.4 = (f32[9,56,128]{2,1,0:T(8,128)S(1)}, f32[9,56,128]{2,1,0:T(8,128)S(1)}, f32[5,56,128]{2,1,0:T(8,128)S(1)}, f32[56,128]{1,0:T(8,128)S(1)}, f32[56,128]{1...) custom-call(f32[56,128]{1,0:T(8,128)S(1)} %collective-permute-done.4.refs_0_, ...), custom_call_target="tpu_custom_call" | custom-call | flops 50000000 | bytes 4194304 | tf_op jit(solution)/shard_map/join/pallas_call | solution.py:455
  39.5 0.1 collective-permute-start.8
  39.6 1.4 %collective-permute-start.9 = (f32[56,128]{1,0:T(8,128)S(1)}, f32[56,128]{1,0:T(8,128)S(1)}, u32[]{:S(2)}, u32[]{:S(2)}) collective-permute-start(f32[56,128]{1,0:T(8,128)S(1)} %get-tuple-element.113), channel_id=1, source_target_pairs={{0,1},{1,0},{2,4},{3,5},{4,2},{5,3},{6,8},{7,9},{8,6},{9,7},{10,12... | collective-permute-start | bytes 86024 | tf_op jit(solution)/shard_map/ppermute | solution.py:493
  41.0 0.9 %collective-permute-start.10 = (f32[56,128]{1,0:T(8,128)S(1)}, f32[56,128]{1,0:T(8,128)S(1)}, u32[]{:S(2)}, u32[]{:S(2)}) collective-permute-start(f32[56,128]{1,0:T(8,128)S(1)} %get-tuple-element.114), channel_id=1, source_target_pairs={{0,255},{1,2},{2,1},{3,4},{4,3},{5,6},{6,5},{7,8},{8,7},{9,10},{10... | collective-permute-start | bytes 86024 | tf_op jit(solution)/shard_map/ppermute | solution.py:493
  41.9 0.0 collective-permute-start.11
  41.9 2.4 %local.6 = (f32[9,56,128]{2,1,0:T(8,128)S(1)}, f32[9,56,128]{2,1,0:T(8,128)S(1)}, f32[9,56,128]{2,1,0:T(8,128)S(1)}, f32[9,24,128]{2,1,0:T(8,128)S(1)}) custom-call(f32[9,56,128]{2,1,0:T(8,128)S(1)} %get-tuple-element.116.refs_0_.refs_13_, f32[9,9,3,128]{3,2,1,0:T(4,128)S(1)} %get-tuple-element.75.s_ref.refs_1_, ...), custom_call_target="tpu_custom_call" | custom-call | flops 50000000 | bytes 8388608 | tf_op jit(solution)/shard_map/local/pallas_call | solution.py:455
  44.3 0.0 collective-permute-done.8.refs_0_
  44.3 3.5 %collective-permute-done.9.refs_1_ = f32[56,128]{1,0:T(8,128)S(1)} collective-permute-done((f32[56,128]{1,0:T(8,128)S(1)}, f32[56,128]{1,0:T(8,128)S(1)}, u32[]{:S(2)}, u32[]{:S(2)}) %collective-permute-start.9) | collective-permute-done | bytes 28704 | tf_op jit(solution)/shard_map/ppermute | solution.py:493
  47.8 0.7 %collective-permute-done.10.refs_2_ = f32[56,128]{1,0:T(8,128)S(1)} collective-permute-done((f32[56,128]{1,0:T(8,128)S(1)}, f32[56,128]{1,0:T(8,128)S(1)}, u32[]{:S(2)}, u32[]{:S(2)}) %collective-permute-start.10) | collective-permute-done | bytes 28704 | tf_op jit(solution)/shard_map/ppermute | solution.py:493
  48.5 0.0 collective-permute-done.11.refs_3_
  48.5 3.7 %join.5 = (f32[9,56,128]{2,1,0:T(8,128)S(1)}, f32[9,56,128]{2,1,0:T(8,128)S(1)}, f32[5,56,128]{2,1,0:T(8,128)S(1)}, f32[56,128]{1,0:T(8,128)S(1)}, f32[56,128]{1...) custom-call(f32[56,128]{1,0:T(8,128)S(1)} %collective-permute-done.8.refs_0_, ...), custom_call_target="tpu_custom_call" | custom-call | flops 50000000 | bytes 4194304 | tf_op jit(solution)/shard_map/join/pallas_call | solution.py:455
  52.2 0.1 collective-permute-start.12
  52.3 2.0 %collective-permute-start.13 = (f32[56,128]{1,0:T(8,128)S(1)}, f32[56,128]{1,0:T(8,128)S(1)}, u32[]{:S(2)}, u32[]{:S(2)}) collective-permute-start(f32[56,128]{1,0:T(8,128)S(1)} %get-tuple-element.124), channel_id=1, source_target_pairs={{0,1},{1,0},{2,4},{3,5},{4,2},{5,3},{6,8},{7,9},{8,6},{9,7},{10,12... | collective-permute-start | bytes 86024 | tf_op jit(solution)/shard_map/ppermute | solution.py:493
  54.3 1.0 %collective-permute-start.14 = (f32[56,128]{1,0:T(8,128)S(1)}, f32[56,128]{1,0:T(8,128)S(1)}, u32[]{:S(2)}, u32[]{:S(2)}) collective-permute-start(f32[56,128]{1,0:T(8,128)S(1)} %get-tuple-element.125), channel_id=1, source_target_pairs={{0,255},{1,2},{2,1},{3,4},{4,3},{5,6},{6,5},{7,8},{8,7},{9,10},{10... | collective-permute-start | bytes 86024 | tf_op jit(solution)/shard_map/ppermute | solution.py:493
  55.3 0.0 collective-permute-start.15
  55.3 1.3 %coarse_own.1.refs_11_ = f32[9,56,128]{2,1,0:T(8,128)S(1)} custom-call(f32[6,9,56,128]{3,2,1,0:T(8,128)S(1)} %get-tuple-element.83.refs_11_.series, f32[9,9,3,128]{3,2,1,0:T(4,128)S(1)} %get-tuple-element.75.s_ref.refs_1_, bf16[112,168]{1,0:T(8,128)(2,1)S(1)} %get-tuple-element.84.refs_2_.refs_15_.w2, ...), custom_call_target="tpu_custom_call" | custom-call | flops 50000000 | bytes 8388608 | tf_op jit(solution)/shard_map/coarse_own/pallas_call | solution.py:455
  56.6 2.1 %local.7 = (f32[9,56,128]{2,1,0:T(8,128)S(1)}, f32[9,56,128]{2,1,0:T(8,128)S(1)}) custom-call(f32[9,56,128]{2,1,0:T(8,128)S(1)} %get-tuple-element.127.refs_0_, f32[9,9,3,128]{3,2,1,0:T(4,128)S(1)} %get-tuple-element.75.s_ref.refs_1_, bf16[112,168]{1,0:T(8,128)(2,1)S(1)} %get-tuple-element.84.refs_2_.refs_15_.w2, ...), custom_call_target="tpu_custom_call" | custom-call | flops 50000000 | bytes 8388608 | tf_op jit(solution)/shard_map/local/pallas_call | solution.py:455
  58.7 0.0 collective-permute-done.12.refs_0_
  58.7 1.8 %collective-permute-done.13.refs_1_ = f32[56,128]{1,0:T(8,128)S(1)} collective-permute-done((f32[56,128]{1,0:T(8,128)S(1)}, f32[56,128]{1,0:T(8,128)S(1)}, u32[]{:S(2)}, u32[]{:S(2)}) %collective-permute-start.13) | collective-permute-done | bytes 28704 | tf_op jit(solution)/shard_map/ppermute | solution.py:493
  60.5 1.4 %collective-permute-done.14.refs_2_ = f32[56,128]{1,0:T(8,128)S(1)} collective-permute-done((f32[56,128]{1,0:T(8,128)S(1)}, f32[56,128]{1,0:T(8,128)S(1)}, u32[]{:S(2)}, u32[]{:S(2)}) %collective-permute-start.14) | collective-permute-done | bytes 28704 | tf_op jit(solution)/shard_map/ppermute | solution.py:493
  61.9 0.0 collective-permute-done.15.refs_3_
  61.9 1.4 %last.1 = f32[9,56,128]{2,1,0:T(8,128)} custom-call(f32[56,128]{1,0:T(8,128)S(1)} %collective-permute-done.12.refs_0_, f32[56,128]{1,0:T(8,128)S(1)} %collective-permute-done.13.refs_1_, f32[56,128]{1,0:T(8,128)S(1)} %collective-permute-done.14.refs_2_, f32[56,128]{1,0:T(8,128)S(1)} %collective-permute-done.15.refs_3_, ...), custom_call_target="tpu_custom_call" | custom-call | flops 50000000 | bytes 4194304 | tf_op jit(solution)/shard_map/last/pallas_call | solution.py:455
  (1 shorter events, 0.0 us)
Async XLA Ops:
  5.5 12.3 %collective-permute-start = (f32[56,128]{1,0:T(8,128)S(1)}, f32[56,128]{1,0:T(8,128)S(1)}, u32[]{:S(2)}, u32[]{:S(2)}) collective-permute-start(f32[56,128]{1,0:T(8,128)S(1)} %get-tuple-element.69), channel_id=1, source_target_pairs={{0,2},{1,3},{2,0},{3,1},{4,6},{5,7},{6,4},{7,5},{8,10},{9,11},{10,... | collective-permute-start | bytes 86024 | tf_op jit(solution)/shard_map/ppermute | solution.py:493
  7.1 10.7 %collective-permute-start.1 = (f32[56,128]{1,0:T(8,128)S(1)}, f32[56,128]{1,0:T(8,128)S(1)}, u32[]{:S(2)}, u32[]{:S(2)}) collective-permute-start(f32[56,128]{1,0:T(8,128)S(1)} %get-tuple-element.70), channel_id=1, source_target_pairs={{0,1},{1,0},{2,4},{3,5},{4,2},{5,3},{6,8},{7,9},{8,6},{9,7},{10,12... | collective-permute-start | bytes 86024 | tf_op jit(solution)/shard_map/ppermute | solution.py:493
  14.7 7.5 %collective-permute-start.2 = (f32[56,128]{1,0:T(8,128)S(1)}, f32[56,128]{1,0:T(8,128)S(1)}, u32[]{:S(2)}, u32[]{:S(2)}) collective-permute-start(f32[56,128]{1,0:T(8,128)S(1)} %get-tuple-element.71), channel_id=1, source_target_pairs={{0,255},{1,2},{2,1},{3,4},{4,3},{5,6},{6,5},{7,8},{8,7},{9,10},{10... | collective-permute-start | bytes 86024 | tf_op jit(solution)/shard_map/ppermute | solution.py:493
  14.7 7.5 %collective-permute-start.3 = (f32[56,128]{1,0:T(8,128)S(1)}, f32[56,128]{1,0:T(8,128)S(1)}, u32[]{:S(2)}, u32[]{:S(2)}) collective-permute-start(f32[56,128]{1,0:T(8,128)S(1)} %get-tuple-element.72), channel_id=1, source_target_pairs={{0,1},{1,0},{2,3},{3,2},{4,5},{5,4},{6,7},{7,6},{8,9},{9,8},{10,11... | collective-permute-start | bytes 86024 | tf_op jit(solution)/shard_map/ppermute | solution.py:493
  25.9 5.0 %collective-permute-start.4 = (f32[56,128]{1,0:T(8,128)S(1)}, f32[56,128]{1,0:T(8,128)S(1)}, u32[]{:S(2)}, u32[]{:S(2)}) collective-permute-start(f32[56,128]{1,0:T(8,128)S(1)} %get-tuple-element.101), channel_id=1, source_target_pairs={{0,2},{1,3},{2,0},{3,1},{4,6},{5,7},{6,4},{7,5},{8,10},{9,11},{10,... | collective-permute-start | bytes 86024 | tf_op jit(solution)/shard_map/ppermute | solution.py:493
  26.2 8.2 %collective-permute-start.5 = (f32[56,128]{1,0:T(8,128)S(1)}, f32[56,128]{1,0:T(8,128)S(1)}, u32[]{:S(2)}, u32[]{:S(2)}) collective-permute-start(f32[56,128]{1,0:T(8,128)S(1)} %get-tuple-element.102), channel_id=1, source_target_pairs={{0,1},{1,0},{2,4},{3,5},{4,2},{5,3},{6,8},{7,9},{8,6},{9,7},{10,12... | collective-permute-start | bytes 86024 | tf_op jit(solution)/shard_map/ppermute | solution.py:493
  28.3 7.5 %collective-permute-start.6 = (f32[56,128]{1,0:T(8,128)S(1)}, f32[56,128]{1,0:T(8,128)S(1)}, u32[]{:S(2)}, u32[]{:S(2)}) collective-permute-start(f32[56,128]{1,0:T(8,128)S(1)} %get-tuple-element.103), channel_id=1, source_target_pairs={{0,255},{1,2},{2,1},{3,4},{4,3},{5,6},{6,5},{7,8},{8,7},{9,10},{10... | collective-permute-start | bytes 86024 | tf_op jit(solution)/shard_map/ppermute | solution.py:493
  28.5 7.3 %collective-permute-start.7 = (f32[56,128]{1,0:T(8,128)S(1)}, f32[56,128]{1,0:T(8,128)S(1)}, u32[]{:S(2)}, u32[]{:S(2)}) collective-permute-start(f32[56,128]{1,0:T(8,128)S(1)} %get-tuple-element.104.after), channel_id=1, source_target_pairs={{0,1},{1,0},{2,3},{3,2},{4,5},{5,4},{6,7},{7,6},{8,9},{9,8},{10,11... | collective-permute-start | bytes 86024 | tf_op jit(solution)/shard_map/ppermute | solution.py:493
  39.5 4.8 %collective-permute-start.8 = (f32[56,128]{1,0:T(8,128)S(1)}, f32[56,128]{1,0:T(8,128)S(1)}, u32[]{:S(2)}, u32[]{:S(2)}) collective-permute-start(f32[56,128]{1,0:T(8,128)S(1)} %get-tuple-element.112), channel_id=1, source_target_pairs={{0,2},{1,3},{2,0},{3,1},{4,6},{5,7},{6,4},{7,5},{8,10},{9,11},{10,... | collective-permute-start | bytes 86024 | tf_op jit(solution)/shard_map/ppermute | solution.py:493
  39.6 8.2 %collective-permute-start.9 = (f32[56,128]{1,0:T(8,128)S(1)}, f32[56,128]{1,0:T(8,128)S(1)}, u32[]{:S(2)}, u32[]{:S(2)}) collective-permute-start(f32[56,128]{1,0:T(8,128)S(1)} %get-tuple-element.113), channel_id=1, source_target_pairs={{0,1},{1,0},{2,4},{3,5},{4,2},{5,3},{6,8},{7,9},{8,6},{9,7},{10,12... | collective-permute-start | bytes 86024 | tf_op jit(solution)/shard_map/ppermute | solution.py:493
  41.0 7.5 %collective-permute-start.10 = (f32[56,128]{1,0:T(8,128)S(1)}, f32[56,128]{1,0:T(8,128)S(1)}, u32[]{:S(2)}, u32[]{:S(2)}) collective-permute-start(f32[56,128]{1,0:T(8,128)S(1)} %get-tuple-element.114), channel_id=1, source_target_pairs={{0,255},{1,2},{2,1},{3,4},{4,3},{5,6},{6,5},{7,8},{8,7},{9,10},{10... | collective-permute-start | bytes 86024 | tf_op jit(solution)/shard_map/ppermute | solution.py:493
  41.9 6.6 %collective-permute-start.11 = (f32[56,128]{1,0:T(8,128)S(1)}, f32[56,128]{1,0:T(8,128)S(1)}, u32[]{:S(2)}, u32[]{:S(2)}) collective-permute-start(f32[56,128]{1,0:T(8,128)S(1)} %get-tuple-element.115), channel_id=1, source_target_pairs={{0,1},{1,0},{2,3},{3,2},{4,5},{5,4},{6,7},{7,6},{8,9},{9,8},{10,11... | collective-permute-start | bytes 86024 | tf_op jit(solution)/shard_map/ppermute | solution.py:493
  52.2 6.5 %collective-permute-start.12 = (f32[56,128]{1,0:T(8,128)S(1)}, f32[56,128]{1,0:T(8,128)S(1)}, u32[]{:S(2)}, u32[]{:S(2)}) collective-permute-start(f32[56,128]{1,0:T(8,128)S(1)} %get-tuple-element.123), channel_id=1, source_target_pairs={{0,2},{1,3},{2,0},{3,1},{4,6},{5,7},{6,4},{7,5},{8,10},{9,11},{10,... | collective-permute-start | bytes 86024 | tf_op jit(solution)/shard_map/ppermute | solution.py:493
  52.3 8.2 %collective-permute-start.13 = (f32[56,128]{1,0:T(8,128)S(1)}, f32[56,128]{1,0:T(8,128)S(1)}, u32[]{:S(2)}, u32[]{:S(2)}) collective-permute-start(f32[56,128]{1,0:T(8,128)S(1)} %get-tuple-element.124), channel_id=1, source_target_pairs={{0,1},{1,0},{2,4},{3,5},{4,2},{5,3},{6,8},{7,9},{8,6},{9,7},{10,12... | collective-permute-start | bytes 86024 | tf_op jit(solution)/shard_map/ppermute | solution.py:493
  54.3 7.5 %collective-permute-start.14 = (f32[56,128]{1,0:T(8,128)S(1)}, f32[56,128]{1,0:T(8,128)S(1)}, u32[]{:S(2)}, u32[]{:S(2)}) collective-permute-start(f32[56,128]{1,0:T(8,128)S(1)} %get-tuple-element.125), channel_id=1, source_target_pairs={{0,255},{1,2},{2,1},{3,4},{4,3},{5,6},{6,5},{7,8},{8,7},{9,10},{10... | collective-permute-start | bytes 86024 | tf_op jit(solution)/shard_map/ppermute | solution.py:493
  55.3 6.6 %collective-permute-start.15 = (f32[56,128]{1,0:T(8,128)S(1)}, f32[56,128]{1,0:T(8,128)S(1)}, u32[]{:S(2)}, u32[]{:S(2)}) collective-permute-start(f32[56,128]{1,0:T(8,128)S(1)} %get-tuple-element.126), channel_id=1, source_target_pairs={{0,1},{1,0},{2,3},{3,2},{4,5},{5,4},{6,7},{7,6},{8,9},{9,8},{10,11... | collective-permute-start | bytes 86024 | tf_op jit(solution)/shard_map/ppermute | solution.py:493

commit v5 on v3

--- a/solution.py
+++ b/solution.py
@@ -335,7 +335,7 @@
 
 
 def join_kernel(last, *refs):
-    (g2, g3, g1, g0, q_ref, u_ref, nl_ref, nacc_ref, fp_ref, lr2, nb_ref, or_ref, coh, fine_ref,
+    (g3, g2, g1, g0, q_ref, u_ref, nl_ref, nacc_ref, fp_ref, lr2, nb_ref, or_ref, coh, fine_ref,
      pack_ref, w2, p2, piece, se, sf, order_ref, spot_ref) = refs[:22]
     table = unpack((g0, g1, g2, g3))
     masks = orient_masks(or_ref)
@@ -474,7 +474,7 @@
             coarse = call(
                 coarse_kernel, "coarse_own", [(BIG, F32)], [(BIG, F32), (TAB, F32)],
                 [series, s_mat, w2, p2, fm, l2, outs[4]], 8)[0]
-        common = [got[2], got[3], got[1], got[0], state, u, near, total if total is not None else near, fp, lr2, nb, turn_code,
+        common = [got[3], got[2], got[1], got[0], state, u, near, total if total is not None else near, fp, lr2, nb, turn_code,
                   coh, fine, pack, w2, p2]
         if last:
             out = call(

time: 62.9 us -> 62 us (0.986)
  waiting for transfers between devices: 19.1 us -> 13.9 us
  starting transfers between devices: 16.6 us -> 20.8 us
    ppermute x16, waiting for transfers between devices: 19.1 us -> 13.9 us  [exchange(): got[k] = lax.ppermute(messages[k], 'dom', pairings[k])]
    ppermute x16, starting transfers between devices: 16.6 us -> 20.8 us  [exchange(): got[k] = lax.ppermute(messages[k], 'dom', pairings[k])]
  transfers between devices with their start and end apart: 16 -> 16, of which waited for: 8 -> 7; matrix products, arithmetic and copies ran while one was open for 0% -> 0% of each run, Pallas kernels for 12% -> 12%
where the time goes in v5:
time: 62 us; the launch traced here: 61.9 us
  Pallas kernels  27 us (44%)
  starting transfers between devices  20.8 us (34%)
  waiting for transfers between devices  13.9 us (22%)
    pallas_call x11, Pallas kernels, call(): pl.pallas_call(kernel, name=name, out_shape=[jax.ShapeDtypeStruct(s, d) f...  27 us
    ppermute x16, starting transfers between devices, exchange(): got[k] = lax.ppermute(messages[k], 'dom', pairings[k])  20.8 us
    ppermute x16, waiting for transfers between devices, exchange(): got[k] = lax.ppermute(messages[k], 'dom', pairings[k])  13.9 us
  transfers between devices with their start and end apart: 16, of which 7 were waited for; matrix products, arithmetic and copies ran while one was open for 0% of the time, Pallas kernels for 12%

profile of v5, /device:TPU:24, one launch (start us, length us, event | category | flops | bytes accessed | tf_op | source)
XLA Modules:
  0.0 61.9 jit_solution(11450456262183690763)
XLA Ops:
  0.0 5.5 %first.1 = (f32[9,9,3,128]{3,2,1,0:T(4,128)S(1)}, bf16[112,168]{1,0:T(8,128)(2,1)S(1)}, bf16[192,56]{1,0:T(8,128)(2,1)S(1)}, f32[6,9,56,128]{3,2,1,0:T(8,128)S(1...) custom-call(f32[9,56,128]{2,1,0:T(8,128)} %bitcast.11, ...), custom_call_target="tpu_custom_call" | custom-call | flops 50000000 | bytes 4194304 | tf_op jit(solution)/shard_map/first/pallas_call | solution.py:398
  5.5 8.3 %collective-permute-start = (f32[56,128]{1,0:T(8,128)S(1)}, f32[56,128]{1,0:T(8,128)S(1)}, u32[]{:S(2)}, u32[]{:S(2)}) collective-permute-start(f32[56,128]{1,0:T(8,128)S(1)} %get-tuple-element.66), channel_id=1, source_target_pairs={{0,1},{1,0},{2,4},{3,5},{4,2},{5,3},{6,8},{7,9},{8,6},{9,7},{10,12... | collective-permute-start | bytes 86024 | tf_op jit(solution)/shard_map/ppermute | solution.py:436
  13.9 0.0 collective-permute-start.1
  13.9 0.2 collective-permute-start.2
  14.1 1.9 %collective-permute-start.3 = (f32[56,128]{1,0:T(8,128)S(1)}, f32[56,128]{1,0:T(8,128)S(1)}, u32[]{:S(2)}, u32[]{:S(2)}) collective-permute-start(f32[56,128]{1,0:T(8,128)S(1)} %get-tuple-element.69), channel_id=1, source_target_pairs={{0,1},{1,0},{2,3},{3,2},{4,5},{5,4},{6,7},{7,6},{8,9},{9,8},{10,11... | collective-permute-start | bytes 86024 | tf_op jit(solution)/shard_map/ppermute | solution.py:436
  16.0 0.8 %lifts.1 = (bf16[112,96]{1,0:T(8,128)(2,1)S(1)}, bf16[112,288]{1,0:T(8,128)(2,1)S(1)}, s32[8,128]{1,0:T(8,128)S(1)}, s32[2,8,128]{2,1,0:T(8,128)S(1)}, f32[5,10,3,128]{3,2,1,0:T(4,128)S(1)}) custom-call(f32[21,4,56]{2,1,0:T(4,128)S(1)} %get-tuple-element.76.lift, f32[3,21,21]{2,1,0:T(8,128)S(1)} %get-tuple-element.77.rotate, ...), custom_call_target="tpu_custom_call" | custom-call | flops 50000000 | bytes 4194304 | tf_op jit(solution)/shard_map/lifts/pallas_call | solution.py:398
  16.8 1.4 %local.4 = (f32[9,56,128]{2,1,0:T(8,128)S(1)}, f32[9,96,128]{2,1,0:T(8,128)S(1)}, f32[9,56,128]{2,1,0:T(8,128)S(1)}) custom-call(f32[9,56,128]{2,1,0:T(8,128)S(1)} %slice_bitcast_fusion.q_ref.refs_4_, f32[9,56,128]{2,1,0:T(8,128)S(1)} %get-tuple-element.71.pred, f32[9,96,128]{2,1,0:T(8,128)S(1)} %get-tuple-element.72.t_ref, ...), custom_call_target="tpu_custom_call" | custom-call | flops 50000000 | bytes 4194304 | tf_op jit(solution)/shard_map/local/pallas_call | solution.py:398
  18.2 0.0 collective-permute-done.refs_0_
  18.2 0.0 collective-permute-done.1.refs_1_
  18.2 3.2 %collective-permute-done.2.refs_2_ = f32[56,128]{1,0:T(8,128)S(1)} collective-permute-done((f32[56,128]{1,0:T(8,128)S(1)}, f32[56,128]{1,0:T(8,128)S(1)}, u32[]{:S(2)}, u32[]{:S(2)}) %collective-permute-start.2) | collective-permute-done | bytes 28704 | tf_op jit(solution)/shard_map/ppermute | solution.py:436
  21.4 0.0 collective-permute-done.3.refs_3_
  21.4 4.1 %join.3 = (f32[9,56,128]{2,1,0:T(8,128)S(1)}, f32[9,96,128]{2,1,0:T(8,128)S(1)}, f32[9,56,128]{2,1,0:T(8,128)S(1)}, f32[9,96,128]{2,1,0:T(8,128)S(1)}, f32[56,12...) custom-call(f32[56,128]{1,0:T(8,128)S(1)} %collective-permute-done.refs_0_, ...), custom_call_target="tpu_custom_call" | custom-call | flops 50000000 | bytes 4194304 | tf_op jit(solution)/shard_map/join/pallas_call | solution.py:398
  25.5 1.1 %collective-permute-start.4 = (f32[56,128]{1,0:T(8,128)S(1)}, f32[56,128]{1,0:T(8,128)S(1)}, u32[]{:S(2)}, u32[]{:S(2)}) collective-permute-start(f32[56,128]{1,0:T(8,128)S(1)} %get-tuple-element.95), channel_id=1, source_target_pairs={{0,1},{1,0},{2,4},{3,5},{4,2},{5,3},{6,8},{7,9},{8,6},{9,7},{10,12... | collective-permute-start | bytes 86024 | tf_op jit(solution)/shard_map/ppermute | solution.py:436
  26.6 0.0 collective-permute-start.5
  26.6 1.4 %collective-permute-start.6 = (f32[56,128]{1,0:T(8,128)S(1)}, f32[56,128]{1,0:T(8,128)S(1)}, u32[]{:S(2)}, u32[]{:S(2)}) collective-permute-start(f32[56,128]{1,0:T(8,128)S(1)} %get-tuple-element.97), channel_id=1, source_target_pairs={{0,255},{1,2},{2,1},{3,4},{4,3},{5,6},{6,5},{7,8},{8,7},{9,10},{10... | collective-permute-start | bytes 86024 | tf_op jit(solution)/shard_map/ppermute | solution.py:436
  28.0 0.8 %collective-permute-start.7 = (f32[56,128]{1,0:T(8,128)S(1)}, f32[56,128]{1,0:T(8,128)S(1)}, u32[]{:S(2)}, u32[]{:S(2)}) collective-permute-start(f32[56,128]{1,0:T(8,128)S(1)} %get-tuple-element.98.after), channel_id=1, source_target_pairs={{0,1},{1,0},{2,3},{3,2},{4,5},{5,4},{6,7},{7,6},{8,9},{9,8},{10,11... | collective-permute-start | bytes 86024 | tf_op jit(solution)/shard_map/ppermute | solution.py:436
  28.8 1.4 %local.5 = (f32[9,56,128]{2,1,0:T(8,128)S(1)}, f32[9,96,128]{2,1,0:T(8,128)S(1)}, f32[9,56,128]{2,1,0:T(8,128)S(1)}) custom-call(f32[9,56,128]{2,1,0:T(8,128)S(1)} %get-tuple-element.99.q_ref.refs_4_, f32[9,56,128]{2,1,0:T(8,128)S(1)} %get-tuple-element.100.pred, f32[9,96,128]{2,1,0:T(8,128)S(1)} %get-tuple-element.101.t_ref, ...), custom_call_target="tpu_custom_call" | custom-call | flops 50000000 | bytes 4194304 | tf_op jit(solution)/shard_map/local/pallas_call | solution.py:398
  30.1 3.5 %collective-permute-done.4.refs_0_ = f32[56,128]{1,0:T(8,128)S(1)} collective-permute-done((f32[56,128]{1,0:T(8,128)S(1)}, f32[56,128]{1,0:T(8,128)S(1)}, u32[]{:S(2)}, u32[]{:S(2)}) %collective-permute-start.4) | collective-permute-done | bytes 28704 | tf_op jit(solution)/shard_map/ppermute | solution.py:436
  33.7 0.0 collective-permute-done.5.refs_1_
  33.7 0.5 collective-permute-done.6.refs_2_
  34.2 0.0 collective-permute-done.7.refs_3_
  34.2 4.1 %join.4 = (f32[9,56,128]{2,1,0:T(8,128)S(1)}, f32[9,96,128]{2,1,0:T(8,128)S(1)}, f32[9,56,128]{2,1,0:T(8,128)S(1)}, f32[9,96,128]{2,1,0:T(8,128)S(1)}, f32[56,12...) custom-call(f32[56,128]{1,0:T(8,128)S(1)} %collective-permute-done.4.refs_0_, ...), custom_call_target="tpu_custom_call" | custom-call | flops 50000000 | bytes 4194304 | tf_op jit(solution)/shard_map/join/pallas_call | solution.py:398
  38.3 1.6 %collective-permute-start.8 = (f32[56,128]{1,0:T(8,128)S(1)}, f32[56,128]{1,0:T(8,128)S(1)}, u32[]{:S(2)}, u32[]{:S(2)}) collective-permute-start(f32[56,128]{1,0:T(8,128)S(1)} %get-tuple-element.106), channel_id=1, source_target_pairs={{0,1},{1,0},{2,4},{3,5},{4,2},{5,3},{6,8},{7,9},{8,6},{9,7},{10,12... | collective-permute-start | bytes 86024 | tf_op jit(solution)/shard_map/ppermute | solution.py:436
  39.9 0.0 collective-permute-start.9
  39.9 0.9 %collective-permute-start.10 = (f32[56,128]{1,0:T(8,128)S(1)}, f32[56,128]{1,0:T(8,128)S(1)}, u32[]{:S(2)}, u32[]{:S(2)}) collective-permute-start(f32[56,128]{1,0:T(8,128)S(1)} %get-tuple-element.108), channel_id=1, source_target_pairs={{0,255},{1,2},{2,1},{3,4},{4,3},{5,6},{6,5},{7,8},{8,7},{9,10},{10... | collective-permute-start | bytes 86024 | tf_op jit(solution)/shard_map/ppermute | solution.py:436
  40.8 1.3 %collective-permute-start.11 = (f32[56,128]{1,0:T(8,128)S(1)}, f32[56,128]{1,0:T(8,128)S(1)}, u32[]{:S(2)}, u32[]{:S(2)}) collective-permute-start(f32[56,128]{1,0:T(8,128)S(1)} %get-tuple-element.109), channel_id=1, source_target_pairs={{0,1},{1,0},{2,3},{3,2},{4,5},{5,4},{6,7},{7,6},{8,9},{9,8},{10,11... | collective-permute-start | bytes 86024 | tf_op jit(solution)/shard_map/ppermute | solution.py:436
  42.0 1.4 %local.6 = (f32[9,56,128]{2,1,0:T(8,128)S(1)}, f32[9,96,128]{2,1,0:T(8,128)S(1)}, f32[9,56,128]{2,1,0:T(8,128)S(1)}) custom-call(f32[9,56,128]{2,1,0:T(8,128)S(1)} %get-tuple-element.110.q_ref.refs_4_, f32[9,56,128]{2,1,0:T(8,128)S(1)} %get-tuple-element.111.pred, f32[9,96,128]{2,1,0:T(8,128)S(1)} %get-tuple-element.112.t_ref, ...), custom_call_target="tpu_custom_call" | custom-call | flops 50000000 | bytes 4194304 | tf_op jit(solution)/shard_map/local/pallas_call | solution.py:398
  43.5 3.0 %collective-permute-done.8.refs_0_ = f32[56,128]{1,0:T(8,128)S(1)} collective-permute-done((f32[56,128]{1,0:T(8,128)S(1)}, f32[56,128]{1,0:T(8,128)S(1)}, u32[]{:S(2)}, u32[]{:S(2)}) %collective-permute-start.8) | collective-permute-done | bytes 28704 | tf_op jit(solution)/shard_map/ppermute | solution.py:436
  46.4 0.0 collective-permute-done.9.refs_1_
  46.4 1.0 %collective-permute-done.10.refs_2_ = f32[56,128]{1,0:T(8,128)S(1)} collective-permute-done((f32[56,128]{1,0:T(8,128)S(1)}, f32[56,128]{1,0:T(8,128)S(1)}, u32[]{:S(2)}, u32[]{:S(2)}) %collective-permute-start.10) | collective-permute-done | bytes 28704 | tf_op jit(solution)/shard_map/ppermute | solution.py:436
  47.4 0.0 collective-permute-done.11.refs_3_
  47.4 4.1 %join.5 = (f32[9,56,128]{2,1,0:T(8,128)S(1)}, f32[9,96,128]{2,1,0:T(8,128)S(1)}, f32[9,56,128]{2,1,0:T(8,128)S(1)}, f32[9,96,128]{2,1,0:T(8,128)S(1)}, f32[56,12...) custom-call(f32[56,128]{1,0:T(8,128)S(1)} %collective-permute-done.8.refs_0_, ...), custom_call_target="tpu_custom_call" | custom-call | flops 50000000 | bytes 4194304 | tf_op jit(solution)/shard_map/join/pallas_call | solution.py:398
  51.5 1.1 %collective-permute-start.12 = (f32[56,128]{1,0:T(8,128)S(1)}, f32[56,128]{1,0:T(8,128)S(1)}, u32[]{:S(2)}, u32[]{:S(2)}) collective-permute-start(f32[56,128]{1,0:T(8,128)S(1)} %get-tuple-element.117), channel_id=1, source_target_pairs={{0,1},{1,0},{2,4},{3,5},{4,2},{5,3},{6,8},{7,9},{8,6},{9,7},{10,12... | collective-permute-start | bytes 86024 | tf_op jit(solution)/shard_map/ppermute | solution.py:436
  52.7 0.0 collective-permute-start.13
  52.7 1.0 %collective-permute-start.14 = (f32[56,128]{1,0:T(8,128)S(1)}, f32[56,128]{1,0:T(8,128)S(1)}, u32[]{:S(2)}, u32[]{:S(2)}) collective-permute-start(f32[56,128]{1,0:T(8,128)S(1)} %get-tuple-element.119), channel_id=1, source_target_pairs={{0,255},{1,2},{2,1},{3,4},{4,3},{5,6},{6,5},{7,8},{8,7},{9,10},{10... | collective-permute-start | bytes 86024 | tf_op jit(solution)/shard_map/ppermute | solution.py:436
  53.7 1.1 %collective-permute-start.15 = (f32[56,128]{1,0:T(8,128)S(1)}, f32[56,128]{1,0:T(8,128)S(1)}, u32[]{:S(2)}, u32[]{:S(2)}) collective-permute-start(f32[56,128]{1,0:T(8,128)S(1)} %get-tuple-element.120), channel_id=1, source_target_pairs={{0,1},{1,0},{2,3},{3,2},{4,5},{5,4},{6,7},{7,6},{8,9},{9,8},{10,11... | collective-permute-start | bytes 86024 | tf_op jit(solution)/shard_map/ppermute | solution.py:436
  54.8 1.2 %coarse_own.1.refs_22_ = f32[9,56,128]{2,1,0:T(8,128)S(1)} custom-call(f32[6,9,56,128]{3,2,1,0:T(8,128)S(1)} %get-tuple-element.70.series, f32[9,9,3,128]{3,2,1,0:T(4,128)S(1)} %get-tuple-element.73.s_ref, bf16[112,168]{1,0:T(8,128)(2,1)S(1)} %get-tuple-element.74.w2.refs_15_, bf16[192,56]{1,0:T(8,128)(2,1)S(1)} %get-tuple-element.89.refs_16_.p2, ...), custom_call_target="tpu_custom_call" | custom-call | flops 50000000 | bytes 8388608 | tf_op jit(solution)/shard_map/coarse_own/pallas_call | solution.py:398
  56.1 1.4 %local.7 = (f32[9,56,128]{2,1,0:T(8,128)S(1)}, f32[9,96,128]{2,1,0:T(8,128)S(1)}) custom-call(f32[9,56,128]{2,1,0:T(8,128)S(1)} %get-tuple-element.121.q_ref.refs_4_, f32[9,56,128]{2,1,0:T(8,128)S(1)} %get-tuple-element.122.pred, f32[9,96,128]{2,1,0:T(8,128)S(1)} %get-tuple-element.123.t_ref, f32[9,9,3,128]{3,2,1,0:T(4,128)S(1)} %get-tuple-element.73.s_ref, ...), custom_call_target="tpu_custom_call" | custom-call | flops 50000000 | bytes 4194304 | tf_op jit(solution)/shard_map/local/pallas_call | solution.py:398
  57.4 2.3 %collective-permute-done.12.refs_0_ = f32[56,128]{1,0:T(8,128)S(1)} collective-permute-done((f32[56,128]{1,0:T(8,128)S(1)}, f32[56,128]{1,0:T(8,128)S(1)}, u32[]{:S(2)}, u32[]{:S(2)}) %collective-permute-start.12) | collective-permute-done | bytes 28704 | tf_op jit(solution)/shard_map/ppermute | solution.py:436
  59.7 0.0 collective-permute-done.13.refs_1_
  59.7 0.5 collective-permute-done.14.refs_2_
  60.2 0.0 collective-permute-done.15.refs_3_
  60.2 1.7 %last.1 = f32[9,56,128]{2,1,0:T(8,128)} custom-call(f32[56,128]{1,0:T(8,128)S(1)} %collective-permute-done.12.refs_0_, f32[56,128]{1,0:T(8,128)S(1)} %collective-permute-done.13.refs_1_, f32[56,128]{1,0:T(8,128)S(1)} %collective-permute-done.14.refs_2_, f32[56,128]{1,0:T(8,128)S(1)} %collective-permute-done.15.refs_3_, ...), custom_call_target="tpu_custom_call" | custom-call | flops 50000000 | bytes 4194304 | tf_op jit(solution)/shard_map/last/pallas_call | solution.py:398
  (1 shorter events, 0.0 us)
Async XLA Ops:
  5.5 12.6 %collective-permute-start = (f32[56,128]{1,0:T(8,128)S(1)}, f32[56,128]{1,0:T(8,128)S(1)}, u32[]{:S(2)}, u32[]{:S(2)}) collective-permute-start(f32[56,128]{1,0:T(8,128)S(1)} %get-tuple-element.66), channel_id=1, source_target_pairs={{0,1},{1,0},{2,4},{3,5},{4,2},{5,3},{6,8},{7,9},{8,6},{9,7},{10,12... | collective-permute-start | bytes 86024 | tf_op jit(solution)/shard_map/ppermute | solution.py:436
  13.9 4.3 %collective-permute-start.1 = (f32[56,128]{1,0:T(8,128)S(1)}, f32[56,128]{1,0:T(8,128)S(1)}, u32[]{:S(2)}, u32[]{:S(2)}) collective-permute-start(f32[56,128]{1,0:T(8,128)S(1)} %get-tuple-element.67), channel_id=1, source_target_pairs={{0,2},{1,3},{2,0},{3,1},{4,6},{5,7},{6,4},{7,5},{8,10},{9,11},{10,... | collective-permute-start | bytes 86024 | tf_op jit(solution)/shard_map/ppermute | solution.py:436
  13.9 7.5 %collective-permute-start.2 = (f32[56,128]{1,0:T(8,128)S(1)}, f32[56,128]{1,0:T(8,128)S(1)}, u32[]{:S(2)}, u32[]{:S(2)}) collective-permute-start(f32[56,128]{1,0:T(8,128)S(1)} %get-tuple-element.68), channel_id=1, source_target_pairs={{0,255},{1,2},{2,1},{3,4},{4,3},{5,6},{6,5},{7,8},{8,7},{9,10},{10... | collective-permute-start | bytes 86024 | tf_op jit(solution)/shard_map/ppermute | solution.py:436
  14.1 7.3 %collective-permute-start.3 = (f32[56,128]{1,0:T(8,128)S(1)}, f32[56,128]{1,0:T(8,128)S(1)}, u32[]{:S(2)}, u32[]{:S(2)}) collective-permute-start(f32[56,128]{1,0:T(8,128)S(1)} %get-tuple-element.69), channel_id=1, source_target_pairs={{0,1},{1,0},{2,3},{3,2},{4,5},{5,4},{6,7},{7,6},{8,9},{9,8},{10,11... | collective-permute-start | bytes 86024 | tf_op jit(solution)/shard_map/ppermute | solution.py:436
  25.5 8.2 %collective-permute-start.4 = (f32[56,128]{1,0:T(8,128)S(1)}, f32[56,128]{1,0:T(8,128)S(1)}, u32[]{:S(2)}, u32[]{:S(2)}) collective-permute-start(f32[56,128]{1,0:T(8,128)S(1)} %get-tuple-element.95), channel_id=1, source_target_pairs={{0,1},{1,0},{2,4},{3,5},{4,2},{5,3},{6,8},{7,9},{8,6},{9,7},{10,12... | collective-permute-start | bytes 86024 | tf_op jit(solution)/shard_map/ppermute | solution.py:436
  26.6 7.0 %collective-permute-start.5 = (f32[56,128]{1,0:T(8,128)S(1)}, f32[56,128]{1,0:T(8,128)S(1)}, u32[]{:S(2)}, u32[]{:S(2)}) collective-permute-start(f32[56,128]{1,0:T(8,128)S(1)} %get-tuple-element.96), channel_id=1, source_target_pairs={{0,2},{1,3},{2,0},{3,1},{4,6},{5,7},{6,4},{7,5},{8,10},{9,11},{10,... | collective-permute-start | bytes 86024 | tf_op jit(solution)/shard_map/ppermute | solution.py:436
  26.6 7.5 %collective-permute-start.6 = (f32[56,128]{1,0:T(8,128)S(1)}, f32[56,128]{1,0:T(8,128)S(1)}, u32[]{:S(2)}, u32[]{:S(2)}) collective-permute-start(f32[56,128]{1,0:T(8,128)S(1)} %get-tuple-element.97), channel_id=1, source_target_pairs={{0,255},{1,2},{2,1},{3,4},{4,3},{5,6},{6,5},{7,8},{8,7},{9,10},{10... | collective-permute-start | bytes 86024 | tf_op jit(solution)/shard_map/ppermute | solution.py:436
  28.0 6.2 %collective-permute-start.7 = (f32[56,128]{1,0:T(8,128)S(1)}, f32[56,128]{1,0:T(8,128)S(1)}, u32[]{:S(2)}, u32[]{:S(2)}) collective-permute-start(f32[56,128]{1,0:T(8,128)S(1)} %get-tuple-element.98.after), channel_id=1, source_target_pairs={{0,1},{1,0},{2,3},{3,2},{4,5},{5,4},{6,7},{7,6},{8,9},{9,8},{10,11... | collective-permute-start | bytes 86024 | tf_op jit(solution)/shard_map/ppermute | solution.py:436
  38.3 8.2 %collective-permute-start.8 = (f32[56,128]{1,0:T(8,128)S(1)}, f32[56,128]{1,0:T(8,128)S(1)}, u32[]{:S(2)}, u32[]{:S(2)}) collective-permute-start(f32[56,128]{1,0:T(8,128)S(1)} %get-tuple-element.106), channel_id=1, source_target_pairs={{0,1},{1,0},{2,4},{3,5},{4,2},{5,3},{6,8},{7,9},{8,6},{9,7},{10,12... | collective-permute-start | bytes 86024 | tf_op jit(solution)/shard_map/ppermute | solution.py:436
  39.9 6.5 %collective-permute-start.9 = (f32[56,128]{1,0:T(8,128)S(1)}, f32[56,128]{1,0:T(8,128)S(1)}, u32[]{:S(2)}, u32[]{:S(2)}) collective-permute-start(f32[56,128]{1,0:T(8,128)S(1)} %get-tuple-element.107), channel_id=1, source_target_pairs={{0,2},{1,3},{2,0},{3,1},{4,6},{5,7},{6,4},{7,5},{8,10},{9,11},{10,... | collective-permute-start | bytes 86024 | tf_op jit(solution)/shard_map/ppermute | solution.py:436
  39.9 7.5 %collective-permute-start.10 = (f32[56,128]{1,0:T(8,128)S(1)}, f32[56,128]{1,0:T(8,128)S(1)}, u32[]{:S(2)}, u32[]{:S(2)}) collective-permute-start(f32[56,128]{1,0:T(8,128)S(1)} %get-tuple-element.108), channel_id=1, source_target_pairs={{0,255},{1,2},{2,1},{3,4},{4,3},{5,6},{6,5},{7,8},{8,7},{9,10},{10... | collective-permute-start | bytes 86024 | tf_op jit(solution)/shard_map/ppermute | solution.py:436
  40.8 6.6 %collective-permute-start.11 = (f32[56,128]{1,0:T(8,128)S(1)}, f32[56,128]{1,0:T(8,128)S(1)}, u32[]{:S(2)}, u32[]{:S(2)}) collective-permute-start(f32[56,128]{1,0:T(8,128)S(1)} %get-tuple-element.109), channel_id=1, source_target_pairs={{0,1},{1,0},{2,3},{3,2},{4,5},{5,4},{6,7},{7,6},{8,9},{9,8},{10,11... | collective-permute-start | bytes 86024 | tf_op jit(solution)/shard_map/ppermute | solution.py:436
  51.5 8.2 %collective-permute-start.12 = (f32[56,128]{1,0:T(8,128)S(1)}, f32[56,128]{1,0:T(8,128)S(1)}, u32[]{:S(2)}, u32[]{:S(2)}) collective-permute-start(f32[56,128]{1,0:T(8,128)S(1)} %get-tuple-element.117), channel_id=1, source_target_pairs={{0,1},{1,0},{2,4},{3,5},{4,2},{5,3},{6,8},{7,9},{8,6},{9,7},{10,12... | collective-permute-start | bytes 86024 | tf_op jit(solution)/shard_map/ppermute | solution.py:436
  52.7 7.0 %collective-permute-start.13 = (f32[56,128]{1,0:T(8,128)S(1)}, f32[56,128]{1,0:T(8,128)S(1)}, u32[]{:S(2)}, u32[]{:S(2)}) collective-permute-start(f32[56,128]{1,0:T(8,128)S(1)} %get-tuple-element.118), channel_id=1, source_target_pairs={{0,2},{1,3},{2,0},{3,1},{4,6},{5,7},{6,4},{7,5},{8,10},{9,11},{10,... | collective-permute-start | bytes 86024 | tf_op jit(solution)/shard_map/ppermute | solution.py:436
  52.7 7.5 %collective-permute-start.14 = (f32[56,128]{1,0:T(8,128)S(1)}, f32[56,128]{1,0:T(8,128)S(1)}, u32[]{:S(2)}, u32[]{:S(2)}) collective-permute-start(f32[56,128]{1,0:T(8,128)S(1)} %get-tuple-element.119), channel_id=1, source_target_pairs={{0,255},{1,2},{2,1},{3,4},{4,3},{5,6},{6,5},{7,8},{8,7},{9,10},{10... | collective-permute-start | bytes 86024 | tf_op jit(solution)/shard_map/ppermute | solution.py:436
  53.7 6.5 %collective-permute-start.15 = (f32[56,128]{1,0:T(8,128)S(1)}, f32[56,128]{1,0:T(8,128)S(1)}, u32[]{:S(2)}, u32[]{:S(2)}) collective-permute-start(f32[56,128]{1,0:T(8,128)S(1)} %get-tuple-element.120), channel_id=1, source_target_pairs={{0,1},{1,0},{2,3},{3,2},{4,5},{5,4},{6,7},{7,6},{8,9},{9,8},{10,11... | collective-permute-start | bytes 86024 | tf_op jit(solution)/shard_map/ppermute | solution.py:436

commit v6 on v4

--- a/solution.py
+++ b/solution.py
@@ -395,7 +395,7 @@
 
 
 def ghost_terms(refs):
-    (g2, g3, g1, g0, flux, lr2, nb_ref, or_ref) = refs
+    (g3, g2, g1, g0, flux, lr2, nb_ref, or_ref) = refs
     table = unpack((g0, g1, g2, g3))
     masks = orient_masks(or_ref)
     for q in range(NQ):
@@ -534,7 +534,7 @@
             coarse = call(
                 coarse_kernel, "coarse_own", [(BIG, F32)], [(BIG, F32), (TAB, F32)],
                 [series, s_mat, w2, p2, fm, l2, outs[3]], 8)[0]
-        common = [got[2], got[3], got[1], got[0], slot_flux, lr2, nb, turn_code, u, near]
+        common = [got[3], got[2], got[1], got[0], slot_flux, lr2, nb, turn_code, u, near]
         if last:
             out = call(
                 last_kernel, "last", [(BIG, F32)], [(BIG, F32)],

time: 63.4 us -> 61.7 us (0.973)
  waiting for transfers between devices: 16.6 us -> 10.2 us
  starting transfers between devices: 17.2 us -> 21.9 us
    ppermute x16, waiting for transfers between devices: 16.6 us -> 10.2 us  [exchange(): got[k] = lax.ppermute(messages[k], 'dom', pairings[k])]
    ppermute x16, starting transfers between devices: 17.2 us -> 21.9 us  [exchange(): got[k] = lax.ppermute(messages[k], 'dom', pairings[k])]
where the time goes in v6:
time: 61.7 us; the launch traced here: 61.6 us
  Pallas kernels  29.3 us (47%)
  starting transfers between devices  21.9 us (35%)
  waiting for transfers between devices  10.2 us (17%)
    pallas_call x11, Pallas kernels, call(): pl.pallas_call(kernel, name=name, out_shape=[jax.ShapeDtypeStruct(s, d) f...  29.3 us
    ppermute x16, starting transfers between devices, exchange(): got[k] = lax.ppermute(messages[k], 'dom', pairings[k])  21.9 us
    ppermute x16, waiting for transfers between devices, exchange(): got[k] = lax.ppermute(messages[k], 'dom', pairings[k])  10.2 us
  transfers between devices with their start and end apart: 16, of which 7 were waited for; matrix products, arithmetic and copies ran while one was open for 0% of the time, Pallas kernels for 18%

profile of v6, /device:TPU:24, one launch (start us, length us, event | category | flops | bytes accessed | tf_op | source)
XLA Modules:
  0.0 61.6 jit_solution(10578467761103809657)
XLA Ops:
  0.0 5.5 %first.1 = (f32[9,9,3,128]{3,2,1,0:T(4,128)S(1)}, bf16[112,168]{1,0:T(8,128)(2,1)S(1)}, bf16[192,56]{1,0:T(8,128)(2,1)S(1)}, f32[6,9,56,128]{3,2,1,0:T(8,128)S(1...) custom-call(f32[9,56,128]{2,1,0:T(8,128)} %bitcast.11, ...), custom_call_target="tpu_custom_call" | custom-call | flops 50000000 | bytes 4194304 | tf_op jit(solution)/shard_map/first/pallas_call | solution.py:455
  5.5 8.3 %collective-permute-start = (f32[56,128]{1,0:T(8,128)S(1)}, f32[56,128]{1,0:T(8,128)S(1)}, u32[]{:S(2)}, u32[]{:S(2)}) collective-permute-start(f32[56,128]{1,0:T(8,128)S(1)} %get-tuple-element.69), channel_id=1, source_target_pairs={{0,1},{1,0},{2,4},{3,5},{4,2},{5,3},{6,8},{7,9},{8,6},{9,7},{10,12... | collective-permute-start | bytes 86024 | tf_op jit(solution)/shard_map/ppermute | solution.py:493
  13.8 0.0 collective-permute-start.1
  13.8 0.2 collective-permute-start.2
  14.1 1.9 %collective-permute-start.3 = (f32[56,128]{1,0:T(8,128)S(1)}, f32[56,128]{1,0:T(8,128)S(1)}, u32[]{:S(2)}, u32[]{:S(2)}) collective-permute-start(f32[56,128]{1,0:T(8,128)S(1)} %get-tuple-element.72), channel_id=1, source_target_pairs={{0,1},{1,0},{2,3},{3,2},{4,5},{5,4},{6,7},{7,6},{8,9},{9,8},{10,11... | collective-permute-start | bytes 86024 | tf_op jit(solution)/shard_map/ppermute | solution.py:493
  16.0 0.8 %lifts.1 = (bf16[112,96]{1,0:T(8,128)(2,1)S(1)}, bf16[112,288]{1,0:T(8,128)(2,1)S(1)}, s32[8,128]{1,0:T(8,128)S(1)}, s32[2,8,128]{2,1,0:T(8,128)S(1)}, f32[5,10,...) custom-call(f32[21,4,56]{2,1,0:T(4,128)S(1)} %get-tuple-element.73.lift, ...), custom_call_target="tpu_custom_call" | custom-call | flops 50000000 | bytes 4194304 | tf_op jit(solution)/shard_map/lifts/pallas_call | solution.py:455
  16.8 2.3 %local.4 = (f32[9,56,128]{2,1,0:T(8,128)S(1)}, f32[9,56,128]{2,1,0:T(8,128)S(1)}, f32[9,56,128]{2,1,0:T(8,128)S(1)}, f32[9,24,128]{2,1,0:T(8,128)S(1)}) custom-call(f32[9,56,128]{2,1,0:T(8,128)S(1)} %slice_bitcast_fusion.refs_0_.refs_13_, f32[9,9,3,128]{3,2,1,0:T(4,128)S(1)} %get-tuple-element.75.s_ref.refs_1_, ...), custom_call_target="tpu_custom_call" | custom-call | flops 50000000 | bytes 8388608 | tf_op jit(solution)/shard_map/local/pallas_call | solution.py:455
  19.1 0.0 collective-permute-done.refs_0_
  19.1 0.0 collective-permute-done.1.refs_1_
  19.1 2.2 %collective-permute-done.2.refs_2_ = f32[56,128]{1,0:T(8,128)S(1)} collective-permute-done((f32[56,128]{1,0:T(8,128)S(1)}, f32[56,128]{1,0:T(8,128)S(1)}, u32[]{:S(2)}, u32[]{:S(2)}) %collective-permute-start.2) | collective-permute-done | bytes 28704 | tf_op jit(solution)/shard_map/ppermute | solution.py:493
  21.4 0.0 collective-permute-done.3.refs_3_
  21.4 3.7 %join.3 = (f32[9,56,128]{2,1,0:T(8,128)S(1)}, f32[9,56,128]{2,1,0:T(8,128)S(1)}, f32[5,56,128]{2,1,0:T(8,128)S(1)}, f32[56,128]{1,0:T(8,128)S(1)}, f32[56,128]{1...) custom-call(f32[56,128]{1,0:T(8,128)S(1)} %collective-permute-done.refs_0_, ...), custom_call_target="tpu_custom_call" | custom-call | flops 50000000 | bytes 4194304 | tf_op jit(solution)/shard_map/join/pallas_call | solution.py:455
  25.1 2.3 %collective-permute-start.4 = (f32[56,128]{1,0:T(8,128)S(1)}, f32[56,128]{1,0:T(8,128)S(1)}, u32[]{:S(2)}, u32[]{:S(2)}) collective-permute-start(f32[56,128]{1,0:T(8,128)S(1)} %get-tuple-element.101), channel_id=1, source_target_pairs={{0,1},{1,0},{2,4},{3,5},{4,2},{5,3},{6,8},{7,9},{8,6},{9,7},{10,12... | collective-permute-start | bytes 86024 | tf_op jit(solution)/shard_map/ppermute | solution.py:493
  27.4 0.0 collective-permute-start.5
  27.4 1.4 %collective-permute-start.6 = (f32[56,128]{1,0:T(8,128)S(1)}, f32[56,128]{1,0:T(8,128)S(1)}, u32[]{:S(2)}, u32[]{:S(2)}) collective-permute-start(f32[56,128]{1,0:T(8,128)S(1)} %get-tuple-element.103), channel_id=1, source_target_pairs={{0,255},{1,2},{2,1},{3,4},{4,3},{5,6},{6,5},{7,8},{8,7},{9,10},{10... | collective-permute-start | bytes 86024 | tf_op jit(solution)/shard_map/ppermute | solution.py:493
  28.7 0.8 %collective-permute-start.7 = (f32[56,128]{1,0:T(8,128)S(1)}, f32[56,128]{1,0:T(8,128)S(1)}, u32[]{:S(2)}, u32[]{:S(2)}) collective-permute-start(f32[56,128]{1,0:T(8,128)S(1)} %get-tuple-element.104.after), channel_id=1, source_target_pairs={{0,1},{1,0},{2,3},{3,2},{4,5},{5,4},{6,7},{7,6},{8,9},{9,8},{10,11... | collective-permute-start | bytes 86024 | tf_op jit(solution)/shard_map/ppermute | solution.py:493
  29.5 2.4 %local.5 = (f32[9,56,128]{2,1,0:T(8,128)S(1)}, f32[9,56,128]{2,1,0:T(8,128)S(1)}, f32[9,56,128]{2,1,0:T(8,128)S(1)}, f32[9,24,128]{2,1,0:T(8,128)S(1)}) custom-call(f32[9,56,128]{2,1,0:T(8,128)S(1)} %get-tuple-element.105.refs_0_.refs_13_, f32[9,9,3,128]{3,2,1,0:T(4,128)S(1)} %get-tuple-element.75.s_ref.refs_1_, ...), custom_call_target="tpu_custom_call" | custom-call | flops 50000000 | bytes 8388608 | tf_op jit(solution)/shard_map/local/pallas_call | solution.py:455
  31.9 1.6 %collective-permute-done.4.refs_0_ = f32[56,128]{1,0:T(8,128)S(1)} collective-permute-done((f32[56,128]{1,0:T(8,128)S(1)}, f32[56,128]{1,0:T(8,128)S(1)}, u32[]{:S(2)}, u32[]{:S(2)}) %collective-permute-start.4) | collective-permute-done | bytes 28704 | tf_op jit(solution)/shard_map/ppermute | solution.py:493
  33.4 0.0 collective-permute-done.5.refs_1_
  33.4 1.4 %collective-permute-done.6.refs_2_ = f32[56,128]{1,0:T(8,128)S(1)} collective-permute-done((f32[56,128]{1,0:T(8,128)S(1)}, f32[56,128]{1,0:T(8,128)S(1)}, u32[]{:S(2)}, u32[]{:S(2)}) %collective-permute-start.6) | collective-permute-done | bytes 28704 | tf_op jit(solution)/shard_map/ppermute | solution.py:493
  34.9 0.0 collective-permute-done.7.refs_3_
  34.9 3.7 %join.4 = (f32[9,56,128]{2,1,0:T(8,128)S(1)}, f32[9,56,128]{2,1,0:T(8,128)S(1)}, f32[5,56,128]{2,1,0:T(8,128)S(1)}, f32[56,128]{1,0:T(8,128)S(1)}, f32[56,128]{1...) custom-call(f32[56,128]{1,0:T(8,128)S(1)} %collective-permute-done.4.refs_0_, ...), custom_call_target="tpu_custom_call" | custom-call | flops 50000000 | bytes 4194304 | tf_op jit(solution)/shard_map/join/pallas_call | solution.py:455
  38.6 1.4 %collective-permute-start.8 = (f32[56,128]{1,0:T(8,128)S(1)}, f32[56,128]{1,0:T(8,128)S(1)}, u32[]{:S(2)}, u32[]{:S(2)}) collective-permute-start(f32[56,128]{1,0:T(8,128)S(1)} %get-tuple-element.112), channel_id=1, source_target_pairs={{0,1},{1,0},{2,4},{3,5},{4,2},{5,3},{6,8},{7,9},{8,6},{9,7},{10,12... | collective-permute-start | bytes 86024 | tf_op jit(solution)/shard_map/ppermute | solution.py:493
  40.0 0.0 collective-permute-start.9
  40.0 1.4 %collective-permute-start.10 = (f32[56,128]{1,0:T(8,128)S(1)}, f32[56,128]{1,0:T(8,128)S(1)}, u32[]{:S(2)}, u32[]{:S(2)}) collective-permute-start(f32[56,128]{1,0:T(8,128)S(1)} %get-tuple-element.114), channel_id=1, source_target_pairs={{0,255},{1,2},{2,1},{3,4},{4,3},{5,6},{6,5},{7,8},{8,7},{9,10},{10... | collective-permute-start | bytes 86024 | tf_op jit(solution)/shard_map/ppermute | solution.py:493
  41.3 0.8 %collective-permute-start.11 = (f32[56,128]{1,0:T(8,128)S(1)}, f32[56,128]{1,0:T(8,128)S(1)}, u32[]{:S(2)}, u32[]{:S(2)}) collective-permute-start(f32[56,128]{1,0:T(8,128)S(1)} %get-tuple-element.115), channel_id=1, source_target_pairs={{0,1},{1,0},{2,3},{3,2},{4,5},{5,4},{6,7},{7,6},{8,9},{9,8},{10,11... | collective-permute-start | bytes 86024 | tf_op jit(solution)/shard_map/ppermute | solution.py:493
  42.1 2.4 %local.6 = (f32[9,56,128]{2,1,0:T(8,128)S(1)}, f32[9,56,128]{2,1,0:T(8,128)S(1)}, f32[9,56,128]{2,1,0:T(8,128)S(1)}, f32[9,24,128]{2,1,0:T(8,128)S(1)}) custom-call(f32[9,56,128]{2,1,0:T(8,128)S(1)} %get-tuple-element.116.refs_0_.refs_13_, f32[9,9,3,128]{3,2,1,0:T(4,128)S(1)} %get-tuple-element.75.s_ref.refs_1_, ...), custom_call_target="tpu_custom_call" | custom-call | flops 50000000 | bytes 8388608 | tf_op jit(solution)/shard_map/local/pallas_call | solution.py:455
  44.5 2.3 %collective-permute-done.8.refs_0_ = f32[56,128]{1,0:T(8,128)S(1)} collective-permute-done((f32[56,128]{1,0:T(8,128)S(1)}, f32[56,128]{1,0:T(8,128)S(1)}, u32[]{:S(2)}, u32[]{:S(2)}) %collective-permute-start.8) | collective-permute-done | bytes 28704 | tf_op jit(solution)/shard_map/ppermute | solution.py:493
  46.8 0.0 collective-permute-done.9.refs_1_
  46.8 0.7 %collective-permute-done.10.refs_2_ = f32[56,128]{1,0:T(8,128)S(1)} collective-permute-done((f32[56,128]{1,0:T(8,128)S(1)}, f32[56,128]{1,0:T(8,128)S(1)}, u32[]{:S(2)}, u32[]{:S(2)}) %collective-permute-start.10) | collective-permute-done | bytes 28704 | tf_op jit(solution)/shard_map/ppermute | solution.py:493
  47.5 0.0 collective-permute-done.11.refs_3_
  47.5 3.7 %join.5 = (f32[9,56,128]{2,1,0:T(8,128)S(1)}, f32[9,56,128]{2,1,0:T(8,128)S(1)}, f32[5,56,128]{2,1,0:T(8,128)S(1)}, f32[56,128]{1,0:T(8,128)S(1)}, f32[56,128]{1...) custom-call(f32[56,128]{1,0:T(8,128)S(1)} %collective-permute-done.8.refs_0_, ...), custom_call_target="tpu_custom_call" | custom-call | flops 50000000 | bytes 4194304 | tf_op jit(solution)/shard_map/join/pallas_call | solution.py:455
  51.2 1.4 %collective-permute-start.12 = (f32[56,128]{1,0:T(8,128)S(1)}, f32[56,128]{1,0:T(8,128)S(1)}, u32[]{:S(2)}, u32[]{:S(2)}) collective-permute-start(f32[56,128]{1,0:T(8,128)S(1)} %get-tuple-element.123), channel_id=1, source_target_pairs={{0,1},{1,0},{2,4},{3,5},{4,2},{5,3},{6,8},{7,9},{8,6},{9,7},{10,12... | collective-permute-start | bytes 86024 | tf_op jit(solution)/shard_map/ppermute | solution.py:493
  52.6 0.0 collective-permute-start.13
  52.6 1.8 %collective-permute-start.14 = (f32[56,128]{1,0:T(8,128)S(1)}, f32[56,128]{1,0:T(8,128)S(1)}, u32[]{:S(2)}, u32[]{:S(2)}) collective-permute-start(f32[56,128]{1,0:T(8,128)S(1)} %get-tuple-element.125), channel_id=1, source_target_pairs={{0,255},{1,2},{2,1},{3,4},{4,3},{5,6},{6,5},{7,8},{8,7},{9,10},{10... | collective-permute-start | bytes 86024 | tf_op jit(solution)/shard_map/ppermute | solution.py:493
  54.4 0.4 collective-permute-start.15
  54.7 1.3 %coarse_own.1.refs_11_ = f32[9,56,128]{2,1,0:T(8,128)S(1)} custom-call(f32[6,9,56,128]{3,2,1,0:T(8,128)S(1)} %get-tuple-element.83.refs_11_.series, f32[9,9,3,128]{3,2,1,0:T(4,128)S(1)} %get-tuple-element.75.s_ref.refs_1_, bf16[112,168]{1,0:T(8,128)(2,1)S(1)} %get-tuple-element.84.refs_2_.refs_15_.w2, ...), custom_call_target="tpu_custom_call" | custom-call | flops 50000000 | bytes 8388608 | tf_op jit(solution)/shard_map/coarse_own/pallas_call | solution.py:455
  56.0 2.1 %local.7 = (f32[9,56,128]{2,1,0:T(8,128)S(1)}, f32[9,56,128]{2,1,0:T(8,128)S(1)}) custom-call(f32[9,56,128]{2,1,0:T(8,128)S(1)} %get-tuple-element.127.refs_0_, f32[9,9,3,128]{3,2,1,0:T(4,128)S(1)} %get-tuple-element.75.s_ref.refs_1_, bf16[112,168]{1,0:T(8,128)(2,1)S(1)} %get-tuple-element.84.refs_2_.refs_15_.w2, ...), custom_call_target="tpu_custom_call" | custom-call | flops 50000000 | bytes 8388608 | tf_op jit(solution)/shard_map/local/pallas_call | solution.py:455
  58.2 1.2 %collective-permute-done.12.refs_0_ = f32[56,128]{1,0:T(8,128)S(1)} collective-permute-done((f32[56,128]{1,0:T(8,128)S(1)}, f32[56,128]{1,0:T(8,128)S(1)}, u32[]{:S(2)}, u32[]{:S(2)}) %collective-permute-start.12) | collective-permute-done | bytes 28704 | tf_op jit(solution)/shard_map/ppermute | solution.py:493
  59.4 0.0 collective-permute-done.13.refs_1_
  59.4 0.7 %collective-permute-done.14.refs_2_ = f32[56,128]{1,0:T(8,128)S(1)} collective-permute-done((f32[56,128]{1,0:T(8,128)S(1)}, f32[56,128]{1,0:T(8,128)S(1)}, u32[]{:S(2)}, u32[]{:S(2)}) %collective-permute-start.14) | collective-permute-done | bytes 28704 | tf_op jit(solution)/shard_map/ppermute | solution.py:493
  60.1 0.0 collective-permute-done.15.refs_3_
  60.1 1.4 %last.1 = f32[9,56,128]{2,1,0:T(8,128)} custom-call(f32[56,128]{1,0:T(8,128)S(1)} %collective-permute-done.12.refs_0_, f32[56,128]{1,0:T(8,128)S(1)} %collective-permute-done.13.refs_1_, f32[56,128]{1,0:T(8,128)S(1)} %collective-permute-done.14.refs_2_, f32[56,128]{1,0:T(8,128)S(1)} %collective-permute-done.15.refs_3_, ...), custom_call_target="tpu_custom_call" | custom-call | flops 50000000 | bytes 4194304 | tf_op jit(solution)/shard_map/last/pallas_call | solution.py:455
  (1 shorter events, 0.0 us)
Async XLA Ops:
  5.5 13.6 %collective-permute-start = (f32[56,128]{1,0:T(8,128)S(1)}, f32[56,128]{1,0:T(8,128)S(1)}, u32[]{:S(2)}, u32[]{:S(2)}) collective-permute-start(f32[56,128]{1,0:T(8,128)S(1)} %get-tuple-element.69), channel_id=1, source_target_pairs={{0,1},{1,0},{2,4},{3,5},{4,2},{5,3},{6,8},{7,9},{8,6},{9,7},{10,12... | collective-permute-start | bytes 86024 | tf_op jit(solution)/shard_map/ppermute | solution.py:493
  13.8 5.3 %collective-permute-start.1 = (f32[56,128]{1,0:T(8,128)S(1)}, f32[56,128]{1,0:T(8,128)S(1)}, u32[]{:S(2)}, u32[]{:S(2)}) collective-permute-start(f32[56,128]{1,0:T(8,128)S(1)} %get-tuple-element.70), channel_id=1, source_target_pairs={{0,2},{1,3},{2,0},{3,1},{4,6},{5,7},{6,4},{7,5},{8,10},{9,11},{10,... | collective-permute-start | bytes 86024 | tf_op jit(solution)/shard_map/ppermute | solution.py:493
  13.8 7.5 %collective-permute-start.2 = (f32[56,128]{1,0:T(8,128)S(1)}, f32[56,128]{1,0:T(8,128)S(1)}, u32[]{:S(2)}, u32[]{:S(2)}) collective-permute-start(f32[56,128]{1,0:T(8,128)S(1)} %get-tuple-element.71), channel_id=1, source_target_pairs={{0,255},{1,2},{2,1},{3,4},{4,3},{5,6},{6,5},{7,8},{8,7},{9,10},{10... | collective-permute-start | bytes 86024 | tf_op jit(solution)/shard_map/ppermute | solution.py:493
  14.1 7.3 %collective-permute-start.3 = (f32[56,128]{1,0:T(8,128)S(1)}, f32[56,128]{1,0:T(8,128)S(1)}, u32[]{:S(2)}, u32[]{:S(2)}) collective-permute-start(f32[56,128]{1,0:T(8,128)S(1)} %get-tuple-element.72), channel_id=1, source_target_pairs={{0,1},{1,0},{2,3},{3,2},{4,5},{5,4},{6,7},{7,6},{8,9},{9,8},{10,11... | collective-permute-start | bytes 86024 | tf_op jit(solution)/shard_map/ppermute | solution.py:493
  25.1 8.4 %collective-permute-start.4 = (f32[56,128]{1,0:T(8,128)S(1)}, f32[56,128]{1,0:T(8,128)S(1)}, u32[]{:S(2)}, u32[]{:S(2)}) collective-permute-start(f32[56,128]{1,0:T(8,128)S(1)} %get-tuple-element.101), channel_id=1, source_target_pairs={{0,1},{1,0},{2,4},{3,5},{4,2},{5,3},{6,8},{7,9},{8,6},{9,7},{10,12... | collective-permute-start | bytes 86024 | tf_op jit(solution)/shard_map/ppermute | solution.py:493
  27.4 6.1 %collective-permute-start.5 = (f32[56,128]{1,0:T(8,128)S(1)}, f32[56,128]{1,0:T(8,128)S(1)}, u32[]{:S(2)}, u32[]{:S(2)}) collective-permute-start(f32[56,128]{1,0:T(8,128)S(1)} %get-tuple-element.102), channel_id=1, source_target_pairs={{0,2},{1,3},{2,0},{3,1},{4,6},{5,7},{6,4},{7,5},{8,10},{9,11},{10,... | collective-permute-start | bytes 86024 | tf_op jit(solution)/shard_map/ppermute | solution.py:493
  27.4 7.5 %collective-permute-start.6 = (f32[56,128]{1,0:T(8,128)S(1)}, f32[56,128]{1,0:T(8,128)S(1)}, u32[]{:S(2)}, u32[]{:S(2)}) collective-permute-start(f32[56,128]{1,0:T(8,128)S(1)} %get-tuple-element.103), channel_id=1, source_target_pairs={{0,255},{1,2},{2,1},{3,4},{4,3},{5,6},{6,5},{7,8},{8,7},{9,10},{10... | collective-permute-start | bytes 86024 | tf_op jit(solution)/shard_map/ppermute | solution.py:493
  28.7 6.2 %collective-permute-start.7 = (f32[56,128]{1,0:T(8,128)S(1)}, f32[56,128]{1,0:T(8,128)S(1)}, u32[]{:S(2)}, u32[]{:S(2)}) collective-permute-start(f32[56,128]{1,0:T(8,128)S(1)} %get-tuple-element.104.after), channel_id=1, source_target_pairs={{0,1},{1,0},{2,3},{3,2},{4,5},{5,4},{6,7},{7,6},{8,9},{9,8},{10,11... | collective-permute-start | bytes 86024 | tf_op jit(solution)/shard_map/ppermute | solution.py:493
  38.6 8.2 %collective-permute-start.8 = (f32[56,128]{1,0:T(8,128)S(1)}, f32[56,128]{1,0:T(8,128)S(1)}, u32[]{:S(2)}, u32[]{:S(2)}) collective-permute-start(f32[56,128]{1,0:T(8,128)S(1)} %get-tuple-element.112), channel_id=1, source_target_pairs={{0,1},{1,0},{2,4},{3,5},{4,2},{5,3},{6,8},{7,9},{8,6},{9,7},{10,12... | collective-permute-start | bytes 86024 | tf_op jit(solution)/shard_map/ppermute | solution.py:493
  40.0 6.8 %collective-permute-start.9 = (f32[56,128]{1,0:T(8,128)S(1)}, f32[56,128]{1,0:T(8,128)S(1)}, u32[]{:S(2)}, u32[]{:S(2)}) collective-permute-start(f32[56,128]{1,0:T(8,128)S(1)} %get-tuple-element.113), channel_id=1, source_target_pairs={{0,2},{1,3},{2,0},{3,1},{4,6},{5,7},{6,4},{7,5},{8,10},{9,11},{10,... | collective-permute-start | bytes 86024 | tf_op jit(solution)/shard_map/ppermute | solution.py:493
  40.0 7.5 %collective-permute-start.10 = (f32[56,128]{1,0:T(8,128)S(1)}, f32[56,128]{1,0:T(8,128)S(1)}, u32[]{:S(2)}, u32[]{:S(2)}) collective-permute-start(f32[56,128]{1,0:T(8,128)S(1)} %get-tuple-element.114), channel_id=1, source_target_pairs={{0,255},{1,2},{2,1},{3,4},{4,3},{5,6},{6,5},{7,8},{8,7},{9,10},{10... | collective-permute-start | bytes 86024 | tf_op jit(solution)/shard_map/ppermute | solution.py:493
  41.3 6.2 %collective-permute-start.11 = (f32[56,128]{1,0:T(8,128)S(1)}, f32[56,128]{1,0:T(8,128)S(1)}, u32[]{:S(2)}, u32[]{:S(2)}) collective-permute-start(f32[56,128]{1,0:T(8,128)S(1)} %get-tuple-element.115), channel_id=1, source_target_pairs={{0,1},{1,0},{2,3},{3,2},{4,5},{5,4},{6,7},{7,6},{8,9},{9,8},{10,11... | collective-permute-start | bytes 86024 | tf_op jit(solution)/shard_map/ppermute | solution.py:493
  51.2 8.2 %collective-permute-start.12 = (f32[56,128]{1,0:T(8,128)S(1)}, f32[56,128]{1,0:T(8,128)S(1)}, u32[]{:S(2)}, u32[]{:S(2)}) collective-permute-start(f32[56,128]{1,0:T(8,128)S(1)} %get-tuple-element.123), channel_id=1, source_target_pairs={{0,1},{1,0},{2,4},{3,5},{4,2},{5,3},{6,8},{7,9},{8,6},{9,7},{10,12... | collective-permute-start | bytes 86024 | tf_op jit(solution)/shard_map/ppermute | solution.py:493
  52.6 6.8 %collective-permute-start.13 = (f32[56,128]{1,0:T(8,128)S(1)}, f32[56,128]{1,0:T(8,128)S(1)}, u32[]{:S(2)}, u32[]{:S(2)}) collective-permute-start(f32[56,128]{1,0:T(8,128)S(1)} %get-tuple-element.124), channel_id=1, source_target_pairs={{0,2},{1,3},{2,0},{3,1},{4,6},{5,7},{6,4},{7,5},{8,10},{9,11},{10,... | collective-permute-start | bytes 86024 | tf_op jit(solution)/shard_map/ppermute | solution.py:493
  52.6 7.5 %collective-permute-start.14 = (f32[56,128]{1,0:T(8,128)S(1)}, f32[56,128]{1,0:T(8,128)S(1)}, u32[]{:S(2)}, u32[]{:S(2)}) collective-permute-start(f32[56,128]{1,0:T(8,128)S(1)} %get-tuple-element.125), channel_id=1, source_target_pairs={{0,255},{1,2},{2,1},{3,4},{4,3},{5,6},{6,5},{7,8},{8,7},{9,10},{10... | collective-permute-start | bytes 86024 | tf_op jit(solution)/shard_map/ppermute | solution.py:493
  54.4 5.7 %collective-permute-start.15 = (f32[56,128]{1,0:T(8,128)S(1)}, f32[56,128]{1,0:T(8,128)S(1)}, u32[]{:S(2)}, u32[]{:S(2)}) collective-permute-start(f32[56,128]{1,0:T(8,128)S(1)} %get-tuple-element.126), channel_id=1, source_target_pairs={{0,1},{1,0},{2,3},{3,2},{4,5},{5,4},{6,7},{7,6},{8,9},{9,8},{10,11... | collective-permute-start | bytes 86024 | tf_op jit(solution)/shard_map/ppermute | solution.py:493
